TPU v7x, 256 devices: a whole 4x4x8 slice. The times are simulated.
256 devices in a mesh: ctx: 32 (over z, y), head: 8 (over x, core).
Axes of the slice: x: 4, y: 4, z: 8, core: 2. Of those that a mesh axis runs over, the one named last changes fastest.
Arguments:
- tokens: bfloat16 [16384, 2048], P('ctx'), may hold values from -6 to 6
- w_proj: bfloat16 [2048, 10240], P('ctx', 'head'), may hold values from -0.125 to 0.125
- w_small: bfloat16 [2048, 48], P('ctx', 'head'), may hold values from -0.125 to 0.125
- beta_bias: float32 [16, 2], P('head'), may hold values from 5 to 9
- decay_rate: float32 [16], P('head'), may hold values from 5e-07 to 0.05
- w_out: bfloat16 [2048, 2048], P('head', 'ctx'), may hold values from -0.125 to 0.125
Outputs:
- mixed: bfloat16 [16384, 2048], P(('ctx', 'head'))
All inputs are finite; a program needn't handle non-finite values.
Results may differ from a plain program's by a relative error of at most 0.006.
Values may be sent and summed in bfloat16 or wider, within the bound.
No kernel may reach another device: no remote copies, remote signals or barrier semaphores. Data moves between devices by JAX's collectives and lax.ppermute only.
A program may use at most 128 MiB of HBM per device.

v0:
```python
import math

import jax
import jax.numpy as jnp
from jax import lax
from jax.sharding import PartitionSpec as P

HIGHEST_PRECISION = lax.Precision.HIGHEST


def from_behind(array, axis, by):
    count = lax.axis_size(axis)
    pairs = [(i, i + by) for i in range(count) if 0 <= i + by < count]
    return lax.ppermute(array, axis, pairs)


def matrix_product(left, right):
    return jnp.matmul(left, right, precision=HIGHEST_PRECISION)


def unit_rows(vectors):
    return vectors / jnp.sqrt(jnp.sum(vectors * vectors, axis=-1, keepdims=True) + 1e-06)


def compose(earlier, later):
    return (matrix_product(earlier[0], later[0]), matrix_product(earlier[1], later[0]) + later[1])


def shards(tokens, w_proj, w_small, beta_bias, decay_rate, w_out):
    tok_rows = tokens.shape[0]
    heads_here = beta_bias.shape[0]
    mirrors = beta_bias.shape[1]
    head_width = w_proj.shape[1] // (heads_here * (1 + 2 * mirrors))
    projected = jnp.dot(
        tokens,
        lax.all_gather(w_proj, "ctx", axis=0, tiled=True),
        preferred_element_type=jnp.float32,
    )
    gate_inputs = jnp.dot(
        tokens,
        lax.all_gather(w_small, "ctx", axis=0, tiled=True),
        preferred_element_type=jnp.float32,
    )
    parts = projected.reshape(tok_rows, heads_here, 1 + 2 * mirrors, head_width)
    queries = unit_rows(parts[:, :, 0])
    keys_all = unit_rows(parts[:, :, 1 : 1 + mirrors])
    values_all = parts[:, :, 1 + mirrors :]
    gate_cols = gate_inputs.reshape(tok_rows, heads_here, mirrors + 1)
    betas = 2.0 * jax.nn.sigmoid(gate_cols[:, :, :mirrors] + beta_bias[None])
    log_decay = -decay_rate[None, :] * jax.nn.softplus(gate_cols[:, :, mirrors])
    log_steps = jnp.concatenate(
        [log_decay[:, :, None], jnp.zeros((tok_rows, heads_here, mirrors - 1), jnp.float32)], axis=2
    )
    block_tok = math.gcd(tok_rows, 64)
    blocks = tok_rows // block_tok
    span = block_tok * mirrors

    def to_steps(array):
        moved = jnp.moveaxis(array, 1, 0)
        return moved.reshape((heads_here, blocks, span) + array.shape[3:])

    key_steps = to_steps(keys_all)
    value_steps = to_steps(values_all)
    beta_steps = to_steps(betas)
    running = jnp.cumsum(to_steps(log_steps), axis=-1)
    running_query = running[..., mirrors - 1 :: mirrors]
    query_blocks = jnp.moveaxis(queries, 1, 0).reshape(heads_here, blocks, block_tok, head_width)
    step_index = lax.iota(jnp.int32, span)
    strict = step_index[:, None] > step_index[None, :]
    inner = jnp.einsum("hnsk,hnrk->hnsr", key_steps, key_steps, precision=HIGHEST_PRECISION)
    spread = jnp.where(strict, running[..., :, None] - running[..., None, :], 0.0)
    lower_part = jnp.where(strict, beta_steps[..., :, None] * jnp.exp(spread) * inner, 0.0)
    system = lower_part + jnp.eye(span, dtype=jnp.float32)
    weighted_values = lax.linalg.triangular_solve(
        system, beta_steps[..., None] * value_steps, left_side=True, lower=True
    )
    weighted_keys = lax.linalg.triangular_solve(
        system, (beta_steps * jnp.exp(running))[..., None] * key_steps, left_side=True, lower=True
    )
    tail = jnp.exp(running[..., -1:] - running)
    identity_block = jnp.eye(head_width, dtype=jnp.float32)
    transitions = jnp.exp(running[..., -1])[..., None, None] * identity_block - jnp.einsum(
        "hnsa,hnsb->hnab", weighted_keys * tail[..., None], key_steps, precision=HIGHEST_PRECISION
    )
    writes = jnp.einsum(
        "hnsa,hnsb->hnab", weighted_values * tail[..., None], key_steps, precision=HIGHEST_PRECISION
    )
    inclusive = lax.associative_scan(compose, (transitions, writes), axis=1)
    square_shape = (heads_here, 1, head_width, head_width)
    start_trans = jnp.concatenate(
        [jnp.broadcast_to(identity_block, square_shape), inclusive[0][:, :-1]], axis=1
    )
    start_write = jnp.concatenate(
        [jnp.zeros(square_shape, jnp.float32), inclusive[1][:, :-1]], axis=1
    )
    device_trans = inclusive[0][:, -1]
    device_write = inclusive[1][:, -1]

    def relay(turn, incoming):
        outgoing = matrix_product(incoming, device_trans) + device_write
        return from_behind(outgoing, "ctx", 1)

    state_in = lax.fori_loop(
        0, lax.axis_size("ctx") - 1, relay, jnp.zeros(device_write.shape, jnp.float32)
    )
    states = (
        jnp.einsum("hab,hnbc->hnac", state_in, start_trans, precision=HIGHEST_PRECISION)
        + start_write
    )
    pseudo = weighted_values - jnp.einsum(
        "hnsb,hnab->hnsa", weighted_keys, states, precision=HIGHEST_PRECISION
    )
    token_index = lax.iota(jnp.int32, block_tok)
    visible = step_index[None, :] <= token_index[:, None] * mirrors + mirrors - 1
    scores = jnp.einsum("hntb,hnsb->hnts", query_blocks, key_steps, precision=HIGHEST_PRECISION)
    reach = jnp.where(visible, running_query[..., :, None] - running[..., None, :], 0.0)
    attend = jnp.where(visible, jnp.exp(reach) * scores, 0.0)
    head_out = jnp.exp(running_query)[..., None] * jnp.einsum(
        "hntb,hnab->hnta", query_blocks, states, precision=HIGHEST_PRECISION
    )
    head_out = head_out + jnp.einsum("hnts,hnsa->hnta", attend, pseudo, precision=HIGHEST_PRECISION)
    normed = head_out / jnp.sqrt(jnp.mean(head_out * head_out, axis=-1, keepdims=True) + 1e-06)
    mixed_heads = jnp.moveaxis(normed.reshape(heads_here, tok_rows, head_width), 0, 1)
    mixed_heads = mixed_heads.reshape(tok_rows, heads_here * head_width).astype(jnp.bfloat16)
    grouped = lax.all_gather(w_out, "head", axis=0, tiled=True)
    full_out = lax.all_gather(grouped, "ctx", axis=1, tiled=True)
    group_count = lax.axis_size("head")
    rows_each = tok_rows // group_count
    stacked = mixed_heads.reshape(group_count, rows_each, heads_here * head_width)
    mixed = jnp.einsum(
        "irk,kd->ird",
        lax.all_to_all(stacked, "head", split_axis=0, concat_axis=2, tiled=True),
        full_out,
        preferred_element_type=jnp.float32,
    ).astype(jnp.bfloat16)
    mixed = mixed.reshape(rows_each, full_out.shape[1])
    return mixed


def solution(mesh):
    placed = (
        P("ctx", None),
        P("ctx", "head"),
        P("ctx", "head"),
        P("head", None),
        P("head"),
        P("head", "ctx"),
    )
    return jax.shard_map(
        shards, mesh=mesh, in_specs=placed, out_specs=P(("ctx", "head"), None), check_vma=False
    )
```

profile of v0, /device:TPU:128, one launch (start us, length us, event | category | flops | bytes accessed | tf_op | source)
XLA Modules:
  0.0 744.8 jit_solution(6895089295835122706)
XLA Ops:
  7.3 14.5 %all_gather.14 = bf16[2048,64]{0,1:T(8,128)(2,1)} all-gather(bf16[256,64]{0,1:T(8,128)(2,1)} %param.15), channel_id=1, replica_groups=mesh['ctx'=32,'head'=8] {'head'}, dimensions={0}, use_global_device_ids=true | all-gather | bytes 294912 | tf_op jit(solution)/shard_map/all_gather | solution.py:125
  21.9 48.9 %all-gather = bf16[32,64,6]{1,2,0:T(8,128)(2,1)S(1)} all-gather(bf16[1,64,6]{1,2,0:T(8,128)(2,1)} %bitcast.138), channel_id=1, replica_groups=mesh['ctx'=32,'head'=8] {'ctx'}, dimensions={0}, use_global_device_ids=true | all-gather | bytes 25344 | tf_op jit(solution)/shard_map/all_gather | solution.py:41
  75.1 18.3 %all-gather.4.cloned.1.call-done = bf16[2048,1280]{1,0:T(8,128)(2,1)} async-done(((bf16[64,1280]{1,0:T(8,128)(2,1)}), bf16[2048,1280]{1,0:T(8,128)(2,1)}) %all-gather.4.cloned.1.call-update) | async-done | bytes 5242896 | tf_op jit(solution)/shard_map/all_gather | solution.py:36
  93.4 4.9 fusion.58
  102.0 3.3 fusion.4
  105.4 158.6 %custom-call.4 = f32[2,8,1,128,128]{3,4,2,1,0:T(8,128)} custom-call(f32[2,8,1,128,128]{4,3,2,1,0:T(8,128)} %fusion.4), custom_call_target="InvertDiagBlocksLowerTriangular" | custom-call | tf_op jit(solution)/shard_map/triangular_solve/custom-call.1 | solution.py:77
  264.0 3.4 fusion.13
  267.4 2.2 convolution_subtract_fusion.1
  273.1 3.7 pad.42
  278.5 3.7 pad.43
  282.2 2.1 add.150
  284.3 5.7 pad.45
  290.0 5.7 pad.110
  295.6 2.3 copy.59
  301.5 2.2 fusion.15
  305.5 2.1 pad.48
  308.6 2.1 pad.49
  310.7 2.1 add.157
  312.8 5.7 pad.108
  321.1 5.7 pad.66
  326.8 5.7 pad.50
  333.6 1.9 divide_bitcast_fusion.1
  335.5 2.0 copy.53
  340.1 5.7 pad.44
  347.9 2.5 slice_add_fusion.2
  351.5 356.2 %while.10 = (s32[]{:T(128)}, f32[2,128,128]{2,1,0:T(8,128)S(1)}, f32[2,128,128]{2,1,0:T(8,128)S(1)}, f32[2,128,128]{2,1,0:T(8,128)S(1)}, s32[]{:T(128)}) while((s32[]{:T(128)}, f32[2,128,128]{2,1,0:T(8,128)S(1)}, f32[2,128,128]{2,1,0:T(8,128)S(1)}, f32[2,128,128]{2,1,0:T(8,128)S(1)}, s32[]{:T(128)}) %tuple.23), condition=%wide.region_4.6_spmd, body=%wide.region_3.5_spmd.sunk | while | flops 50364416 | bytes 1048677 | solution.py:103
  352.5 2.3 collective-permute-start
  354.8 8.1 %collective-permute-done = f32[2,128,128]{2,1,0:T(8,128)S(1)} collective-permute-done((f32[2,128,128]{2,1,0:T(8,128)}, f32[2,128,128]{2,1,0:T(8,128)S(1)}, u32[]{:S(2)}, u32[]{:S(2)}) %collective-permute-start) | collective-permute-done | bytes 131104 | tf_op jit(solution)/shard_map/while/body/eval_jaxpr/ppermute | solution.py:14
  365.7 8.5 %collective-permute-done = f32[2,128,128]{2,1,0:T(8,128)S(1)} collective-permute-done((f32[2,128,128]{2,1,0:T(8,128)}, f32[2,128,128]{2,1,0:T(8,128)S(1)}, u32[]{:S(2)}, u32[]{:S(2)}) %collective-permute-start) | collective-permute-done | bytes 131104 | tf_op jit(solution)/shard_map/while/body/eval_jaxpr/ppermute | solution.py:14
  377.0 8.5 %collective-permute-done = f32[2,128,128]{2,1,0:T(8,128)S(1)} collective-permute-done((f32[2,128,128]{2,1,0:T(8,128)}, f32[2,128,128]{2,1,0:T(8,128)S(1)}, u32[]{:S(2)}, u32[]{:S(2)}) %collective-permute-start) | collective-permute-done | bytes 131104 | tf_op jit(solution)/shard_map/while/body/eval_jaxpr/ppermute | solution.py:14
  388.3 8.5 %collective-permute-done = f32[2,128,128]{2,1,0:T(8,128)S(1)} collective-permute-done((f32[2,128,128]{2,1,0:T(8,128)}, f32[2,128,128]{2,1,0:T(8,128)S(1)}, u32[]{:S(2)}, u32[]{:S(2)}) %collective-permute-start) | collective-permute-done | bytes 131104 | tf_op jit(solution)/shard_map/while/body/eval_jaxpr/ppermute | solution.py:14
  399.6 8.5 %collective-permute-done = f32[2,128,128]{2,1,0:T(8,128)S(1)} collective-permute-done((f32[2,128,128]{2,1,0:T(8,128)}, f32[2,128,128]{2,1,0:T(8,128)S(1)}, u32[]{:S(2)}, u32[]{:S(2)}) %collective-permute-start) | collective-permute-done | bytes 131104 | tf_op jit(solution)/shard_map/while/body/eval_jaxpr/ppermute | solution.py:14
  410.9 9.1 %collective-permute-done = f32[2,128,128]{2,1,0:T(8,128)S(1)} collective-permute-done((f32[2,128,128]{2,1,0:T(8,128)}, f32[2,128,128]{2,1,0:T(8,128)S(1)}, u32[]{:S(2)}, u32[]{:S(2)}) %collective-permute-start) | collective-permute-done | bytes 131104 | tf_op jit(solution)/shard_map/while/body/eval_jaxpr/ppermute | solution.py:14
  422.8 9.5 %collective-permute-done = f32[2,128,128]{2,1,0:T(8,128)S(1)} collective-permute-done((f32[2,128,128]{2,1,0:T(8,128)}, f32[2,128,128]{2,1,0:T(8,128)S(1)}, u32[]{:S(2)}, u32[]{:S(2)}) %collective-permute-start) | collective-permute-done | bytes 131104 | tf_op jit(solution)/shard_map/while/body/eval_jaxpr/ppermute | solution.py:14
  435.2 8.7 %collective-permute-done = f32[2,128,128]{2,1,0:T(8,128)S(1)} collective-permute-done((f32[2,128,128]{2,1,0:T(8,128)}, f32[2,128,128]{2,1,0:T(8,128)S(1)}, u32[]{:S(2)}, u32[]{:S(2)}) %collective-permute-start) | collective-permute-done | bytes 131104 | tf_op jit(solution)/shard_map/while/body/eval_jaxpr/ppermute | solution.py:14
  446.7 8.5 %collective-permute-done = f32[2,128,128]{2,1,0:T(8,128)S(1)} collective-permute-done((f32[2,128,128]{2,1,0:T(8,128)}, f32[2,128,128]{2,1,0:T(8,128)S(1)}, u32[]{:S(2)}, u32[]{:S(2)}) %collective-permute-start) | collective-permute-done | bytes 131104 | tf_op jit(solution)/shard_map/while/body/eval_jaxpr/ppermute | solution.py:14
  458.0 8.5 %collective-permute-done = f32[2,128,128]{2,1,0:T(8,128)S(1)} collective-permute-done((f32[2,128,128]{2,1,0:T(8,128)}, f32[2,128,128]{2,1,0:T(8,128)S(1)}, u32[]{:S(2)}, u32[]{:S(2)}) %collective-permute-start) | collective-permute-done | bytes 131104 | tf_op jit(solution)/shard_map/while/body/eval_jaxpr/ppermute | solution.py:14
  469.3 8.5 %collective-permute-done = f32[2,128,128]{2,1,0:T(8,128)S(1)} collective-permute-done((f32[2,128,128]{2,1,0:T(8,128)}, f32[2,128,128]{2,1,0:T(8,128)S(1)}, u32[]{:S(2)}, u32[]{:S(2)}) %collective-permute-start) | collective-permute-done | bytes 131104 | tf_op jit(solution)/shard_map/while/body/eval_jaxpr/ppermute | solution.py:14
  480.6 8.5 %collective-permute-done = f32[2,128,128]{2,1,0:T(8,128)S(1)} collective-permute-done((f32[2,128,128]{2,1,0:T(8,128)}, f32[2,128,128]{2,1,0:T(8,128)S(1)}, u32[]{:S(2)}, u32[]{:S(2)}) %collective-permute-start) | collective-permute-done | bytes 131104 | tf_op jit(solution)/shard_map/while/body/eval_jaxpr/ppermute | solution.py:14
  491.9 8.5 %collective-permute-done = f32[2,128,128]{2,1,0:T(8,128)S(1)} collective-permute-done((f32[2,128,128]{2,1,0:T(8,128)}, f32[2,128,128]{2,1,0:T(8,128)S(1)}, u32[]{:S(2)}, u32[]{:S(2)}) %collective-permute-start) | collective-permute-done | bytes 131104 | tf_op jit(solution)/shard_map/while/body/eval_jaxpr/ppermute | solution.py:14
  503.2 8.5 %collective-permute-done = f32[2,128,128]{2,1,0:T(8,128)S(1)} collective-permute-done((f32[2,128,128]{2,1,0:T(8,128)}, f32[2,128,128]{2,1,0:T(8,128)S(1)}, u32[]{:S(2)}, u32[]{:S(2)}) %collective-permute-start) | collective-permute-done | bytes 131104 | tf_op jit(solution)/shard_map/while/body/eval_jaxpr/ppermute | solution.py:14
  514.5 8.7 %collective-permute-done = f32[2,128,128]{2,1,0:T(8,128)S(1)} collective-permute-done((f32[2,128,128]{2,1,0:T(8,128)}, f32[2,128,128]{2,1,0:T(8,128)S(1)}, u32[]{:S(2)}, u32[]{:S(2)}) %collective-permute-start) | collective-permute-done | bytes 131104 | tf_op jit(solution)/shard_map/while/body/eval_jaxpr/ppermute | solution.py:14
  526.1 9.8 %collective-permute-done = f32[2,128,128]{2,1,0:T(8,128)S(1)} collective-permute-done((f32[2,128,128]{2,1,0:T(8,128)}, f32[2,128,128]{2,1,0:T(8,128)S(1)}, u32[]{:S(2)}, u32[]{:S(2)}) %collective-permute-start) | collective-permute-done | bytes 131104 | tf_op jit(solution)/shard_map/while/body/eval_jaxpr/ppermute | solution.py:14
  538.7 9.0 %collective-permute-done = f32[2,128,128]{2,1,0:T(8,128)S(1)} collective-permute-done((f32[2,128,128]{2,1,0:T(8,128)}, f32[2,128,128]{2,1,0:T(8,128)S(1)}, u32[]{:S(2)}, u32[]{:S(2)}) %collective-permute-start) | collective-permute-done | bytes 131104 | tf_op jit(solution)/shard_map/while/body/eval_jaxpr/ppermute | solution.py:14
  550.6 8.5 %collective-permute-done = f32[2,128,128]{2,1,0:T(8,128)S(1)} collective-permute-done((f32[2,128,128]{2,1,0:T(8,128)}, f32[2,128,128]{2,1,0:T(8,128)S(1)}, u32[]{:S(2)}, u32[]{:S(2)}) %collective-permute-start) | collective-permute-done | bytes 131104 | tf_op jit(solution)/shard_map/while/body/eval_jaxpr/ppermute | solution.py:14
  561.9 8.5 %collective-permute-done = f32[2,128,128]{2,1,0:T(8,128)S(1)} collective-permute-done((f32[2,128,128]{2,1,0:T(8,128)}, f32[2,128,128]{2,1,0:T(8,128)S(1)}, u32[]{:S(2)}, u32[]{:S(2)}) %collective-permute-start) | collective-permute-done | bytes 131104 | tf_op jit(solution)/shard_map/while/body/eval_jaxpr/ppermute | solution.py:14
  573.2 8.5 %collective-permute-done = f32[2,128,128]{2,1,0:T(8,128)S(1)} collective-permute-done((f32[2,128,128]{2,1,0:T(8,128)}, f32[2,128,128]{2,1,0:T(8,128)S(1)}, u32[]{:S(2)}, u32[]{:S(2)}) %collective-permute-start) | collective-permute-done | bytes 131104 | tf_op jit(solution)/shard_map/while/body/eval_jaxpr/ppermute | solution.py:14
  584.5 8.5 %collective-permute-done = f32[2,128,128]{2,1,0:T(8,128)S(1)} collective-permute-done((f32[2,128,128]{2,1,0:T(8,128)}, f32[2,128,128]{2,1,0:T(8,128)S(1)}, u32[]{:S(2)}, u32[]{:S(2)}) %collective-permute-start) | collective-permute-done | bytes 131104 | tf_op jit(solution)/shard_map/while/body/eval_jaxpr/ppermute | solution.py:14
  595.8 8.5 %collective-permute-done = f32[2,128,128]{2,1,0:T(8,128)S(1)} collective-permute-done((f32[2,128,128]{2,1,0:T(8,128)}, f32[2,128,128]{2,1,0:T(8,128)S(1)}, u32[]{:S(2)}, u32[]{:S(2)}) %collective-permute-start) | collective-permute-done | bytes 131104 | tf_op jit(solution)/shard_map/while/body/eval_jaxpr/ppermute | solution.py:14
  607.1 8.5 %collective-permute-done = f32[2,128,128]{2,1,0:T(8,128)S(1)} collective-permute-done((f32[2,128,128]{2,1,0:T(8,128)}, f32[2,128,128]{2,1,0:T(8,128)S(1)}, u32[]{:S(2)}, u32[]{:S(2)}) %collective-permute-start) | collective-permute-done | bytes 131104 | tf_op jit(solution)/shard_map/while/body/eval_jaxpr/ppermute | solution.py:14
  618.4 8.5 %collective-permute-done = f32[2,128,128]{2,1,0:T(8,128)S(1)} collective-permute-done((f32[2,128,128]{2,1,0:T(8,128)}, f32[2,128,128]{2,1,0:T(8,128)S(1)}, u32[]{:S(2)}, u32[]{:S(2)}) %collective-permute-start) | collective-permute-done | bytes 131104 | tf_op jit(solution)/shard_map/while/body/eval_jaxpr/ppermute | solution.py:14
  629.7 9.5 %collective-permute-done = f32[2,128,128]{2,1,0:T(8,128)S(1)} collective-permute-done((f32[2,128,128]{2,1,0:T(8,128)}, f32[2,128,128]{2,1,0:T(8,128)S(1)}, u32[]{:S(2)}, u32[]{:S(2)}) %collective-permute-start) | collective-permute-done | bytes 131104 | tf_op jit(solution)/shard_map/while/body/eval_jaxpr/ppermute | solution.py:14
  642.0 9.1 %collective-permute-done = f32[2,128,128]{2,1,0:T(8,128)S(1)} collective-permute-done((f32[2,128,128]{2,1,0:T(8,128)}, f32[2,128,128]{2,1,0:T(8,128)S(1)}, u32[]{:S(2)}, u32[]{:S(2)}) %collective-permute-start) | collective-permute-done | bytes 131104 | tf_op jit(solution)/shard_map/while/body/eval_jaxpr/ppermute | solution.py:14
  654.0 8.5 %collective-permute-done = f32[2,128,128]{2,1,0:T(8,128)S(1)} collective-permute-done((f32[2,128,128]{2,1,0:T(8,128)}, f32[2,128,128]{2,1,0:T(8,128)S(1)}, u32[]{:S(2)}, u32[]{:S(2)}) %collective-permute-start) | collective-permute-done | bytes 131104 | tf_op jit(solution)/shard_map/while/body/eval_jaxpr/ppermute | solution.py:14
  665.3 8.5 %collective-permute-done = f32[2,128,128]{2,1,0:T(8,128)S(1)} collective-permute-done((f32[2,128,128]{2,1,0:T(8,128)}, f32[2,128,128]{2,1,0:T(8,128)S(1)}, u32[]{:S(2)}, u32[]{:S(2)}) %collective-permute-start) | collective-permute-done | bytes 131104 | tf_op jit(solution)/shard_map/while/body/eval_jaxpr/ppermute | solution.py:14
  676.6 8.5 %collective-permute-done = f32[2,128,128]{2,1,0:T(8,128)S(1)} collective-permute-done((f32[2,128,128]{2,1,0:T(8,128)}, f32[2,128,128]{2,1,0:T(8,128)S(1)}, u32[]{:S(2)}, u32[]{:S(2)}) %collective-permute-start) | collective-permute-done | bytes 131104 | tf_op jit(solution)/shard_map/while/body/eval_jaxpr/ppermute | solution.py:14
  687.9 8.5 %collective-permute-done = f32[2,128,128]{2,1,0:T(8,128)S(1)} collective-permute-done((f32[2,128,128]{2,1,0:T(8,128)}, f32[2,128,128]{2,1,0:T(8,128)S(1)}, u32[]{:S(2)}, u32[]{:S(2)}) %collective-permute-start) | collective-permute-done | bytes 131104 | tf_op jit(solution)/shard_map/while/body/eval_jaxpr/ppermute | solution.py:14
  699.2 8.5 %collective-permute-done = f32[2,128,128]{2,1,0:T(8,128)S(1)} collective-permute-done((f32[2,128,128]{2,1,0:T(8,128)}, f32[2,128,128]{2,1,0:T(8,128)S(1)}, u32[]{:S(2)}, u32[]{:S(2)}) %collective-permute-start) | collective-permute-done | bytes 131104 | tf_op jit(solution)/shard_map/while/body/eval_jaxpr/ppermute | solution.py:14
  708.6 2.5 fusion
  711.2 2.1 convolution_multiply_fusion.2
  713.4 2.1 fusion.5
  715.5 2.3 convolution_subtract_fusion
  719.7 11.4 %all_to_all.15 = bf16[8,64,256]{2,1,0:T(8,128)(2,1)S(1)} all-to-all(bf16[8,64,256]{2,1,0:T(8,128)(2,1)S(1)} %convert_element_type.33), channel_id=1, replica_groups=mesh['ctx'=32,'head'=8] {'head'}, dimensions={0} | all-to-all | bytes 524288 | tf_op jit(solution)/shard_map/all_to_all | solution.py:132
  731.2 6.7 convolution_convert_fusion
  (183 shorter events, 118.2 us)
Async XLA Ops:
  6.5 64.3 %copy-start = (bf16[512,2048]{1,0:T(8,128)(2,1)S(1)}, bf16[512,2048]{1,0:T(8,128)(2,1)}, u32[]{:S(2)}) copy-start(bf16[512,2048]{1,0:T(8,128)(2,1)} %param.10) | copy-start | bytes 6291460
  6.5 65.0 %copy-start.25 = (f32[2]{0:T(128)S(1)}, f32[2]{0:T(128)}, u32[]{:S(2)}) copy-start(f32[2]{0:T(128)} %param.14) | copy-start | bytes 28
  6.5 66.6 %copy-start.24 = (f32[2,2]{1,0:T(2,128)S(1)}, f32[2,2]{1,0:T(2,128)}, u32[]{:S(2)}) copy-start(f32[2,2]{1,0:T(2,128)} %param.13) | copy-start | bytes 52
  6.5 86.9 %all-gather.4.cloned.1.call-start = ((), (), s32[]{:S(2)}) async-start(), calls=%async_computation.1 | async-start | bytes 5406720 | tf_op jit(solution)/shard_map/all_gather | solution.py:36
  7.3 723.9 %all-gather.6.cloned.1.call-start = ((), (), s32[]{:S(2)}) async-start(), calls=%async_computation.2 | async-start | bytes 8650752 | tf_op jit(solution)/shard_map/all_gather | solution.py:126
  21.8 245.6 %copy-start.17 = (f32[128,128]{1,0:T(8,128)}, f32[128,128]{1,0:T(8,128)S(1)}, u32[]{:S(2)}) copy-start(f32[128,128]{1,0:T(8,128)S(1)} %fusion.44) | copy-start | bytes 196612
  73.1 25.2 %copy-start.20 = (f32[2,8,64]{2,1,0:T(8,128)}, f32[2,8,64]{2,1,0:T(8,128)S(1)}, u32[]{:S(2)}) copy-start(f32[2,8,64]{2,1,0:T(8,128)S(1)} %slice.117) | copy-start | bytes 12292
  73.8 193.6 %copy-start.18 = (f32[2,8,128]{2,1,0:T(8,128)}, f32[2,8,128]{2,1,0:T(8,128)S(1)}, u32[]{:S(2)}) copy-start(f32[2,8,128]{2,1,0:T(8,128)S(1)} %get-tuple-element.39) | copy-start | bytes 24580
  98.3 2.2 copy-start.7
  267.4 3.9 copy-start.5
  269.6 1.0 copy-start.1
  271.3 0.8 copy-start.8
  271.7 0.6 copy-start.16
  297.9 1.7 copy-start.11
  297.9 3.6 copy-start.19
  299.6 4.1 copy-start.2
  301.5 2.9 copy-start.3
  301.5 2.9 copy-start.9
  303.7 1.7 copy-start.12
  304.9 0.7 copy-start.15
  310.7 9.6 %slice-start.1 = ((f32[2,8,128,128]{3,2,1,0:T(8,128)}), f32[2,1,128,128]{3,2,1,0:T(8,128)S(1)}, s32[]{:S(2)}) async-start(f32[2,8,128,128]{3,2,1,0:T(8,128)} %copy-done.12), calls=%async_computation.4 | async-start | bytes 262144 | tf_op jit(solution)/shard_map/slice | solution.py:88
  326.8 12.4 %slice-start = ((f32[2,8,128,128]{3,2,1,0:T(8,128)}), f32[2,1,128,128]{3,2,1,0:T(8,128)S(1)}, s32[]{:S(2)}) async-start(f32[2,8,128,128]{3,2,1,0:T(8,128)} %copy-done.1), calls=%async_computation.3 | async-start | bytes 262144 | tf_op jit(solution)/shard_map/slice | solution.py:88
  345.8 4.6 copy-start.13
  345.8 4.6 copy-start.14
  351.5 359.7 %copy-start.23 = (f32[2,8,64]{2,1,0:T(8,128)S(1)}, f32[2,8,64]{2,1,0:T(8,128)}, u32[]{:S(2)}) copy-start(f32[2,8,64]{2,1,0:T(8,128)} %exp.39) | copy-start | bytes 12292
  352.5 10.4 %collective-permute-start = (f32[2,128,128]{2,1,0:T(8,128)}, f32[2,128,128]{2,1,0:T(8,128)S(1)}, u32[]{:S(2)}, u32[]{:S(2)}) collective-permute-start(f32[2,128,128]{2,1,0:T(8,128)} %convolution_add_fusion.6), channel_id=1, source_target_pairs={{0,8},{8,16},{16,24},{24,32},{32,40},{40,48},{48,56},{56,64},{64,7... | collective-permute-start | bytes 393224 | tf_op jit(solution)/shard_map/while/body/eval_jaxpr/ppermute | solution.py:14
  363.8 10.4 %collective-permute-start = (f32[2,128,128]{2,1,0:T(8,128)}, f32[2,128,128]{2,1,0:T(8,128)S(1)}, u32[]{:S(2)}, u32[]{:S(2)}) collective-permute-start(f32[2,128,128]{2,1,0:T(8,128)} %convolution_add_fusion.6), channel_id=1, source_target_pairs={{0,8},{8,16},{16,24},{24,32},{32,40},{40,48},{48,56},{56,64},{64,7... | collective-permute-start | bytes 393224 | tf_op jit(solution)/shard_map/while/body/eval_jaxpr/ppermute | solution.py:14
  375.1 10.4 %collective-permute-start = (f32[2,128,128]{2,1,0:T(8,128)}, f32[2,128,128]{2,1,0:T(8,128)S(1)}, u32[]{:S(2)}, u32[]{:S(2)}) collective-permute-start(f32[2,128,128]{2,1,0:T(8,128)} %convolution_add_fusion.6), channel_id=1, source_target_pairs={{0,8},{8,16},{16,24},{24,32},{32,40},{40,48},{48,56},{56,64},{64,7... | collective-permute-start | bytes 393224 | tf_op jit(solution)/shard_map/while/body/eval_jaxpr/ppermute | solution.py:14
  386.4 10.4 %collective-permute-start = (f32[2,128,128]{2,1,0:T(8,128)}, f32[2,128,128]{2,1,0:T(8,128)S(1)}, u32[]{:S(2)}, u32[]{:S(2)}) collective-permute-start(f32[2,128,128]{2,1,0:T(8,128)} %convolution_add_fusion.6), channel_id=1, source_target_pairs={{0,8},{8,16},{16,24},{24,32},{32,40},{40,48},{48,56},{56,64},{64,7... | collective-permute-start | bytes 393224 | tf_op jit(solution)/shard_map/while/body/eval_jaxpr/ppermute | solution.py:14
  397.7 10.4 %collective-permute-start = (f32[2,128,128]{2,1,0:T(8,128)}, f32[2,128,128]{2,1,0:T(8,128)S(1)}, u32[]{:S(2)}, u32[]{:S(2)}) collective-permute-start(f32[2,128,128]{2,1,0:T(8,128)} %convolution_add_fusion.6), channel_id=1, source_target_pairs={{0,8},{8,16},{16,24},{24,32},{32,40},{40,48},{48,56},{56,64},{64,7... | collective-permute-start | bytes 393224 | tf_op jit(solution)/shard_map/while/body/eval_jaxpr/ppermute | solution.py:14
  409.0 11.0 %collective-permute-start = (f32[2,128,128]{2,1,0:T(8,128)}, f32[2,128,128]{2,1,0:T(8,128)S(1)}, u32[]{:S(2)}, u32[]{:S(2)}) collective-permute-start(f32[2,128,128]{2,1,0:T(8,128)} %convolution_add_fusion.6), channel_id=1, source_target_pairs={{0,8},{8,16},{16,24},{24,32},{32,40},{40,48},{48,56},{56,64},{64,7... | collective-permute-start | bytes 393224 | tf_op jit(solution)/shard_map/while/body/eval_jaxpr/ppermute | solution.py:14
  420.9 11.4 %collective-permute-start = (f32[2,128,128]{2,1,0:T(8,128)}, f32[2,128,128]{2,1,0:T(8,128)S(1)}, u32[]{:S(2)}, u32[]{:S(2)}) collective-permute-start(f32[2,128,128]{2,1,0:T(8,128)} %convolution_add_fusion.6), channel_id=1, source_target_pairs={{0,8},{8,16},{16,24},{24,32},{32,40},{40,48},{48,56},{56,64},{64,7... | collective-permute-start | bytes 393224 | tf_op jit(solution)/shard_map/while/body/eval_jaxpr/ppermute | solution.py:14
  433.3 10.6 %collective-permute-start = (f32[2,128,128]{2,1,0:T(8,128)}, f32[2,128,128]{2,1,0:T(8,128)S(1)}, u32[]{:S(2)}, u32[]{:S(2)}) collective-permute-start(f32[2,128,128]{2,1,0:T(8,128)} %convolution_add_fusion.6), channel_id=1, source_target_pairs={{0,8},{8,16},{16,24},{24,32},{32,40},{40,48},{48,56},{56,64},{64,7... | collective-permute-start | bytes 393224 | tf_op jit(solution)/shard_map/while/body/eval_jaxpr/ppermute | solution.py:14
  444.8 10.4 %collective-permute-start = (f32[2,128,128]{2,1,0:T(8,128)}, f32[2,128,128]{2,1,0:T(8,128)S(1)}, u32[]{:S(2)}, u32[]{:S(2)}) collective-permute-start(f32[2,128,128]{2,1,0:T(8,128)} %convolution_add_fusion.6), channel_id=1, source_target_pairs={{0,8},{8,16},{16,24},{24,32},{32,40},{40,48},{48,56},{56,64},{64,7... | collective-permute-start | bytes 393224 | tf_op jit(solution)/shard_map/while/body/eval_jaxpr/ppermute | solution.py:14
  456.1 10.4 %collective-permute-start = (f32[2,128,128]{2,1,0:T(8,128)}, f32[2,128,128]{2,1,0:T(8,128)S(1)}, u32[]{:S(2)}, u32[]{:S(2)}) collective-permute-start(f32[2,128,128]{2,1,0:T(8,128)} %convolution_add_fusion.6), channel_id=1, source_target_pairs={{0,8},{8,16},{16,24},{24,32},{32,40},{40,48},{48,56},{56,64},{64,7... | collective-permute-start | bytes 393224 | tf_op jit(solution)/shard_map/while/body/eval_jaxpr/ppermute | solution.py:14
  467.4 10.4 %collective-permute-start = (f32[2,128,128]{2,1,0:T(8,128)}, f32[2,128,128]{2,1,0:T(8,128)S(1)}, u32[]{:S(2)}, u32[]{:S(2)}) collective-permute-start(f32[2,128,128]{2,1,0:T(8,128)} %convolution_add_fusion.6), channel_id=1, source_target_pairs={{0,8},{8,16},{16,24},{24,32},{32,40},{40,48},{48,56},{56,64},{64,7... | collective-permute-start | bytes 393224 | tf_op jit(solution)/shard_map/while/body/eval_jaxpr/ppermute | solution.py:14
  478.7 10.4 %collective-permute-start = (f32[2,128,128]{2,1,0:T(8,128)}, f32[2,128,128]{2,1,0:T(8,128)S(1)}, u32[]{:S(2)}, u32[]{:S(2)}) collective-permute-start(f32[2,128,128]{2,1,0:T(8,128)} %convolution_add_fusion.6), channel_id=1, source_target_pairs={{0,8},{8,16},{16,24},{24,32},{32,40},{40,48},{48,56},{56,64},{64,7... | collective-permute-start | bytes 393224 | tf_op jit(solution)/shard_map/while/body/eval_jaxpr/ppermute | solution.py:14
  490.0 10.4 %collective-permute-start = (f32[2,128,128]{2,1,0:T(8,128)}, f32[2,128,128]{2,1,0:T(8,128)S(1)}, u32[]{:S(2)}, u32[]{:S(2)}) collective-permute-start(f32[2,128,128]{2,1,0:T(8,128)} %convolution_add_fusion.6), channel_id=1, source_target_pairs={{0,8},{8,16},{16,24},{24,32},{32,40},{40,48},{48,56},{56,64},{64,7... | collective-permute-start | bytes 393224 | tf_op jit(solution)/shard_map/while/body/eval_jaxpr/ppermute | solution.py:14
  501.3 10.4 %collective-permute-start = (f32[2,128,128]{2,1,0:T(8,128)}, f32[2,128,128]{2,1,0:T(8,128)S(1)}, u32[]{:S(2)}, u32[]{:S(2)}) collective-permute-start(f32[2,128,128]{2,1,0:T(8,128)} %convolution_add_fusion.6), channel_id=1, source_target_pairs={{0,8},{8,16},{16,24},{24,32},{32,40},{40,48},{48,56},{56,64},{64,7... | collective-permute-start | bytes 393224 | tf_op jit(solution)/shard_map/while/body/eval_jaxpr/ppermute | solution.py:14
  512.6 10.6 %collective-permute-start = (f32[2,128,128]{2,1,0:T(8,128)}, f32[2,128,128]{2,1,0:T(8,128)S(1)}, u32[]{:S(2)}, u32[]{:S(2)}) collective-permute-start(f32[2,128,128]{2,1,0:T(8,128)} %convolution_add_fusion.6), channel_id=1, source_target_pairs={{0,8},{8,16},{16,24},{24,32},{32,40},{40,48},{48,56},{56,64},{64,7... | collective-permute-start | bytes 393224 | tf_op jit(solution)/shard_map/while/body/eval_jaxpr/ppermute | solution.py:14
  524.1 11.7 %collective-permute-start = (f32[2,128,128]{2,1,0:T(8,128)}, f32[2,128,128]{2,1,0:T(8,128)S(1)}, u32[]{:S(2)}, u32[]{:S(2)}) collective-permute-start(f32[2,128,128]{2,1,0:T(8,128)} %convolution_add_fusion.6), channel_id=1, source_target_pairs={{0,8},{8,16},{16,24},{24,32},{32,40},{40,48},{48,56},{56,64},{64,7... | collective-permute-start | bytes 393224 | tf_op jit(solution)/shard_map/while/body/eval_jaxpr/ppermute | solution.py:14
  536.8 10.9 %collective-permute-start = (f32[2,128,128]{2,1,0:T(8,128)}, f32[2,128,128]{2,1,0:T(8,128)S(1)}, u32[]{:S(2)}, u32[]{:S(2)}) collective-permute-start(f32[2,128,128]{2,1,0:T(8,128)} %convolution_add_fusion.6), channel_id=1, source_target_pairs={{0,8},{8,16},{16,24},{24,32},{32,40},{40,48},{48,56},{56,64},{64,7... | collective-permute-start | bytes 393224 | tf_op jit(solution)/shard_map/while/body/eval_jaxpr/ppermute | solution.py:14
  548.6 10.4 %collective-permute-start = (f32[2,128,128]{2,1,0:T(8,128)}, f32[2,128,128]{2,1,0:T(8,128)S(1)}, u32[]{:S(2)}, u32[]{:S(2)}) collective-permute-start(f32[2,128,128]{2,1,0:T(8,128)} %convolution_add_fusion.6), channel_id=1, source_target_pairs={{0,8},{8,16},{16,24},{24,32},{32,40},{40,48},{48,56},{56,64},{64,7... | collective-permute-start | bytes 393224 | tf_op jit(solution)/shard_map/while/body/eval_jaxpr/ppermute | solution.py:14
  560.0 10.4 %collective-permute-start = (f32[2,128,128]{2,1,0:T(8,128)}, f32[2,128,128]{2,1,0:T(8,128)S(1)}, u32[]{:S(2)}, u32[]{:S(2)}) collective-permute-start(f32[2,128,128]{2,1,0:T(8,128)} %convolution_add_fusion.6), channel_id=1, source_target_pairs={{0,8},{8,16},{16,24},{24,32},{32,40},{40,48},{48,56},{56,64},{64,7... | collective-permute-start | bytes 393224 | tf_op jit(solution)/shard_map/while/body/eval_jaxpr/ppermute | solution.py:14
  571.3 10.4 %collective-permute-start = (f32[2,128,128]{2,1,0:T(8,128)}, f32[2,128,128]{2,1,0:T(8,128)S(1)}, u32[]{:S(2)}, u32[]{:S(2)}) collective-permute-start(f32[2,128,128]{2,1,0:T(8,128)} %convolution_add_fusion.6), channel_id=1, source_target_pairs={{0,8},{8,16},{16,24},{24,32},{32,40},{40,48},{48,56},{56,64},{64,7... | collective-permute-start | bytes 393224 | tf_op jit(solution)/shard_map/while/body/eval_jaxpr/ppermute | solution.py:14
  582.6 10.4 %collective-permute-start = (f32[2,128,128]{2,1,0:T(8,128)}, f32[2,128,128]{2,1,0:T(8,128)S(1)}, u32[]{:S(2)}, u32[]{:S(2)}) collective-permute-start(f32[2,128,128]{2,1,0:T(8,128)} %convolution_add_fusion.6), channel_id=1, source_target_pairs={{0,8},{8,16},{16,24},{24,32},{32,40},{40,48},{48,56},{56,64},{64,7... | collective-permute-start | bytes 393224 | tf_op jit(solution)/shard_map/while/body/eval_jaxpr/ppermute | solution.py:14
  593.9 10.4 %collective-permute-start = (f32[2,128,128]{2,1,0:T(8,128)}, f32[2,128,128]{2,1,0:T(8,128)S(1)}, u32[]{:S(2)}, u32[]{:S(2)}) collective-permute-start(f32[2,128,128]{2,1,0:T(8,128)} %convolution_add_fusion.6), channel_id=1, source_target_pairs={{0,8},{8,16},{16,24},{24,32},{32,40},{40,48},{48,56},{56,64},{64,7... | collective-permute-start | bytes 393224 | tf_op jit(solution)/shard_map/while/body/eval_jaxpr/ppermute | solution.py:14
  605.2 10.4 %collective-permute-start = (f32[2,128,128]{2,1,0:T(8,128)}, f32[2,128,128]{2,1,0:T(8,128)S(1)}, u32[]{:S(2)}, u32[]{:S(2)}) collective-permute-start(f32[2,128,128]{2,1,0:T(8,128)} %convolution_add_fusion.6), channel_id=1, source_target_pairs={{0,8},{8,16},{16,24},{24,32},{32,40},{40,48},{48,56},{56,64},{64,7... | collective-permute-start | bytes 393224 | tf_op jit(solution)/shard_map/while/body/eval_jaxpr/ppermute | solution.py:14
  616.5 10.4 %collective-permute-start = (f32[2,128,128]{2,1,0:T(8,128)}, f32[2,128,128]{2,1,0:T(8,128)S(1)}, u32[]{:S(2)}, u32[]{:S(2)}) collective-permute-start(f32[2,128,128]{2,1,0:T(8,128)} %convolution_add_fusion.6), channel_id=1, source_target_pairs={{0,8},{8,16},{16,24},{24,32},{32,40},{40,48},{48,56},{56,64},{64,7... | collective-permute-start | bytes 393224 | tf_op jit(solution)/shard_map/while/body/eval_jaxpr/ppermute | solution.py:14
  627.8 11.4 %collective-permute-start = (f32[2,128,128]{2,1,0:T(8,128)}, f32[2,128,128]{2,1,0:T(8,128)S(1)}, u32[]{:S(2)}, u32[]{:S(2)}) collective-permute-start(f32[2,128,128]{2,1,0:T(8,128)} %convolution_add_fusion.6), channel_id=1, source_target_pairs={{0,8},{8,16},{16,24},{24,32},{32,40},{40,48},{48,56},{56,64},{64,7... | collective-permute-start | bytes 393224 | tf_op jit(solution)/shard_map/while/body/eval_jaxpr/ppermute | solution.py:14
  640.1 11.0 %collective-permute-start = (f32[2,128,128]{2,1,0:T(8,128)}, f32[2,128,128]{2,1,0:T(8,128)S(1)}, u32[]{:S(2)}, u32[]{:S(2)}) collective-permute-start(f32[2,128,128]{2,1,0:T(8,128)} %convolution_add_fusion.6), channel_id=1, source_target_pairs={{0,8},{8,16},{16,24},{24,32},{32,40},{40,48},{48,56},{56,64},{64,7... | collective-permute-start | bytes 393224 | tf_op jit(solution)/shard_map/while/body/eval_jaxpr/ppermute | solution.py:14
  652.1 10.4 %collective-permute-start = (f32[2,128,128]{2,1,0:T(8,128)}, f32[2,128,128]{2,1,0:T(8,128)S(1)}, u32[]{:S(2)}, u32[]{:S(2)}) collective-permute-start(f32[2,128,128]{2,1,0:T(8,128)} %convolution_add_fusion.6), channel_id=1, source_target_pairs={{0,8},{8,16},{16,24},{24,32},{32,40},{40,48},{48,56},{56,64},{64,7... | collective-permute-start | bytes 393224 | tf_op jit(solution)/shard_map/while/body/eval_jaxpr/ppermute | solution.py:14
  663.4 10.4 %collective-permute-start = (f32[2,128,128]{2,1,0:T(8,128)}, f32[2,128,128]{2,1,0:T(8,128)S(1)}, u32[]{:S(2)}, u32[]{:S(2)}) collective-permute-start(f32[2,128,128]{2,1,0:T(8,128)} %convolution_add_fusion.6), channel_id=1, source_target_pairs={{0,8},{8,16},{16,24},{24,32},{32,40},{40,48},{48,56},{56,64},{64,7... | collective-permute-start | bytes 393224 | tf_op jit(solution)/shard_map/while/body/eval_jaxpr/ppermute | solution.py:14
  674.7 10.4 %collective-permute-start = (f32[2,128,128]{2,1,0:T(8,128)}, f32[2,128,128]{2,1,0:T(8,128)S(1)}, u32[]{:S(2)}, u32[]{:S(2)}) collective-permute-start(f32[2,128,128]{2,1,0:T(8,128)} %convolution_add_fusion.6), channel_id=1, source_target_pairs={{0,8},{8,16},{16,24},{24,32},{32,40},{40,48},{48,56},{56,64},{64,7... | collective-permute-start | bytes 393224 | tf_op jit(solution)/shard_map/while/body/eval_jaxpr/ppermute | solution.py:14
  686.0 10.4 %collective-permute-start = (f32[2,128,128]{2,1,0:T(8,128)}, f32[2,128,128]{2,1,0:T(8,128)S(1)}, u32[]{:S(2)}, u32[]{:S(2)}) collective-permute-start(f32[2,128,128]{2,1,0:T(8,128)} %convolution_add_fusion.6), channel_id=1, source_target_pairs={{0,8},{8,16},{16,24},{24,32},{32,40},{40,48},{48,56},{56,64},{64,7... | collective-permute-start | bytes 393224 | tf_op jit(solution)/shard_map/while/body/eval_jaxpr/ppermute | solution.py:14
  697.3 10.4 %collective-permute-start = (f32[2,128,128]{2,1,0:T(8,128)}, f32[2,128,128]{2,1,0:T(8,128)S(1)}, u32[]{:S(2)}, u32[]{:S(2)}) collective-permute-start(f32[2,128,128]{2,1,0:T(8,128)} %convolution_add_fusion.6), channel_id=1, source_target_pairs={{0,8},{8,16},{16,24},{24,32},{32,40},{40,48},{48,56},{56,64},{64,7... | collective-permute-start | bytes 393224 | tf_op jit(solution)/shard_map/while/body/eval_jaxpr/ppermute | solution.py:14
  707.7 3.5 copy-start.10
  708.6 4.8 copy-start.21
  708.6 4.8 copy-start.22
  711.2 4.4 copy-start.4
  711.2 4.4 copy-start.6
Sparse Core Ops, SparseCore 0:
  9.9 83.4 all-gather.3
  96.0 96.2 all-gather.5
where the time goes:
time: 748 us; the launch traced here: 745 us
  waiting for transfers between devices  287 us (38%)
  other arithmetic  182 us (24%)
  blocking collectives  74.8 us (10%)
  matrix products  70.9 us (9%)
  starting transfers between devices  59.6 us (8%)
  local copies, waits for them, and re-layouts  56.5 us (8%)
  between operations  14.1 us (2%)
    ppermute x31, waiting for transfers between devices, from_behind(): return lax.ppermute(array, axis, pairs)  268 us
    another operation x2, other arithmetic, shards(): lax.linalg.triangular_solve(system, (beta_steps * jnp.exp(running))[...,...  159 us
    ppermute x31, starting transfers between devices, from_behind(): return lax.ppermute(array, axis, pairs)  59.5 us
    all_gather x1, blocking collectives, shards(): lax.all_gather(w_small, 'ctx', axis=0, tiled=True)  48.9 us
    dot_general x41, matrix products, matrix_product(): return jnp.matmul(left, right, precision=HIGHEST_PRECISION)  35.3 us
    pad x7, local copies, waits for them, and re-layouts, shards(): inclusive = lax.associative_scan(compose, (transitions, writes), axis=1)  28.8 us
    all_gather x1, waiting for transfers between devices, shards(): lax.all_gather(w_proj, 'ctx', axis=0, tiled=True)  18.3 us
  transfers between devices with their start and end apart: 33, of which 32 were waited for; matrix products, arithmetic and copies ran while one was open for 40% of the time, Pallas kernels for 0%

commit v1 on v0

v1 whole, which is shorter than its diff:
```python
import functools

import jax
import jax.numpy as jnp
from jax import lax
from jax.experimental import pallas as pl
from jax.experimental.pallas import tpu as pltpu
from jax.sharding import PartitionSpec as P

F32 = jnp.float32
BF16 = jnp.bfloat16
LANES = 128
BLOCK = 64
ROWS = (((1,), (0,)), ((), ()))
NT = (((1,), (1,)), ((), ()))
TN = (((0,), (0,)), ((), ()))


def split(array):
    high = array.astype(BF16)
    return high, (array - high.astype(F32)).astype(BF16)


def dot1(left, right, dims):
    return lax.dot_general(left, right, dims, preferred_element_type=F32)


def dot3(left, right, dims):
    return (
        dot1(left[0], right[0], dims)
        + dot1(left[0], right[1], dims)
        + dot1(left[1], right[0], dims)
    )


def shift(array, by):
    count = lax.axis_size("ctx")
    return lax.ppermute(array, "ctx", [(i, i + by) for i in range(count - by)])


def around(array, y_size, dz, dy):
    count = lax.axis_size("ctx")
    z_size = count // y_size
    pairs = [
        (z * y_size + y, ((z + dz) % z_size) * y_size + (y + dy) % y_size)
        for z in range(z_size)
        for y in range(y_size)
    ]
    return lax.ppermute(array, "ctx", pairs)


def unit(rows):
    return rows / jnp.sqrt(jnp.sum(rows * rows, axis=-1, keepdims=True) + 1e-06)


def local_kernel(head, proj_ref, gate_ref, row_ref, state_ref, query_ref, out_ref):
    tokens = proj_ref.shape[0]
    width = LANES
    blocks = tokens // BLOCK
    span = 2 * BLOCK
    gates = gate_ref[...]
    bias = row_ref[0:1, :]
    rate = row_ref[1:2, :]
    betas = 2.0 / (1.0 + jnp.exp(-(gates + bias)))
    soft = jnp.maximum(gates, 0.0) + jnp.log1p(jnp.exp(-jnp.abs(gates)))
    log_decay = -rate * soft
    row64 = lax.broadcasted_iota(jnp.int32, (BLOCK, BLOCK), 0)
    col64 = lax.broadcasted_iota(jnp.int32, (BLOCK, BLOCK), 1)
    lower = jnp.where(row64 >= col64, 1.0, 0.0).astype(F32)
    base = 3 * head
    row_i = lax.broadcasted_iota(jnp.int32, (span, span), 0)
    col_i = lax.broadcasted_iota(jnp.int32, (span, span), 1)
    row_t, row_r = row_i % BLOCK, row_i // BLOCK
    col_t, col_r = col_i % BLOCK, col_i // BLOCK
    strict = (row_t > col_t) | ((row_t == col_t) & (row_r > col_r))
    within = (row_t == col_t) & (row_r > col_r)
    eye = jnp.where(row_i == col_i, 1.0, 0.0).astype(F32)
    visible = (
        lax.broadcasted_iota(jnp.int32, (BLOCK, span), 0)
        >= lax.broadcasted_iota(jnp.int32, (BLOCK, span), 1) % BLOCK
    )
    levels = []
    size = 1
    while size < BLOCK:
        levels.append(
            (row_t // (2 * size) == col_t // (2 * size))
            & ((row_t // size) % 2 == 1)
            & ((col_t // size) % 2 == 0)
        )
        size *= 2

    def prepare(n):
        rows = slice(n * BLOCK, (n + 1) * BLOCK)
        query = unit(proj_ref[rows, 0:width])
        keys = jnp.concatenate(
            [
                unit(proj_ref[rows, width : 2 * width]),
                unit(proj_ref[rows, 2 * width : 3 * width]),
            ],
            axis=0,
        )
        values = jnp.concatenate(
            [proj_ref[rows, 3 * width : 4 * width], proj_ref[rows, 4 * width : 5 * width]], axis=0
        )
        beta = jnp.concatenate(
            [betas[rows, base : base + 1], betas[rows, base + 1 : base + 2]], axis=0
        )
        running = jnp.dot(
            lower, log_decay[rows], precision=lax.Precision.HIGHEST, preferred_element_type=F32
        )
        across = jnp.transpose(running)[base + 2 : base + 3, :]
        down = running[:, base + 2 : base + 3]
        across = jnp.concatenate([across, across], axis=1)
        reach = jnp.exp(jnp.where(visible, down - across, 0.0))
        keys_s = split(keys)
        both = jnp.concatenate([query, keys], axis=0)
        scores = dot3(split(both), keys_s, NT)
        attend = jnp.where(visible, reach, 0.0) * scores[:BLOCK]
        system = jnp.where(
            strict, beta * jnp.concatenate([reach, reach], axis=0) * scores[BLOCK:], 0.0
        )
        grow = jnp.exp(down)
        grow2 = jnp.concatenate([grow, grow], axis=0)
        last = running[BLOCK - 1 : BLOCK, base + 2 : base + 3]
        tail = jnp.exp(last - down)
        tail2 = jnp.concatenate([tail, tail], axis=0)
        right = jnp.concatenate([beta * grow2 * keys, beta * values], axis=1)
        return dict(
            query=query * grow,
            keys=keys_s,
            attend=attend,
            system=system,
            right=right,
            tail=tail2,
            last=jnp.exp(last),
            inverse=eye - jnp.where(within, system, 0.0),
        )

    parts = [prepare(n) for n in range(blocks)]
    for level in levels:
        for part in parts:
            inverse = split(part["inverse"])
            corner = split(jnp.where(level, part["system"], 0.0))
            middle = dot3(corner, inverse, ROWS)
            part["inverse"] = part["inverse"] - dot3(inverse, split(middle), ROWS)
    for part in parts:
        solved = dot3(split(part["inverse"]), split(part["right"]), ROWS)
        part["step"] = dot3(split(solved * part["tail"]), part["keys"], TN)
        seen = dot3(split(part["attend"]), split(solved), ROWS)
        part["query"] = part["query"] - seen[:, :width]
        part["seen"] = seen[:, width:]
    zero = jnp.zeros((width, width), F32)
    state = jnp.concatenate([eye, zero], axis=0)
    for n, part in enumerate(parts):
        rows = slice(n * BLOCK, (n + 1) * BLOCK)
        state_s = split(state)
        reads = dot3(split(part["query"]), state_s, NT)
        query_ref[rows, :] = reads[:, :width]
        out_ref[rows, :] = reads[:, width:] + part["seen"]
        move = part["last"] * eye - part["step"][:width]
        state = dot3(state_s, split(move), ROWS)
        state = state + jnp.concatenate([zero, part["step"][width:]], axis=0)
    state_ref[...] = state


def local_pass(proj, gates, rows, head):
    tokens = proj.shape[0]
    whole = lambda: (0, 0)
    return pl.pallas_call(
        functools.partial(local_kernel, head),
        out_shape=(
            jax.ShapeDtypeStruct((2 * LANES, LANES), F32),
            jax.ShapeDtypeStruct((tokens, LANES), F32),
            jax.ShapeDtypeStruct((tokens, LANES), F32),
        ),
        name=f"local{head}",
    )(proj, gates, rows)


def finish_kernel(state_ref, query_ref, part_ref, out_ref):
    heads = state_ref.shape[0]
    for head in range(heads):
        total = part_ref[head] + dot3(split(query_ref[head]), split(state_ref[head]), NT)
        scale = jnp.sqrt(jnp.mean(total * total, axis=-1, keepdims=True) + 1e-06)
        out_ref[:, head * LANES : (head + 1) * LANES] = (total / scale).astype(BF16)


def compose_kernel(before_ref, now_ref, out_ref):
    for head in range(now_ref.shape[0]):
        now = now_ref[head]
        moved = dot3(
            split(before_ref[head].astype(F32)), split(now[:LANES].astype(F32)), ROWS
        )
        rows = before_ref.shape[1]
        if rows > LANES:
            out_ref[head, : rows - LANES] = moved[: rows - LANES]
        out_ref[head, rows - LANES :] = moved[rows - LANES :] + now[LANES:].astype(F32)


def compose(before, now):
    return pl.pallas_call(
        compose_kernel,
        out_shape=jax.ShapeDtypeStruct(before.shape, F32),
        name="compose",
    )(before, now)


def shards(tokens, w_proj, w_small, beta_bias, decay_rate, w_out):
    tok_rows = tokens.shape[0]
    heads_here = beta_bias.shape[0]
    mirrors = beta_bias.shape[1]
    each = w_proj.shape[1] // heads_here
    small = jnp.pad(w_small, ((0, 0), (0, LANES - w_small.shape[1])))
    joined = jnp.concatenate([w_proj, small], axis=1)
    weights = lax.all_gather(joined, "ctx", axis=0, tiled=True)
    projected = jnp.dot(tokens, weights, preferred_element_type=F32)
    gates = projected[:, heads_here * each :]
    bias = jnp.pad(beta_bias, ((0, 0), (0, 1))).reshape(1, -1)
    rate = jnp.pad(decay_rate[:, None], ((0, 0), (mirrors, 0))).reshape(1, -1)
    rows = jnp.concatenate([bias, rate], axis=0)
    rows = jnp.pad(rows, ((0, 6), (0, LANES - rows.shape[1])))
    found = [
        local_pass(projected[:, head * each : (head + 1) * each], gates, rows, head)
        for head in range(heads_here)
    ]
    window = jnp.stack([f[0] for f in found])
    queries = jnp.stack([f[1] for f in found])
    partial = jnp.stack([f[2] for f in found])
    by = 1
    count = lax.axis_size("ctx")
    while 2 * by < count:
        window = compose(shift(window, by), window)
        by *= 2
    near = shift(window, 1)
    far = shift(window[:, LANES:], by + 1)
    state_in = compose(far, near)
    normed = pl.pallas_call(
        finish_kernel,
        out_shape=jax.ShapeDtypeStruct((tok_rows, heads_here * LANES), BF16),
        name="finish",
    )(state_in, queries, partial)
    group_count = lax.axis_size("head")
    rows_each = tok_rows // group_count
    stacked = normed.reshape(group_count, rows_each, heads_here * LANES)
    taken = lax.all_to_all(stacked, "head", split_axis=0, concat_axis=0, tiled=True)
    flipped = lax.all_gather(w_out.T, ("head", "ctx"), axis=0, tiled=True)
    flipped = flipped.reshape(group_count, w_out.shape[1] * count, w_out.shape[0])
    mixed = jnp.einsum("hrk,hdk->rd", taken, flipped, preferred_element_type=F32)
    return mixed.astype(BF16)


def solution(mesh):
    placed = (
        P("ctx", None),
        P("ctx", "head"),
        P("ctx", "head"),
        P("head", None),
        P("head"),
        P("head", "ctx"),
    )
    return jax.shard_map(
        shards, mesh=mesh, in_specs=placed, out_specs=P(("ctx", "head"), None), check_vma=False
    )
```

time: 748 us -> 238 us (0.32)
  the two profiles are of different devices: /device:TPU:128 before, /device:TPU:1 now
where the time goes in v1:
time: 238 us; the launch traced here: 237 us
  waiting for transfers between devices  109 us (46%)
  Pallas kernels  36 us (15%)
  starting transfers between devices  31.9 us (13%)
  blocking collectives  19 us (8%)
  between operations  13.5 us (6%)
  matrix products  12.4 us (5%)
  local copies, waits for them, and re-layouts  10.2 us (4%)
  other arithmetic  5.32 us (2%)
    all_gather x1, waiting for transfers between devices, shards(): weights = lax.all_gather(joined, 'ctx', axis=0, tiled=True)  86.4 us
    ppermute x6, starting transfers between devices, shift(): return lax.ppermute(array, 'ctx', [(i, i + by) for i in range(count - by)])  31.9 us
    pallas_call x2, Pallas kernels, local_pass(): pl.pallas_call(functools.partial(local_kernel, head), out_shape=(jax.Shap...  23.5 us
    all_to_all x1, blocking collectives, shards(): lax.all_to_all(stacked, 'head', split_axis=0, concat_axis=0, tiled=True)  19 us
    ppermute x6, waiting for transfers between devices, shift(): return lax.ppermute(array, 'ctx', [(i, i + by) for i in range(count - by)])  14.6 us
    pallas_call x5, Pallas kernels, compose(): pl.pallas_call(compose_kernel, out_shape=jax.ShapeDtypeStruct(before.shap...  9.88 us
    all_gather x1, waiting for transfers between devices, shards(): flipped = lax.all_gather(w_out.T, ('head', 'ctx'), axis=0, tiled=True)  7.27 us
    dot_general x1, matrix products, shards(): jnp.einsum('hrk,hdk->rd', taken, flipped, preferred_element_type=F32)  6.71 us
  transfers between devices with their start and end apart: 8, of which 7 were waited for; matrix products, arithmetic and copies ran while one was open for 6% of the time, Pallas kernels for 15%

profile of v1, /device:TPU:1, one launch (start us, length us, event | category | flops | bytes accessed | tf_op | source)
XLA Modules:
  0.0 237.4 jit_solution(13705181664478288283)
XLA Ops:
  6.5 0.0 copy-start
  6.5 0.0 all-gather.3.cloned.1.call-start
  6.5 0.9 copy.11
  7.5 1.6 fusion.2
  9.1 0.0 all-gather.3.cloned.1.call-update
  9.1 0.0 all-gather.5.cloned.1.call-start
  9.2 0.7 all-gather.5.cloned.1.call-update
  9.9 0.7 copy.12
  10.6 0.1 pad.18.clone
  10.7 0.1 reshape.13
  10.8 0.7 pad.17
  11.4 0.1 reshape.12
  11.5 0.6 select_maximum_fusion.row_ref
  12.1 86.4 %all-gather.3.cloned.1.call-done = bf16[2048,1408]{1,0:T(8,128)(2,1)} async-done(((bf16[64,1408]{1,0:T(8,128)(2,1)}), bf16[2048,1408]{1,0:T(8,128)(2,1)}) %all-gather.3.cloned.1.call-update) | async-done | bytes 5767184 | tf_op jit(solution)/shard_map/all_gather | solution.py:215
  98.5 0.0 copy-done
  98.5 5.7 %convolution_bitcast_fusion = f32[512,1408]{1,0:T(8,128)S(1)} fusion(bf16[512,2048]{1,0:T(8,128)(2,1)S(1)} %copy-done, bf16[2048,1408]{1,0:T(8,128)(2,1)} %all-gather.3.cloned.1.call-done), kind=kOutput, calls=%fused_computation | convolution fusion | flops 2952790016 | bytes 10747904 | tf_op jit(solution)/shard_map/dot_general | solution.py:216
  104.3 0.7 slice.17.gate_ref
  105.0 1.8 fusion.3
  106.7 11.6 %local0.1 = (f32[256,128]{1,0:T(8,128)}, f32[512,128]{1,0:T(8,128)}, f32[512,128]{1,0:T(8,128)}) custom-call(f32[512,640]{1,0:T(8,128)} %get-tuple-element.17.proj_ref, f32[512,128]{1,0:T(8,128)} %slice.17.gate_ref, f32[8,128]{1,0:T(8,128)} %select_maximum_fusion.row_ref), custom_call_target="tpu_custom_call" | custom-call | tf_op jit(solution)/shard_map/local0/pallas_call | solution.py:169
  118.4 0.0 copy-start.7
  118.4 0.0 copy-start.8
  118.4 11.9 %local1.1 = (f32[256,128]{1,0:T(8,128)}, f32[512,128]{1,0:T(8,128)}, f32[512,128]{1,0:T(8,128)}) custom-call(f32[512,640]{1,0:T(8,128)} %get-tuple-element.18.proj_ref, f32[512,128]{1,0:T(8,128)} %slice.17.gate_ref, f32[8,128]{1,0:T(8,128)} %select_maximum_fusion.row_ref), custom_call_target="tpu_custom_call" | custom-call | tf_op jit(solution)/shard_map/local1/pallas_call | solution.py:169
  130.3 0.0 copy-start.9
  130.3 1.0 pad_maximum_fusion.2.now_ref
  131.3 0.0 copy-start.1
  131.3 1.9 collective-permute-start
  133.2 3.3 %collective-permute-done.before_ref = f32[2,256,128]{2,1,0:T(8,128)S(1)} collective-permute-done((f32[2,256,128]{2,1,0:T(8,128)S(1)}, f32[2,256,128]{2,1,0:T(8,128)S(1)}, u32[]{:S(2)}, u32[]{:S(2)}) %collective-permute-start) | collective-permute-done | bytes 262176 | tf_op jit(solution)/shard_map/ppermute | solution.py:38
  136.5 0.0 copy-done.1
  136.5 0.0 copy-start.2
  136.5 0.7 copy-done.2
  137.2 2.0 compose.5.now_ref
  139.2 5.4 %collective-permute-start.1 = (f32[2,256,128]{2,1,0:T(8,128)}, f32[2,256,128]{2,1,0:T(8,128)S(1)}, u32[]{:S(2)}, u32[]{:S(2)}) collective-permute-start(f32[2,256,128]{2,1,0:T(8,128)} %compose.5.now_ref), channel_id=1, source_target_pairs={{0,16},{8,24},{16,32},{24,40},{32,48},{40,56},{48,64},{56,72},{64,... | collective-permute-start | bytes 786440 | tf_op jit(solution)/shard_map/ppermute | solution.py:38
  144.7 3.6 %collective-permute-done.1.before_ref = f32[2,256,128]{2,1,0:T(8,128)S(1)} collective-permute-done((f32[2,256,128]{2,1,0:T(8,128)}, f32[2,256,128]{2,1,0:T(8,128)S(1)}, u32[]{:S(2)}, u32[]{:S(2)}) %collective-permute-start.1) | collective-permute-done | bytes 262176 | tf_op jit(solution)/shard_map/ppermute | solution.py:38
  148.3 0.0 copy-start.3
  148.3 0.7 copy-done.3
  149.0 2.0 compose.6.now_ref
  151.0 6.2 %collective-permute-start.2 = (f32[2,256,128]{2,1,0:T(8,128)}, f32[2,256,128]{2,1,0:T(8,128)S(1)}, u32[]{:S(2)}, u32[]{:S(2)}) collective-permute-start(f32[2,256,128]{2,1,0:T(8,128)} %compose.6.now_ref), channel_id=1, source_target_pairs={{0,32},{8,40},{16,48},{24,56},{32,64},{40,72},{48,80},{56,88},{64,... | collective-permute-start | bytes 786440 | tf_op jit(solution)/shard_map/ppermute | solution.py:38
  157.2 3.6 %collective-permute-done.2.before_ref = f32[2,256,128]{2,1,0:T(8,128)S(1)} collective-permute-done((f32[2,256,128]{2,1,0:T(8,128)}, f32[2,256,128]{2,1,0:T(8,128)S(1)}, u32[]{:S(2)}, u32[]{:S(2)}) %collective-permute-start.2) | collective-permute-done | bytes 262176 | tf_op jit(solution)/shard_map/ppermute | solution.py:38
  160.8 0.0 copy-start.4
  160.8 0.7 copy-done.4
  161.5 2.0 compose.7.now_ref
  163.5 6.3 %collective-permute-start.3 = (f32[2,256,128]{2,1,0:T(8,128)}, f32[2,256,128]{2,1,0:T(8,128)S(1)}, u32[]{:S(2)}, u32[]{:S(2)}) collective-permute-start(f32[2,256,128]{2,1,0:T(8,128)} %compose.7.now_ref), channel_id=1, source_target_pairs={{0,64},{8,72},{16,80},{24,88},{32,96},{40,104},{48,112},{56,120},{... | collective-permute-start | bytes 786440 | tf_op jit(solution)/shard_map/ppermute | solution.py:38
  169.7 4.0 %collective-permute-done.3.before_ref = f32[2,256,128]{2,1,0:T(8,128)S(1)} collective-permute-done((f32[2,256,128]{2,1,0:T(8,128)}, f32[2,256,128]{2,1,0:T(8,128)S(1)}, u32[]{:S(2)}, u32[]{:S(2)}) %collective-permute-start.3) | collective-permute-done | bytes 262176 | tf_op jit(solution)/shard_map/ppermute | solution.py:38
  173.8 0.0 copy-start.5
  173.8 0.7 copy-done.5
  174.5 2.0 compose.8
  176.5 1.3 collective-permute-start.5
  177.8 1.0 slice.19
  178.7 10.7 %collective-permute-start.4 = (f32[2,128,128]{2,1,0:T(8,128)S(1)}, f32[2,128,128]{2,1,0:T(8,128)S(1)}, u32[]{:S(2)}, u32[]{:S(2)}) collective-permute-start(f32[2,128,128]{2,1,0:T(8,128)S(1)} %slice.19), channel_id=1, source_target_pairs={{0,136},{8,144},{16,152},{24,160},{32,168},{40,176},{48,184},{56,1... | collective-permute-start | bytes 393224 | tf_op jit(solution)/shard_map/ppermute | solution.py:38
  189.4 0.0 copy-done.7
  189.4 0.0 copy-done.8
  189.5 0.0 copy-done.9
  189.5 2.1 pad_maximum_fusion
  191.6 0.1 collective-permute-done.4.before_ref
  191.7 0.0 copy-start.10
  191.7 0.0 collective-permute-done.5.now_ref
  191.7 0.6 copy-done.10
  192.3 0.0 copy-start.6
  192.3 0.7 copy-done.6
  193.0 1.9 compose.9.state_ref
  194.9 2.6 %finish.1 = bf16[512,256]{1,0:T(8,128)(2,1)} custom-call(f32[2,128,128]{2,1,0:T(8,128)} %compose.9.state_ref, f32[2,512,128]{2,1,0:T(8,128)} %get-tuple-element.19.query_ref, f32[2,512,128]{2,1,0:T(8,128)} %get-tuple-element.20.part_ref), custom_call_target="tpu_custom_call" | custom-call | tf_op jit(solution)/shard_map/finish/pallas_call | solution.py:237
  197.5 19.0 %all_to_all.5 = bf16[8,64,256]{2,1,0:T(8,128)(2,1)S(1)} all-to-all(bf16[8,64,256]{2,1,0:T(8,128)(2,1)} %bitcast.21), channel_id=1, replica_groups=mesh['ctx'=32,'head'=8] {'head'}, dimensions={0} | all-to-all | bytes 524288 | tf_op jit(solution)/shard_map/all_to_all | solution.py:245
  216.6 7.3 %all-gather.5.cloned.1.call-done = bf16[16384,256]{1,0:T(8,128)(2,1)} async-done(((bf16[64,256]{1,0:T(8,128)(2,1)}), bf16[16384,256]{1,0:T(8,128)(2,1)}) %all-gather.5.cloned.1.call-update) | async-done | bytes 8388624 | tf_op jit(solution)/shard_map/all_gather | solution.py:246
  223.9 6.7 %fusion = bf16[64,2048]{1,0:T(8,128)(2,1)} fusion(bf16[8,64,256]{2,1,0:T(8,128)(2,1)S(1)} %all_to_all.5, bf16[8,2048,256]{2,1,0:T(8,128)(2,1)} %bitcast.20), kind=kOutput, calls=%fused_computation.2 | convolution fusion | flops 537001984 | bytes 8912896 | tf_op jit(solution)/shard_map/hrk,hdk->rd/dot_general | solution.py:248
Async XLA Ops:
  6.5 92.0 %copy-start = (bf16[512,2048]{1,0:T(8,128)(2,1)S(1)}, bf16[512,2048]{1,0:T(8,128)(2,1)}, u32[]{:S(2)}) copy-start(bf16[512,2048]{1,0:T(8,128)(2,1)} %param.6) | copy-start | bytes 6291460
  6.5 92.0 %all-gather.3.cloned.1.call-start = ((), (), s32[]{:S(2)}) async-start(), calls=%async_computation.1 | async-start | bytes 5947392 | tf_op jit(solution)/shard_map/all_gather | solution.py:215
  9.1 214.8 %all-gather.5.cloned.1.call-start = ((), (), s32[]{:S(2)}) async-start(), calls=%async_computation.2 | async-start | bytes 8421376 | tf_op jit(solution)/shard_map/all_gather | solution.py:246
  118.4 71.1 %copy-start.7 = (f32[512,128]{1,0:T(8,128)S(1)}, f32[512,128]{1,0:T(8,128)}, u32[]{:S(2)}) copy-start(f32[512,128]{1,0:T(8,128)} %get-tuple-element.13) | copy-start | bytes 786436
  118.4 71.1 %copy-start.8 = (f32[512,128]{1,0:T(8,128)S(1)}, f32[512,128]{1,0:T(8,128)}, u32[]{:S(2)}) copy-start(f32[512,128]{1,0:T(8,128)} %get-tuple-element.15) | copy-start | bytes 786436
  130.3 59.2 %copy-start.9 = (f32[512,128]{1,0:T(8,128)S(1)}, f32[512,128]{1,0:T(8,128)}, u32[]{:S(2)}) copy-start(f32[512,128]{1,0:T(8,128)} %get-tuple-element.14) | copy-start | bytes 786436
  131.3 5.2 %copy-start.1 = (f32[2,256,128]{2,1,0:T(8,128)}, f32[2,256,128]{2,1,0:T(8,128)S(1)}, u32[]{:S(2)}) copy-start(f32[2,256,128]{2,1,0:T(8,128)S(1)} %pad_maximum_fusion.2.now_ref) | copy-start | bytes 786436
  131.3 5.2 %collective-permute-start = (f32[2,256,128]{2,1,0:T(8,128)S(1)}, f32[2,256,128]{2,1,0:T(8,128)S(1)}, u32[]{:S(2)}, u32[]{:S(2)}) collective-permute-start(f32[2,256,128]{2,1,0:T(8,128)S(1)} %pad_maximum_fusion.2.now_ref), channel_id=1, source_target_pairs={{0,8},{8,16},{16,24},{24,32},{32,40},{40,48},{48,56},{56,64},{64,7... | collective-permute-start | bytes 786440 | tf_op jit(solution)/shard_map/ppermute | solution.py:38
  136.5 0.7 copy-start.2
  139.2 9.1 %collective-permute-start.1 = (f32[2,256,128]{2,1,0:T(8,128)}, f32[2,256,128]{2,1,0:T(8,128)S(1)}, u32[]{:S(2)}, u32[]{:S(2)}) collective-permute-start(f32[2,256,128]{2,1,0:T(8,128)} %compose.5.now_ref), channel_id=1, source_target_pairs={{0,16},{8,24},{16,32},{24,40},{32,48},{40,56},{48,64},{56,72},{64,... | collective-permute-start | bytes 786440 | tf_op jit(solution)/shard_map/ppermute | solution.py:38
  148.3 0.7 copy-start.3
  151.0 9.8 %collective-permute-start.2 = (f32[2,256,128]{2,1,0:T(8,128)}, f32[2,256,128]{2,1,0:T(8,128)S(1)}, u32[]{:S(2)}, u32[]{:S(2)}) collective-permute-start(f32[2,256,128]{2,1,0:T(8,128)} %compose.6.now_ref), channel_id=1, source_target_pairs={{0,32},{8,40},{16,48},{24,56},{32,64},{40,72},{48,80},{56,88},{64,... | collective-permute-start | bytes 786440 | tf_op jit(solution)/shard_map/ppermute | solution.py:38
  160.8 0.7 copy-start.4
  163.5 10.3 %collective-permute-start.3 = (f32[2,256,128]{2,1,0:T(8,128)}, f32[2,256,128]{2,1,0:T(8,128)S(1)}, u32[]{:S(2)}, u32[]{:S(2)}) collective-permute-start(f32[2,256,128]{2,1,0:T(8,128)} %compose.7.now_ref), channel_id=1, source_target_pairs={{0,64},{8,72},{16,80},{24,88},{32,96},{40,104},{48,112},{56,120},{... | collective-permute-start | bytes 786440 | tf_op jit(solution)/shard_map/ppermute | solution.py:38
  173.8 0.7 copy-start.5
  176.5 15.2 %collective-permute-start.5 = (f32[2,256,128]{2,1,0:T(8,128)}, f32[2,256,128]{2,1,0:T(8,128)S(1)}, u32[]{:S(2)}, u32[]{:S(2)}) collective-permute-start(f32[2,256,128]{2,1,0:T(8,128)} %compose.8), channel_id=1, source_target_pairs={{0,8},{8,16},{16,24},{24,32},{32,40},{40,48},{48,56},{56,64},{64,7... | collective-permute-start | bytes 786440 | tf_op jit(solution)/shard_map/ppermute | solution.py:38
  178.7 12.9 %collective-permute-start.4 = (f32[2,128,128]{2,1,0:T(8,128)S(1)}, f32[2,128,128]{2,1,0:T(8,128)S(1)}, u32[]{:S(2)}, u32[]{:S(2)}) collective-permute-start(f32[2,128,128]{2,1,0:T(8,128)S(1)} %slice.19), channel_id=1, source_target_pairs={{0,136},{8,144},{16,152},{24,160},{32,168},{40,176},{48,184},{56,1... | collective-permute-start | bytes 393224 | tf_op jit(solution)/shard_map/ppermute | solution.py:38
  191.7 0.7 copy-start.10
  192.3 0.7 copy-start.6
Sparse Core Ops, SparseCore 0:
  9.9 88.5 all-gather.2
  102.4 121.4 all-gather.4

commit v2 on v1

--- a/solution.py
+++ b/solution.py
@@ -1,10 +1,9 @@
-import functools
-
 import jax
 import jax.numpy as jnp
 from jax import lax
 from jax.experimental import pallas as pl
 from jax.experimental.pallas import tpu as pltpu
+from jax.sharding import Mesh
 from jax.sharding import PartitionSpec as P
 
 F32 = jnp.float32
@@ -33,32 +32,47 @@
     )
 
 
+Y_SIZE = 4
+CTX = ("z", "m", "p")
+
+
+def permute(array, move):
+    count = lax.axis_size(CTX)
+    z_size = count // Y_SIZE
+    pairs = []
+    for z in range(z_size):
+        for y in range(Y_SIZE):
+            to_z, to_y = move(z, y)
+            pairs.append((z * Y_SIZE + y, (to_z % z_size) * Y_SIZE + to_y))
+    return lax.ppermute(array, CTX, pairs)
+
+
+def permute_heads(array, move):
+    count = lax.axis_size("head")
+    return lax.ppermute(array, "head", [(i, move(i) % count) for i in range(count)])
+
+
 def shift(array, by):
-    count = lax.axis_size("ctx")
-    return lax.ppermute(array, "ctx", [(i, i + by) for i in range(count - by)])
-
-
-def around(array, y_size, dz, dy):
-    count = lax.axis_size("ctx")
-    z_size = count // y_size
-    pairs = [
-        (z * y_size + y, ((z + dz) % z_size) * y_size + (y + dy) % y_size)
-        for z in range(z_size)
-        for y in range(y_size)
-    ]
-    return lax.ppermute(array, "ctx", pairs)
+    nodes = lax.axis_size(CTX) // 2
+
+    def place(node, half):
+        return node // 2 * Y_SIZE + ((0, 3), (1, 2))[half][node % 2]
+
+    pairs = [(place(n, s), place(n + by, s)) for s in range(2) for n in range(nodes - by)]
+    return lax.ppermute(array, CTX, pairs)
 
 
 def unit(rows):
     return rows / jnp.sqrt(jnp.sum(rows * rows, axis=-1, keepdims=True) + 1e-06)
 
 
-def local_kernel(head, proj_ref, gate_ref, row_ref, state_ref, query_ref, out_ref):
+def local_kernel(swap_ref, proj_ref, row_ref, state_ref, query_ref, out_ref, held_ref):
+    del swap_ref
     tokens = proj_ref.shape[0]
     width = LANES
     blocks = tokens // BLOCK
     span = 2 * BLOCK
-    gates = gate_ref[...]
+    gates = proj_ref[:, 5 * width :]
     bias = row_ref[0:1, :]
     rate = row_ref[1:2, :]
     betas = 2.0 / (1.0 + jnp.exp(-(gates + bias)))
@@ -67,7 +81,7 @@
     row64 = lax.broadcasted_iota(jnp.int32, (BLOCK, BLOCK), 0)
     col64 = lax.broadcasted_iota(jnp.int32, (BLOCK, BLOCK), 1)
     lower = jnp.where(row64 >= col64, 1.0, 0.0).astype(F32)
-    base = 3 * head
+    base = 0
     row_i = lax.broadcasted_iota(jnp.int32, (span, span), 0)
     col_i = lax.broadcasted_iota(jnp.int32, (span, span), 1)
     row_t, row_r = row_i % BLOCK, row_i // BLOCK
@@ -150,7 +164,13 @@
         part["query"] = part["query"] - seen[:, :width]
         part["seen"] = seen[:, width:]
     zero = jnp.zeros((width, width), F32)
-    state = jnp.concatenate([eye, zero], axis=0)
+
+    @pl.when(pl.program_id(0) == 0)
+    def _():
+        held_ref[:width, :] = eye
+        held_ref[width:, :] = zero
+
+    state = held_ref[...]
     for n, part in enumerate(parts):
         rows = slice(n * BLOCK, (n + 1) * BLOCK)
         state_s = split(state)
@@ -160,41 +180,48 @@
         move = part["last"] * eye - part["step"][:width]
         state = dot3(state_s, split(move), ROWS)
         state = state + jnp.concatenate([zero, part["step"][width:]], axis=0)
+    held_ref[...] = state
     state_ref[...] = state
 
 
-def local_pass(proj, gates, rows, head):
-    tokens = proj.shape[0]
-    whole = lambda: (0, 0)
+def local_pass(swap, proj, rows):
+    tokens = proj.shape[0] // 2
+    half = jax.ShapeDtypeStruct((proj.shape[0], LANES), F32)
+    in_order = pl.BlockSpec((tokens, LANES), lambda i, swap: (i, 0))
     return pl.pallas_call(
-        functools.partial(local_kernel, head),
-        out_shape=(
-            jax.ShapeDtypeStruct((2 * LANES, LANES), F32),
-            jax.ShapeDtypeStruct((tokens, LANES), F32),
-            jax.ShapeDtypeStruct((tokens, LANES), F32),
+        local_kernel,
+        grid_spec=pltpu.PrefetchScalarGridSpec(
+            num_scalar_prefetch=1,
+            grid=(2,),
+            in_specs=[
+                pl.BlockSpec((tokens, proj.shape[1]), lambda i, swap: (i ^ swap[0], 0)),
+                pl.BlockSpec(rows.shape, lambda i, swap: (0, 0)),
+            ],
+            out_specs=[
+                pl.BlockSpec((2 * LANES, LANES), lambda i, swap: (0, 0)),
+                in_order,
+                in_order,
+            ],
+            scratch_shapes=[pltpu.VMEM((2 * LANES, LANES), F32)],
         ),
-        name=f"local{head}",
-    )(proj, gates, rows)
+        out_shape=(jax.ShapeDtypeStruct((2 * LANES, LANES), F32), half, half),
+        name="local",
+    )(swap, proj, rows)
 
 
 def finish_kernel(state_ref, query_ref, part_ref, out_ref):
-    heads = state_ref.shape[0]
-    for head in range(heads):
-        total = part_ref[head] + dot3(split(query_ref[head]), split(state_ref[head]), NT)
-        scale = jnp.sqrt(jnp.mean(total * total, axis=-1, keepdims=True) + 1e-06)
-        out_ref[:, head * LANES : (head + 1) * LANES] = (total / scale).astype(BF16)
+    total = part_ref[...] + dot3(split(query_ref[...]), split(state_ref[...]), NT)
+    scale = jnp.sqrt(jnp.mean(total * total, axis=-1, keepdims=True) + 1e-06)
+    out_ref[...] = (total / scale).astype(BF16)
 
 
 def compose_kernel(before_ref, now_ref, out_ref):
-    for head in range(now_ref.shape[0]):
-        now = now_ref[head]
-        moved = dot3(
-            split(before_ref[head].astype(F32)), split(now[:LANES].astype(F32)), ROWS
-        )
-        rows = before_ref.shape[1]
-        if rows > LANES:
-            out_ref[head, : rows - LANES] = moved[: rows - LANES]
-        out_ref[head, rows - LANES :] = moved[rows - LANES :] + now[LANES:].astype(F32)
+    rows = before_ref.shape[0]
+    now = now_ref[...]
+    moved = dot3(split(before_ref[...]), split(now[:LANES]), ROWS)
+    if rows > LANES:
+        out_ref[: rows - LANES] = moved[: rows - LANES]
+    out_ref[rows - LANES :] = moved[rows - LANES :] + now[LANES:]
 
 
 def compose(before, now):
@@ -205,59 +232,116 @@
     )(before, now)
 
 
+def at(buffer, block, index):
+    return lax.dynamic_update_slice_in_dim(buffer, block[None], index, axis=0)
+
+
 def shards(tokens, w_proj, w_small, beta_bias, decay_rate, w_out):
-    tok_rows = tokens.shape[0]
-    heads_here = beta_bias.shape[0]
-    mirrors = beta_bias.shape[1]
-    each = w_proj.shape[1] // heads_here
-    small = jnp.pad(w_small, ((0, 0), (0, LANES - w_small.shape[1])))
-    joined = jnp.concatenate([w_proj, small], axis=1)
-    weights = lax.all_gather(joined, "ctx", axis=0, tiled=True)
-    projected = jnp.dot(tokens, weights, preferred_element_type=F32)
-    gates = projected[:, heads_here * each :]
-    bias = jnp.pad(beta_bias, ((0, 0), (0, 1))).reshape(1, -1)
-    rate = jnp.pad(decay_rate[:, None], ((0, 0), (mirrors, 0))).reshape(1, -1)
-    rows = jnp.concatenate([bias, rate], axis=0)
-    rows = jnp.pad(rows, ((0, 6), (0, LANES - rows.shape[1])))
-    found = [
-        local_pass(projected[:, head * each : (head + 1) * each], gates, rows, head)
-        for head in range(heads_here)
-    ]
-    window = jnp.stack([f[0] for f in found])
-    queries = jnp.stack([f[1] for f in found])
-    partial = jnp.stack([f[2] for f in found])
+    tok_rows, depth = tokens.shape
+    ctx = lax.axis_index(CTX)
+    count = lax.axis_size(CTX)
+    z_size = count // Y_SIZE
+    z, y = ctx // Y_SIZE, ctx % Y_SIZE
+    pair, place = y // 2, y % 2
+    second = (y + 1) // 2 % 2 == 1
+    group = lax.axis_index("head")
+    groups = lax.axis_size("head")
+    rows_each = tok_rows // groups
+    column, core = group // 2, group % 2
+    columns = groups // 2
+
+    flipped = lax.all_gather(w_out.T, ("head",) + CTX, axis=0, tiled=True)
+    flipped = flipped.reshape(groups, w_out.shape[1] * count, w_out.shape[0])
+
+    each = w_proj.shape[1] // 2
+    gates = w_small.shape[1] // 2
+    small = jnp.zeros((w_small.shape[0], LANES - gates), BF16)
+    first_half = jnp.concatenate([w_proj[:, :each], w_small[:, :gates], small], axis=1)
+    second_half = jnp.concatenate([w_proj[:, each:], w_small[:, gates:], small], axis=1)
+    own = jnp.where(second, second_half, first_half)
+    other = jnp.where(second, first_half, second_half)
+
+    across = permute(other, lambda z, y: (z, y ^ 1))
+    part = lax.dynamic_slice_in_dim(tokens, group * rows_each, rows_each, axis=0)
+    part = permute(part, lambda z, y: (z, y ^ 1))
+    duo = jnp.where(
+        place == 0,
+        jnp.concatenate([own, across], axis=0),
+        jnp.concatenate([across, own], axis=0),
+    )
+    mate = permute(duo, lambda z, y: (z, 3 - y))
+    quad = jnp.where(
+        pair == 0,
+        jnp.concatenate([duo, mate], axis=0),
+        jnp.concatenate([mate, duo], axis=0),
+    )
+    weights = jnp.zeros((z_size,) + quad.shape, BF16)
+    weights = at(weights, quad, z)
+    parts = jnp.zeros((columns,) + part.shape, BF16)
+    parts = at(parts, part, column)
+    up = down = quad
+    for step in range(1, z_size // 2):
+        up = permute(up, lambda z, y: (z + 1, y))
+        down = permute(down, lambda z, y: (z - 1, y))
+        weights = at(weights, up, (z - step) % z_size)
+        weights = at(weights, down, (z + step) % z_size)
+    up = permute(up, lambda z, y: (z + 1, y))
+    weights = at(weights, up, (z - z_size // 2) % z_size)
+    for step in range(1, columns):
+        moved = permute_heads(part, lambda i, step=step: i + 2 * step)
+        parts = at(parts, moved, (column - step) % columns)
+    theirs = permute_heads(parts, lambda i: i ^ 1)
+    even = jnp.where(core == 0, parts, theirs)
+    odd = jnp.where(core == 0, theirs, parts)
+    partner = jnp.stack([even, odd], axis=1).reshape(tok_rows, depth)
+    both = jnp.concatenate([tokens, partner], axis=0)
+    weights = weights.reshape(depth, quad.shape[1])
+    projected = jnp.dot(both, weights, preferred_element_type=F32)
+
+    bias = jnp.where(second, beta_bias[1], beta_bias[0])
+    rate = jnp.where(second, decay_rate[1:], decay_rate[:1])
+    rows = jnp.stack(
+        [
+            jnp.pad(bias, (0, LANES - bias.shape[0])),
+            jnp.pad(rate, (bias.shape[0], LANES - bias.shape[0] - 1)),
+        ]
+    )
+    rows = jnp.pad(rows, ((0, 6), (0, 0)))
+    window, queries, partial = local_pass(place.reshape(1), projected, rows)
     by = 1
-    count = lax.axis_size("ctx")
-    while 2 * by < count:
+    while 4 * by < count:
         window = compose(shift(window, by), window)
         by *= 2
     near = shift(window, 1)
-    far = shift(window[:, LANES:], by + 1)
+    far = shift(window[LANES:], by + 1)
     state_in = compose(far, near)
     normed = pl.pallas_call(
         finish_kernel,
-        out_shape=jax.ShapeDtypeStruct((tok_rows, heads_here * LANES), BF16),
+        out_shape=jax.ShapeDtypeStruct((2 * tok_rows, LANES), BF16),
         name="finish",
     )(state_in, queries, partial)
-    group_count = lax.axis_size("head")
-    rows_each = tok_rows // group_count
-    stacked = normed.reshape(group_count, rows_each, heads_here * LANES)
-    taken = lax.all_to_all(stacked, "head", split_axis=0, concat_axis=0, tiled=True)
-    flipped = lax.all_gather(w_out.T, ("head", "ctx"), axis=0, tiled=True)
-    flipped = flipped.reshape(group_count, w_out.shape[1] * count, w_out.shape[0])
+    stacked = normed.reshape(2 * groups, rows_each, LANES)
+    taken = lax.all_to_all(stacked, ("p", "head"), split_axis=0, concat_axis=0, tiled=True)
+    taken = taken.reshape(2, groups, rows_each, LANES)
+    taken = jnp.where(pair == 0, taken, taken[::-1])
+    taken = jnp.concatenate([taken[0], taken[1]], axis=2)
     mixed = jnp.einsum("hrk,hdk->rd", taken, flipped, preferred_element_type=F32)
     return mixed.astype(BF16)
 
 
 def solution(mesh):
+    sizes = dict(mesh.shape)
+    finer = Mesh(
+        mesh.devices.reshape(sizes["ctx"] // Y_SIZE, 2, 2, sizes["head"]), CTX + ("head",)
+    )
     placed = (
-        P("ctx", None),
-        P("ctx", "head"),
-        P("ctx", "head"),
+        P(CTX, None),
+        P(CTX, "head"),
+        P(CTX, "head"),
         P("head", None),
         P("head"),
-        P("head", "ctx"),
+        P("head", CTX),
     )
     return jax.shard_map(
-        shards, mesh=mesh, in_specs=placed, out_specs=P(("ctx", "head"), None), check_vma=False
-    )
+        shards, mesh=finer, in_specs=placed, out_specs=P(CTX + ("head",), None), check_vma=False
+    )

time: 238 us -> 186 us (0.78)
  waiting for transfers between devices: 109 us -> 40.7 us
  starting transfers between devices: 31.9 us -> 55.9 us
  Pallas kernels: 36 us -> 31.4 us
  other arithmetic: 5.32 us -> 2.02 us
    all_gather x2 -> x1, waiting for transfers between devices: 93.7 us -> 0.02 us  [shards(): flipped = lax.all_gather(w_out.T, ('head',) + CTX, axis=0, tiled=True)]
    ppermute x6 -> x19, waiting for transfers between devices: 14.6 us -> 39.9 us  [the longest x10 26.5 us: permute(): return lax.ppermute(array, CTX, pairs)]
    ppermute x6 -> x19, starting transfers between devices: 31.9 us -> 55.9 us  [the longest x5 29 us: shift(): return lax.ppermute(array, CTX, pairs)]
    pallas_call x5 -> x4, Pallas kernels: 9.88 us -> 7.24 us  [compose(): pl.pallas_call(compose_kernel, out_shape=jax.ShapeDtypeStruct(before.shap...]
    unnamed x24 -> x12, local copies, waits for them, and re-layouts: 5.86 us -> 3.25 us
    pallas_call x3 -> x2, Pallas kernels: 26.1 us -> 24.2 us  [the longest x1 21.7 us: local_pass(): pl.pallas_call(local_kernel, grid_spec=pltpu.PrefetchScalarGridSpec(num_s...]
  transfers between devices with their start and end apart: 8 -> 20, of which waited for: 7 -> 11; matrix products, arithmetic and copies ran while one was open for 6% -> 7% of each run, Pallas kernels for 15% -> 17%
where the time goes in v2:
time: 186 us; the launch traced here: 185 us
  starting transfers between devices  55.9 us (30%)
  waiting for transfers between devices  40.7 us (22%)
  Pallas kernels  31.4 us (17%)
  blocking collectives  19.5 us (10%)
  between operations  14.9 us (8%)
  matrix products  11.8 us (6%)
  local copies, waits for them, and re-layouts  9.14 us (5%)
  other arithmetic  2.02 us (1%)
    ppermute x5, starting transfers between devices, shift(): return lax.ppermute(array, CTX, pairs)  29 us
    ppermute x10, waiting for transfers between devices, permute(): return lax.ppermute(array, CTX, pairs)  26.5 us
    pallas_call x1, Pallas kernels, local_pass(): pl.pallas_call(local_kernel, grid_spec=pltpu.PrefetchScalarGridSpec(num_s...  21.7 us
    all_to_all x1, blocking collectives, shards(): lax.all_to_all(stacked, ('p', 'head'), split_axis=0, concat_axis=0, tiled...  19.5 us
    ppermute x10, starting transfers between devices, permute(): return lax.ppermute(array, CTX, pairs)  19.4 us
    ppermute x5, waiting for transfers between devices, shift(): return lax.ppermute(array, CTX, pairs)  10.4 us
    ppermute x4, starting transfers between devices, permute_heads(): lax.ppermute(array, 'head', [(i, move(i) % count) for i in range(count)])  7.47 us
    pallas_call x4, Pallas kernels, compose(): pl.pallas_call(compose_kernel, out_shape=jax.ShapeDtypeStruct(before.shap...  7.24 us
  transfers between devices with their start and end apart: 20, of which 11 were waited for; matrix products, arithmetic and copies ran while one was open for 7% of the time, Pallas kernels for 17%

profile of v2, /device:TPU:1, one launch (start us, length us, event | category | flops | bytes accessed | tf_op | source)
XLA Modules:
  0.0 185.3 jit_solution(14649272550745939805)
XLA Ops:
  6.5 0.7 all-gather.2.cloned.1.call-update
  7.3 1.0 constant_dynamic-slice_fusion
  8.2 2.2 %collective-permute-start = (bf16[64,2048]{1,0:T(8,128)(2,1)S(1)}, bf16[64,2048]{1,0:T(8,128)(2,1)S(1)}, u32[]{:S(2)}, u32[]{:S(2)}) collective-permute-start(bf16[64,2048]{1,0:T(8,128)(2,1)S(1)} %constant_dynamic-slice_fusion), channel_id=1, source_target_pairs={{0,8},{8,0},{16,24},{24,16},{32,40},{40,32},{48,56},{56,48},{64,72... | collective-permute-start | bytes 786440 | tf_op jit(solution)/shard_map/ppermute | solution.py:47
  10.4 0.8 fusion.13
  11.2 0.1 copy.8
  11.3 0.1 copy.9
  11.4 0.1 pad.36.clone
  11.5 0.9 fusion.12
  12.5 0.1 broadcast_select_fusion.1
  12.5 0.2 collective-permute-start.5
  12.7 1.3 fusion.14
  15.3 0.1 pad_bitcast_fusion
  15.4 0.8 fusion.9
  16.1 0.6 select_maximum_fusion.row_ref
  16.7 0.7 collective-permute-done.5
  17.5 3.8 %collective-permute-start.6 = (bf16[128,768]{1,0:T(8,128)(2,1)S(1)}, bf16[128,768]{1,0:T(8,128)(2,1)S(1)}, u32[]{:S(2)}, u32[]{:S(2)}) collective-permute-start(bf16[128,768]{1,0:T(8,128)(2,1)S(1)} %maximum_select_fusion.2), channel_id=1, source_target_pairs={{0,24},{8,16},{16,8},{24,0},{32,56},{40,48},{48,40},{56,32},{64,88... | collective-permute-start | bytes 589832 | tf_op jit(solution)/shard_map/ppermute | solution.py:47
  21.3 1.2 collective-permute-start.1
  22.5 2.5 %collective-permute-start.2 = (bf16[64,2048]{1,0:T(8,128)(2,1)S(1)}, bf16[64,2048]{1,0:T(8,128)(2,1)S(1)}, u32[]{:S(2)}, u32[]{:S(2)}) collective-permute-start(bf16[64,2048]{1,0:T(8,128)(2,1)S(1)} %collective-permute-done), channel_id=1, source_target_pairs={{0,4},{1,5},{2,6},{3,7},{4,0},{5,1},{6,2},{7,3},{8,12},{9,13},{10,... | collective-permute-start | bytes 786440 | tf_op jit(solution)/shard_map/ppermute | solution.py:52
  25.0 1.2 collective-permute-start.3
  26.1 0.1 broadcast_in_dim.43
  26.3 0.1 maximum_select_fusion.1
  26.4 1.7 collective-permute-start.7
  28.1 4.0 %collective-permute-start.8 = (bf16[256,768]{1,0:T(8,128)(2,1)S(1)}, bf16[256,768]{1,0:T(8,128)(2,1)S(1)}, u32[]{:S(2)}, u32[]{:S(2)}) collective-permute-start(bf16[256,768]{1,0:T(8,128)(2,1)S(1)} %maximum_select_fusion.1), channel_id=1, source_target_pairs={{0,224},{8,232},{16,240},{24,248},{32,0},{40,8},{48,16},{56,24},{6... | collective-permute-start | bytes 1179656 | tf_op jit(solution)/shard_map/ppermute | solution.py:47
  32.1 0.2 broadcast_in_dim.48
  32.3 0.1 fusion.5
  32.5 2.9 %collective-permute-done.2 = bf16[64,2048]{1,0:T(8,128)(2,1)S(1)} collective-permute-done((bf16[64,2048]{1,0:T(8,128)(2,1)S(1)}, bf16[64,2048]{1,0:T(8,128)(2,1)S(1)}, u32[]{:S(2)}, u32[]{:S(2)}) %collective-permute-start.2) | collective-permute-done | bytes 262176 | tf_op jit(solution)/shard_map/ppermute | solution.py:52
  35.4 0.2 collective-permute-done.3
  35.5 2.7 %collective-permute-start.4 = (bf16[4,64,2048]{2,1,0:T(8,128)(2,1)S(1)}, bf16[4,64,2048]{2,1,0:T(8,128)(2,1)S(1)}, u32[]{:S(2)}, u32[]{:S(2)}) collective-permute-start(bf16[4,64,2048]{2,1,0:T(8,128)(2,1)S(1)} %bitcast_dynamic-update-slice_fusion.7), channel_id=1, source_target_pairs={{0,1},{1,0},{2,3},{3,2},{4,5},{5,4},{6,7},{7,6},{8,9},{9,8},{10,11... | collective-permute-start | bytes 3145736 | tf_op jit(solution)/shard_map/ppermute | solution.py:52
  38.2 0.9 collective-permute-done.7
  39.1 0.8 collective-permute-start.9
  39.9 4.0 %collective-permute-start.10 = (bf16[256,768]{1,0:T(8,128)(2,1)S(1)}, bf16[256,768]{1,0:T(8,128)(2,1)S(1)}, u32[]{:S(2)}, u32[]{:S(2)}) collective-permute-start(bf16[256,768]{1,0:T(8,128)(2,1)S(1)} %collective-permute-done.8), channel_id=1, source_target_pairs={{0,224},{8,232},{16,240},{24,248},{32,0},{40,8},{48,16},{56,24},{6... | collective-permute-start | bytes 1179656 | tf_op jit(solution)/shard_map/ppermute | solution.py:47
  44.0 8.3 %collective-permute-done.9 = bf16[256,768]{1,0:T(8,128)(2,1)S(1)} collective-permute-done((bf16[256,768]{1,0:T(8,128)(2,1)S(1)}, bf16[256,768]{1,0:T(8,128)(2,1)S(1)}, u32[]{:S(2)}, u32[]{:S(2)}) %collective-permute-start.9) | collective-permute-done | bytes 393248 | tf_op jit(solution)/shard_map/ppermute | solution.py:47
  52.3 2.7 %collective-permute-start.12 = (bf16[256,768]{1,0:T(8,128)(2,1)S(1)}, bf16[256,768]{1,0:T(8,128)(2,1)S(1)}, u32[]{:S(2)}, u32[]{:S(2)}) collective-permute-start(bf16[256,768]{1,0:T(8,128)(2,1)S(1)} %collective-permute-done.10), channel_id=1, source_target_pairs={{0,224},{8,232},{16,240},{24,248},{32,0},{40,8},{48,16},{56,24},{6... | collective-permute-start | bytes 1179656 | tf_op jit(solution)/shard_map/ppermute | solution.py:47
  55.0 7.2 %collective-permute-done.11 = bf16[256,768]{1,0:T(8,128)(2,1)S(1)} collective-permute-done((bf16[256,768]{1,0:T(8,128)(2,1)S(1)}, bf16[256,768]{1,0:T(8,128)(2,1)S(1)}, u32[]{:S(2)}, u32[]{:S(2)}) %collective-permute-start.11) | collective-permute-done | bytes 393248 | tf_op jit(solution)/shard_map/ppermute | solution.py:47
  62.3 0.1 select_bitcast_fusion.1
  62.5 0.0 copy-start.5
  62.5 0.2 pad_maximum_fusion
  62.7 9.4 %collective-permute-done.13 = bf16[256,768]{1,0:T(8,128)(2,1)S(1)} collective-permute-done((bf16[256,768]{1,0:T(8,128)(2,1)S(1)}, bf16[256,768]{1,0:T(8,128)(2,1)S(1)}, u32[]{:S(2)}, u32[]{:S(2)}) %collective-permute-start.13) | collective-permute-done | bytes 393248 | tf_op jit(solution)/shard_map/ppermute | solution.py:47
  72.1 5.1 %fusion.proj_ref = f32[1024,768]{1,0:T(8,128)} fusion(bf16[2048,768]{1,0:T(8,128)(2,1)S(1)} %bitcast.55, bf16[512,2048]{1,0:T(8,128)(2,1)S(1)} %bitcast.56, bf16[512,2048]{1,0:T(8,128)(2,1)S(1)} %copy-done.5), kind=kOutput, calls=%fused_computation | convolution fusion | flops 3229614080 | bytes 10485760 | tf_op jit(solution)/shard_map/dot_general | solution.py:299
  77.2 21.7 %local.1 = (f32[256,128]{1,0:T(8,128)}, f32[1024,128]{1,0:T(8,128)}, f32[1024,128]{1,0:T(8,128)}) custom-call(s32[1]{0:T(128)} %bitcast.swap_ref, f32[1024,768]{1,0:T(8,128)} %fusion.proj_ref, f32[8,128]{1,0:T(8,128)} %select_maximum_fusion.row_ref), custom_call_target="tpu_custom_call" | custom-call | tf_op jit(solution)/shard_map/local/pallas_call | solution.py:191
  98.9 1.3 collective-permute-start.14
  100.2 3.0 %collective-permute-done.14.before_ref = f32[256,128]{1,0:T(8,128)S(1)} collective-permute-done((f32[256,128]{1,0:T(8,128)}, f32[256,128]{1,0:T(8,128)S(1)}, u32[]{:S(2)}, u32[]{:S(2)}) %collective-permute-start.14) | collective-permute-done | bytes 131104 | tf_op jit(solution)/shard_map/ppermute | solution.py:62
  103.2 0.7 copy-done
  103.9 1.8 compose.4.now_ref
  105.7 4.8 %collective-permute-start.15 = (f32[256,128]{1,0:T(8,128)}, f32[256,128]{1,0:T(8,128)S(1)}, u32[]{:S(2)}, u32[]{:S(2)}) collective-permute-start(f32[256,128]{1,0:T(8,128)} %compose.4.now_ref), channel_id=1, source_target_pairs={{0,32},{24,56},{32,64},{56,88},{64,96},{88,120},{96,128},{120,152}... | collective-permute-start | bytes 393224 | tf_op jit(solution)/shard_map/ppermute | solution.py:62
  110.5 2.5 %collective-permute-done.15.before_ref = f32[256,128]{1,0:T(8,128)S(1)} collective-permute-done((f32[256,128]{1,0:T(8,128)}, f32[256,128]{1,0:T(8,128)S(1)}, u32[]{:S(2)}, u32[]{:S(2)}) %collective-permute-start.15) | collective-permute-done | bytes 131104 | tf_op jit(solution)/shard_map/ppermute | solution.py:62
  113.0 0.7 copy-done.1
  113.6 1.9 compose.5.now_ref
  115.5 6.3 %collective-permute-start.16 = (f32[256,128]{1,0:T(8,128)}, f32[256,128]{1,0:T(8,128)S(1)}, u32[]{:S(2)}, u32[]{:S(2)}) collective-permute-start(f32[256,128]{1,0:T(8,128)} %compose.5.now_ref), channel_id=1, source_target_pairs={{0,64},{24,88},{32,96},{56,120},{64,128},{88,152},{96,160},{120,18... | collective-permute-start | bytes 393224 | tf_op jit(solution)/shard_map/ppermute | solution.py:62
  121.8 3.6 %collective-permute-done.16.before_ref = f32[256,128]{1,0:T(8,128)S(1)} collective-permute-done((f32[256,128]{1,0:T(8,128)}, f32[256,128]{1,0:T(8,128)S(1)}, u32[]{:S(2)}, u32[]{:S(2)}) %collective-permute-start.16) | collective-permute-done | bytes 131104 | tf_op jit(solution)/shard_map/ppermute | solution.py:62
  125.4 0.7 copy-done.2
  126.1 1.8 compose.6
  127.9 4.4 %collective-permute-start.18 = (f32[256,128]{1,0:T(8,128)}, f32[256,128]{1,0:T(8,128)S(1)}, u32[]{:S(2)}, u32[]{:S(2)}) collective-permute-start(f32[256,128]{1,0:T(8,128)} %compose.6), channel_id=1, source_target_pairs={{0,24},{24,32},{32,56},{56,64},{64,88},{88,96},{96,120},{120,128},... | collective-permute-start | bytes 393224 | tf_op jit(solution)/shard_map/ppermute | solution.py:62
  132.3 0.9 slice.44
  133.1 12.2 %collective-permute-start.17 = (f32[128,128]{1,0:T(8,128)S(1)}, f32[128,128]{1,0:T(8,128)S(1)}, u32[]{:S(2)}, u32[]{:S(2)}) collective-permute-start(f32[128,128]{1,0:T(8,128)S(1)} %slice.44), channel_id=1, source_target_pairs={{0,152},{24,160},{32,184},{56,192},{64,216},{88,224},{96,248},{8,1... | collective-permute-start | bytes 196616 | tf_op jit(solution)/shard_map/ppermute | solution.py:62
  145.3 1.3 collective-permute-done.17.before_ref
  146.6 0.6 copy-done.4
  147.3 0.7 copy-done.3
  147.9 1.8 compose.7.state_ref
  149.7 2.5 %finish.1 = bf16[1024,128]{1,0:T(8,128)(2,1)} custom-call(f32[128,128]{1,0:T(8,128)} %compose.7.state_ref, f32[1024,128]{1,0:T(8,128)} %get-tuple-element.9.query_ref, f32[1024,128]{1,0:T(8,128)} %get-tuple-element.10.part_ref), custom_call_target="tpu_custom_call" | custom-call | tf_op jit(solution)/shard_map/finish/pallas_call | solution.py:318
  152.1 19.5 %all_to_all.5 = bf16[16,64,128]{2,1,0:T(8,128)(2,1)S(1)} all-to-all(bf16[16,64,128]{2,1,0:T(8,128)(2,1)} %bitcast.59), channel_id=1, replica_groups=mesh['z'=8,'m'=2,'p'=2,'head'=8] {'p','head'}, dimensions={0} | all-to-all | bytes 524288 | tf_op jit(solution)/shard_map/all_to_all | solution.py:324
  171.6 0.1 reverse_select_fusion
  171.7 0.0 all-gather.2.cloned.1.call-done
  171.7 6.7 %fusion.4 = bf16[64,2048]{1,0:T(8,128)(2,1)} fusion(bf16[8,2048,256]{2,1,0:T(8,128)(2,1)} %bitcast.54, bf16[8,64,128]{2,1,0:T(8,128)(2,1)S(1)} %get-tuple-element.14, bf16[8,64,128]{2,1,0:T(8,128)(2,1)S(1)} %get-tuple-element.13), kind=kOutput, calls=%fused_computation.5 | convolution fusion | flops 537526272 | bytes 8912896 | tf_op jit(solution)/shard_map/hrk,hdk->rd/dot_general | solution.py:328
  (32 shorter events, 0.4 us)
Async XLA Ops:
  6.5 165.2 %all-gather.2.cloned.1.call-start = ((), (), s32[]{:S(2)}) async-start(), calls=%async_computation.1 | async-start | bytes 8421376 | tf_op jit(solution)/shard_map/all_gather | solution.py:253
  8.2 13.1 %collective-permute-start = (bf16[64,2048]{1,0:T(8,128)(2,1)S(1)}, bf16[64,2048]{1,0:T(8,128)(2,1)S(1)}, u32[]{:S(2)}, u32[]{:S(2)}) collective-permute-start(bf16[64,2048]{1,0:T(8,128)(2,1)S(1)} %constant_dynamic-slice_fusion), channel_id=1, source_target_pairs={{0,8},{8,0},{16,24},{24,16},{32,40},{40,32},{48,56},{56,48},{64,72... | collective-permute-start | bytes 786440 | tf_op jit(solution)/shard_map/ppermute | solution.py:47
  12.5 4.9 %collective-permute-start.5 = (bf16[64,768]{1,0:T(8,128)(2,1)S(1)}, bf16[64,768]{1,0:T(8,128)(2,1)S(1)}, u32[]{:S(2)}, u32[]{:S(2)}) collective-permute-start(bf16[64,768]{1,0:T(8,128)(2,1)S(1)} %get-tuple-element.16), channel_id=1, source_target_pairs={{0,8},{8,0},{16,24},{24,16},{32,40},{40,32},{48,56},{56,48},{64,72... | collective-permute-start | bytes 294920 | tf_op jit(solution)/shard_map/ppermute | solution.py:47
  17.5 8.8 %collective-permute-start.6 = (bf16[128,768]{1,0:T(8,128)(2,1)S(1)}, bf16[128,768]{1,0:T(8,128)(2,1)S(1)}, u32[]{:S(2)}, u32[]{:S(2)}) collective-permute-start(bf16[128,768]{1,0:T(8,128)(2,1)S(1)} %maximum_select_fusion.2), channel_id=1, source_target_pairs={{0,24},{8,16},{16,8},{24,0},{32,56},{40,48},{48,40},{56,32},{64,88... | collective-permute-start | bytes 589832 | tf_op jit(solution)/shard_map/ppermute | solution.py:47
  21.3 11.1 %collective-permute-start.1 = (bf16[64,2048]{1,0:T(8,128)(2,1)S(1)}, bf16[64,2048]{1,0:T(8,128)(2,1)S(1)}, u32[]{:S(2)}, u32[]{:S(2)}) collective-permute-start(bf16[64,2048]{1,0:T(8,128)(2,1)S(1)} %collective-permute-done), channel_id=1, source_target_pairs={{0,2},{1,3},{2,4},{3,5},{4,6},{5,7},{6,0},{7,1},{8,10},{9,11},{10,... | collective-permute-start | bytes 786440 | tf_op jit(solution)/shard_map/ppermute | solution.py:52
  22.5 12.8 %collective-permute-start.2 = (bf16[64,2048]{1,0:T(8,128)(2,1)S(1)}, bf16[64,2048]{1,0:T(8,128)(2,1)S(1)}, u32[]{:S(2)}, u32[]{:S(2)}) collective-permute-start(bf16[64,2048]{1,0:T(8,128)(2,1)S(1)} %collective-permute-done), channel_id=1, source_target_pairs={{0,4},{1,5},{2,6},{3,7},{4,0},{5,1},{6,2},{7,3},{8,12},{9,13},{10,... | collective-permute-start | bytes 786440 | tf_op jit(solution)/shard_map/ppermute | solution.py:52
  25.0 10.5 %collective-permute-start.3 = (bf16[64,2048]{1,0:T(8,128)(2,1)S(1)}, bf16[64,2048]{1,0:T(8,128)(2,1)S(1)}, u32[]{:S(2)}, u32[]{:S(2)}) collective-permute-start(bf16[64,2048]{1,0:T(8,128)(2,1)S(1)} %collective-permute-done), channel_id=1, source_target_pairs={{0,6},{1,7},{2,0},{3,1},{4,2},{5,3},{6,4},{7,5},{8,14},{9,15},{10,... | collective-permute-start | bytes 786440 | tf_op jit(solution)/shard_map/ppermute | solution.py:52
  26.4 12.7 %collective-permute-start.7 = (bf16[256,768]{1,0:T(8,128)(2,1)S(1)}, bf16[256,768]{1,0:T(8,128)(2,1)S(1)}, u32[]{:S(2)}, u32[]{:S(2)}) collective-permute-start(bf16[256,768]{1,0:T(8,128)(2,1)S(1)} %maximum_select_fusion.1), channel_id=1, source_target_pairs={{0,32},{8,40},{16,48},{24,56},{32,64},{40,72},{48,80},{56,88},{64,... | collective-permute-start | bytes 1179656 | tf_op jit(solution)/shard_map/ppermute | solution.py:47
  28.1 11.8 %collective-permute-start.8 = (bf16[256,768]{1,0:T(8,128)(2,1)S(1)}, bf16[256,768]{1,0:T(8,128)(2,1)S(1)}, u32[]{:S(2)}, u32[]{:S(2)}) collective-permute-start(bf16[256,768]{1,0:T(8,128)(2,1)S(1)} %maximum_select_fusion.1), channel_id=1, source_target_pairs={{0,224},{8,232},{16,240},{24,248},{32,0},{40,8},{48,16},{56,24},{6... | collective-permute-start | bytes 1179656 | tf_op jit(solution)/shard_map/ppermute | solution.py:47
  35.5 26.8 %collective-permute-start.4 = (bf16[4,64,2048]{2,1,0:T(8,128)(2,1)S(1)}, bf16[4,64,2048]{2,1,0:T(8,128)(2,1)S(1)}, u32[]{:S(2)}, u32[]{:S(2)}) collective-permute-start(bf16[4,64,2048]{2,1,0:T(8,128)(2,1)S(1)} %bitcast_dynamic-update-slice_fusion.7), channel_id=1, source_target_pairs={{0,1},{1,0},{2,3},{3,2},{4,5},{5,4},{6,7},{7,6},{8,9},{9,8},{10,11... | collective-permute-start | bytes 3145736 | tf_op jit(solution)/shard_map/ppermute | solution.py:52
  39.1 13.2 %collective-permute-start.9 = (bf16[256,768]{1,0:T(8,128)(2,1)S(1)}, bf16[256,768]{1,0:T(8,128)(2,1)S(1)}, u32[]{:S(2)}, u32[]{:S(2)}) collective-permute-start(bf16[256,768]{1,0:T(8,128)(2,1)S(1)} %collective-permute-done.7), channel_id=1, source_target_pairs={{0,32},{8,40},{16,48},{24,56},{32,64},{40,72},{48,80},{56,88},{64,... | collective-permute-start | bytes 1179656 | tf_op jit(solution)/shard_map/ppermute | solution.py:47
  39.9 12.4 %collective-permute-start.10 = (bf16[256,768]{1,0:T(8,128)(2,1)S(1)}, bf16[256,768]{1,0:T(8,128)(2,1)S(1)}, u32[]{:S(2)}, u32[]{:S(2)}) collective-permute-start(bf16[256,768]{1,0:T(8,128)(2,1)S(1)} %collective-permute-done.8), channel_id=1, source_target_pairs={{0,224},{8,232},{16,240},{24,248},{32,0},{40,8},{48,16},{56,24},{6... | collective-permute-start | bytes 1179656 | tf_op jit(solution)/shard_map/ppermute | solution.py:47
  52.3 10.0 %collective-permute-start.11 = (bf16[256,768]{1,0:T(8,128)(2,1)S(1)}, bf16[256,768]{1,0:T(8,128)(2,1)S(1)}, u32[]{:S(2)}, u32[]{:S(2)}) collective-permute-start(bf16[256,768]{1,0:T(8,128)(2,1)S(1)} %collective-permute-done.9), channel_id=1, source_target_pairs={{0,32},{8,40},{16,48},{24,56},{32,64},{40,72},{48,80},{56,88},{64,... | collective-permute-start | bytes 1179656 | tf_op jit(solution)/shard_map/ppermute | solution.py:47
  52.3 10.0 %collective-permute-start.12 = (bf16[256,768]{1,0:T(8,128)(2,1)S(1)}, bf16[256,768]{1,0:T(8,128)(2,1)S(1)}, u32[]{:S(2)}, u32[]{:S(2)}) collective-permute-start(bf16[256,768]{1,0:T(8,128)(2,1)S(1)} %collective-permute-done.10), channel_id=1, source_target_pairs={{0,224},{8,232},{16,240},{24,248},{32,0},{40,8},{48,16},{56,24},{6... | collective-permute-start | bytes 1179656 | tf_op jit(solution)/shard_map/ppermute | solution.py:47
  62.2 9.8 %collective-permute-start.13 = (bf16[256,768]{1,0:T(8,128)(2,1)S(1)}, bf16[256,768]{1,0:T(8,128)(2,1)S(1)}, u32[]{:S(2)}, u32[]{:S(2)}) collective-permute-start(bf16[256,768]{1,0:T(8,128)(2,1)S(1)} %collective-permute-done.11), channel_id=1, source_target_pairs={{0,32},{8,40},{16,48},{24,56},{32,64},{40,72},{48,80},{56,88},{64,... | collective-permute-start | bytes 1179656 | tf_op jit(solution)/shard_map/ppermute | solution.py:47
  62.5 9.6 %copy-start.5 = (bf16[512,2048]{1,0:T(8,128)(2,1)S(1)}, bf16[512,2048]{1,0:T(8,128)(2,1)}, u32[]{:S(2)}) copy-start(bf16[512,2048]{1,0:T(8,128)(2,1)} %param.6) | copy-start | bytes 6291460
  98.9 4.3 %collective-permute-start.14 = (f32[256,128]{1,0:T(8,128)}, f32[256,128]{1,0:T(8,128)S(1)}, u32[]{:S(2)}, u32[]{:S(2)}) collective-permute-start(f32[256,128]{1,0:T(8,128)} %get-tuple-element.8.now_ref), channel_id=1, source_target_pairs={{0,24},{24,32},{32,56},{56,64},{64,88},{88,96},{96,120},{120,128},... | collective-permute-start | bytes 393224 | tf_op jit(solution)/shard_map/ppermute | solution.py:62
  103.2 0.7 copy-start
  105.7 7.3 %collective-permute-start.15 = (f32[256,128]{1,0:T(8,128)}, f32[256,128]{1,0:T(8,128)S(1)}, u32[]{:S(2)}, u32[]{:S(2)}) collective-permute-start(f32[256,128]{1,0:T(8,128)} %compose.4.now_ref), channel_id=1, source_target_pairs={{0,32},{24,56},{32,64},{56,88},{64,96},{88,120},{96,128},{120,152}... | collective-permute-start | bytes 393224 | tf_op jit(solution)/shard_map/ppermute | solution.py:62
  113.0 0.7 copy-start.1
  115.5 9.9 %collective-permute-start.16 = (f32[256,128]{1,0:T(8,128)}, f32[256,128]{1,0:T(8,128)S(1)}, u32[]{:S(2)}, u32[]{:S(2)}) collective-permute-start(f32[256,128]{1,0:T(8,128)} %compose.5.now_ref), channel_id=1, source_target_pairs={{0,64},{24,88},{32,96},{56,120},{64,128},{88,152},{96,160},{120,18... | collective-permute-start | bytes 393224 | tf_op jit(solution)/shard_map/ppermute | solution.py:62
  125.4 0.7 copy-start.2
  127.9 18.7 %collective-permute-start.18 = (f32[256,128]{1,0:T(8,128)}, f32[256,128]{1,0:T(8,128)S(1)}, u32[]{:S(2)}, u32[]{:S(2)}) collective-permute-start(f32[256,128]{1,0:T(8,128)} %compose.6), channel_id=1, source_target_pairs={{0,24},{24,32},{32,56},{56,64},{64,88},{88,96},{96,120},{120,128},... | collective-permute-start | bytes 393224 | tf_op jit(solution)/shard_map/ppermute | solution.py:62
  133.1 13.5 %collective-permute-start.17 = (f32[128,128]{1,0:T(8,128)S(1)}, f32[128,128]{1,0:T(8,128)S(1)}, u32[]{:S(2)}, u32[]{:S(2)}) collective-permute-start(f32[128,128]{1,0:T(8,128)S(1)} %slice.44), channel_id=1, source_target_pairs={{0,152},{24,160},{32,184},{56,192},{64,216},{88,224},{96,248},{8,1... | collective-permute-start | bytes 196616 | tf_op jit(solution)/shard_map/ppermute | solution.py:62
  146.6 0.6 copy-start.4
  147.3 0.7 copy-start.3
Sparse Core Ops, SparseCore 0:
  11.2 124.1 all-gather.1

commit v3 on v2

--- a/solution.py
+++ b/solution.py
@@ -25,11 +25,16 @@
 
 
 def dot3(left, right, dims):
-    return (
-        dot1(left[0], right[0], dims)
-        + dot1(left[0], right[1], dims)
-        + dot1(left[1], right[0], dims)
-    )
+    (lc,), (rc,) = dims[0]
+    kept = right[0].shape[1 - rc]
+    lhs = jnp.concatenate(left, axis=lc)
+    if kept == LANES:
+        rhs = jnp.concatenate(right, axis=1 - rc)
+        rhs = jnp.concatenate([rhs, rhs], axis=rc)
+        out = dot1(lhs, rhs, dims)
+        return out[:, :LANES] + out[:, LANES:]
+    rhs = jnp.concatenate([right[0], right[0]], axis=rc)
+    return dot1(lhs, rhs, dims) + dot1(left[0], right[1], dims)
 
 
 Y_SIZE = 4
@@ -215,21 +220,10 @@
     out_ref[...] = (total / scale).astype(BF16)
 
 
-def compose_kernel(before_ref, now_ref, out_ref):
-    rows = before_ref.shape[0]
-    now = now_ref[...]
-    moved = dot3(split(before_ref[...]), split(now[:LANES]), ROWS)
-    if rows > LANES:
-        out_ref[: rows - LANES] = moved[: rows - LANES]
-    out_ref[rows - LANES :] = moved[rows - LANES :] + now[LANES:]
-
-
 def compose(before, now):
-    return pl.pallas_call(
-        compose_kernel,
-        out_shape=jax.ShapeDtypeStruct(before.shape, F32),
-        name="compose",
-    )(before, now)
+    moved = jnp.matmul(before, now[:LANES], precision=lax.Precision.HIGHEST)
+    kept = lax.broadcasted_iota(jnp.int32, now.shape, 0) >= LANES
+    return moved + jnp.where(kept, now, 0.0)[-before.shape[0] :]
 
 
 def at(buffer, block, index):
@@ -261,20 +255,14 @@
     own = jnp.where(second, second_half, first_half)
     other = jnp.where(second, first_half, second_half)
 
-    across = permute(other, lambda z, y: (z, y ^ 1))
     part = lax.dynamic_slice_in_dim(tokens, group * rows_each, rows_each, axis=0)
     part = permute(part, lambda z, y: (z, y ^ 1))
-    duo = jnp.where(
-        place == 0,
-        jnp.concatenate([own, across], axis=0),
-        jnp.concatenate([across, own], axis=0),
-    )
-    mate = permute(duo, lambda z, y: (z, 3 - y))
-    quad = jnp.where(
-        pair == 0,
-        jnp.concatenate([duo, mate], axis=0),
-        jnp.concatenate([mate, duo], axis=0),
-    )
+    quad = jnp.zeros((Y_SIZE,) + own.shape, BF16)
+    quad = at(quad, own, y)
+    for flip, block in ((3, own), (1, other), (2, other)):
+        came = permute(block, lambda z, y, flip=flip: (z, y ^ flip))
+        quad = at(quad, came, y ^ flip)
+    quad = quad.reshape(Y_SIZE * own.shape[0], own.shape[1])
     weights = jnp.zeros((z_size,) + quad.shape, BF16)
     weights = at(weights, quad, z)
     parts = jnp.zeros((columns,) + part.shape, BF16)
@@ -285,8 +273,15 @@
         down = permute(down, lambda z, y: (z - 1, y))
         weights = at(weights, up, (z - step) % z_size)
         weights = at(weights, down, (z + step) % z_size)
-    up = permute(up, lambda z, y: (z + 1, y))
-    weights = at(weights, up, (z - z_size // 2) % z_size)
+    middle = quad.shape[0] // 2
+    last = jnp.concatenate(
+        [
+            permute(up[:middle], lambda z, y: (z + 1, y)),
+            permute(down[middle:], lambda z, y: (z - 1, y)),
+        ],
+        axis=0,
+    )
+    weights = at(weights, last, (z + z_size // 2) % z_size)
     for step in range(1, columns):
         moved = permute_heads(part, lambda i, step=step: i + 2 * step)
         parts = at(parts, moved, (column - step) % columns)

time: 186 us -> 165 us (0.89)
  blocking collectives: 19.5 us -> 0 us
  starting transfers between devices: 55.9 us -> 72.5 us
  Pallas kernels: 31.4 us -> 19.2 us
  waiting for transfers between devices: 40.7 us -> 34.7 us
  matrix products: 11.8 us -> 14.3 us
  local copies, waits for them, and re-layouts: 9.14 us -> 6.78 us
    all_to_all x1 -> x0, blocking collectives: 19.5 us -> none  [shards(): lax.all_to_all(stacked, ('p', 'head'), split_axis=0, concat_axis=0, tiled...]
    all_to_all x0 -> x1, starting transfers between devices: none -> 17 us  [shards(): lax.all_to_all(stacked, ('p', 'head'), split_axis=0, concat_axis=0, tiled...]
    ppermute x10 -> x12, waiting for transfers between devices: 26.5 us -> 14.3 us  [permute(): return lax.ppermute(array, CTX, pairs)]
    pallas_call x4 -> x0, Pallas kernels: 7.24 us -> none  [compose(): pl.pallas_call(compose_kernel, out_shape=jax.ShapeDtypeStruct(before.shap...]
    all_to_all x0 -> x1, waiting for transfers between devices: none -> 7.2 us  [shards(): lax.all_to_all(stacked, ('p', 'head'), split_axis=0, concat_axis=0, tiled...]
    pallas_call x1, Pallas kernels: 21.7 us -> 16.7 us  [local_pass(): pl.pallas_call(local_kernel, grid_spec=pltpu.PrefetchScalarGridSpec(num_s...]
    dot_general x0 -> x4, matrix products: none -> 2.58 us  [compose(): moved = jnp.matmul(before, now[:LANES], precision=lax.Precision.HIGHEST)]
    unnamed x12 -> x2, local copies, waits for them, and re-layouts: 3.25 us -> 1.38 us
  transfers between devices with their start and end apart: 20 -> 23, of which waited for: 11 -> 11; matrix products, arithmetic and copies ran while one was open for 7% -> 9% of each run, Pallas kernels for 17% -> 12%
where the time goes in v3:
time: 165 us; the launch traced here: 164 us
  starting transfers between devices  72.5 us (44%)
  waiting for transfers between devices  34.7 us (21%)
  Pallas kernels  19.2 us (12%)
  between operations  15.1 us (9%)
  matrix products  14.3 us (9%)
  local copies, waits for them, and re-layouts  6.78 us (4%)
  other arithmetic  1.89 us (1%)
    ppermute x5, starting transfers between devices, shift(): return lax.ppermute(array, CTX, pairs)  28.5 us
    ppermute x12, starting transfers between devices, permute(): return lax.ppermute(array, CTX, pairs)  19.6 us
    all_to_all x1, starting transfers between devices, shards(): lax.all_to_all(stacked, ('p', 'head'), split_axis=0, concat_axis=0, tiled...  17 us
    pallas_call x1, Pallas kernels, local_pass(): pl.pallas_call(local_kernel, grid_spec=pltpu.PrefetchScalarGridSpec(num_s...  16.7 us
    ppermute x12, waiting for transfers between devices, permute(): return lax.ppermute(array, CTX, pairs)  14.3 us
    ppermute x5, waiting for transfers between devices, shift(): return lax.ppermute(array, CTX, pairs)  8.64 us
    ppermute x4, starting transfers between devices, permute_heads(): lax.ppermute(array, 'head', [(i, move(i) % count) for i in range(count)])  7.41 us
    all_to_all x1, waiting for transfers between devices, shards(): lax.all_to_all(stacked, ('p', 'head'), split_axis=0, concat_axis=0, tiled...  7.2 us
  transfers between devices with their start and end apart: 23, of which 11 were waited for; matrix products, arithmetic and copies ran while one was open for 9% of the time, Pallas kernels for 12%

profile of v3, /device:TPU:1, one launch (start us, length us, event | category | flops | bytes accessed | tf_op | source)
XLA Modules:
  0.0 164.5 jit_solution(1478571604002502416)
XLA Ops:
  6.5 0.7 all-gather.2.cloned.1.call-update
  7.3 0.8 fusion.18
  8.1 0.1 copy.10
  8.2 0.1 copy.11
  8.3 0.1 pad.32.clone
  8.4 1.0 fusion.17
  9.3 0.1 broadcast_select_fusion
  9.4 2.2 %collective-permute-start.6 = (bf16[64,768]{1,0:T(8,128)(2,1)S(1)}, bf16[64,768]{1,0:T(8,128)(2,1)S(1)}, u32[]{:S(2)}, u32[]{:S(2)}) collective-permute-start(bf16[64,768]{1,0:T(8,128)(2,1)S(1)} %get-tuple-element.15), channel_id=1, source_target_pairs={{0,8},{8,0},{16,24},{24,16},{32,40},{40,32},{48,56},{56,48},{64,72... | collective-permute-start | bytes 294920 | tf_op jit(solution)/shard_map/ppermute | solution.py:52
  11.6 2.6 %collective-permute-start.7 = (bf16[64,768]{1,0:T(8,128)(2,1)S(1)}, bf16[64,768]{1,0:T(8,128)(2,1)S(1)}, u32[]{:S(2)}, u32[]{:S(2)}) collective-permute-start(bf16[64,768]{1,0:T(8,128)(2,1)S(1)} %get-tuple-element.15), channel_id=1, source_target_pairs={{0,16},{8,24},{16,0},{24,8},{32,48},{40,56},{48,32},{56,40},{64,80... | collective-permute-start | bytes 294920 | tf_op jit(solution)/shard_map/ppermute | solution.py:52
  14.2 1.0 constant_dynamic-slice_fusion
  15.2 0.1 collective-permute-start
  15.3 0.6 collective-permute-start.5
  15.9 0.1 copy.8
  16.0 0.1 copy.9
  16.2 1.3 fusion.19
  18.8 0.1 pad_bitcast_fusion
  18.9 0.8 fusion.14
  19.7 0.6 select_maximum_fusion.row_ref
  20.3 0.9 collective-permute-done.5
  21.2 0.0 collective-permute-done.6
  21.3 1.7 %collective-permute-start.8 = (bf16[256,768]{1,0:T(8,128)(2,1)S(1)}, bf16[256,768]{1,0:T(8,128)(2,1)S(1)}, u32[]{:S(2)}, u32[]{:S(2)}) collective-permute-start(bf16[256,768]{1,0:T(8,128)(2,1)S(1)} %bitcast.79), channel_id=1, source_target_pairs={{0,32},{8,40},{16,48},{24,56},{32,64},{40,72},{48,80},{56,88},{64,... | collective-permute-start | bytes 1179656 | tf_op jit(solution)/shard_map/ppermute | solution.py:52
  23.0 4.0 %collective-permute-start.9 = (bf16[256,768]{1,0:T(8,128)(2,1)S(1)}, bf16[256,768]{1,0:T(8,128)(2,1)S(1)}, u32[]{:S(2)}, u32[]{:S(2)}) collective-permute-start(bf16[256,768]{1,0:T(8,128)(2,1)S(1)} %bitcast.80), channel_id=1, source_target_pairs={{0,224},{8,232},{16,240},{24,248},{32,0},{40,8},{48,16},{56,24},{6... | collective-permute-start | bytes 1179656 | tf_op jit(solution)/shard_map/ppermute | solution.py:52
  27.0 0.2 broadcast_in_dim.69
  27.3 0.0 collective-permute-done
  27.3 1.3 collective-permute-start.1
  28.6 2.5 %collective-permute-start.2 = (bf16[64,2048]{1,0:T(8,128)(2,1)S(1)}, bf16[64,2048]{1,0:T(8,128)(2,1)S(1)}, u32[]{:S(2)}, u32[]{:S(2)}) collective-permute-start(bf16[64,2048]{1,0:T(8,128)(2,1)S(1)} %collective-permute-done), channel_id=1, source_target_pairs={{0,4},{1,5},{2,6},{3,7},{4,0},{5,1},{6,2},{7,3},{8,12},{9,13},{10,... | collective-permute-start | bytes 786440 | tf_op jit(solution)/shard_map/ppermute | solution.py:57
  31.0 1.2 collective-permute-start.3
  32.2 0.1 broadcast_in_dim.64
  32.3 2.8 %collective-permute-done.8 = bf16[256,768]{1,0:T(8,128)(2,1)S(1)} collective-permute-done((bf16[256,768]{1,0:T(8,128)(2,1)S(1)}, bf16[256,768]{1,0:T(8,128)(2,1)S(1)}, u32[]{:S(2)}, u32[]{:S(2)}) %collective-permute-start.8) | collective-permute-done | bytes 393248 | tf_op jit(solution)/shard_map/ppermute | solution.py:52
  35.1 0.0 collective-permute-start.10
  35.2 2.7 %collective-permute-start.11 = (bf16[256,768]{1,0:T(8,128)(2,1)S(1)}, bf16[256,768]{1,0:T(8,128)(2,1)S(1)}, u32[]{:S(2)}, u32[]{:S(2)}) collective-permute-start(bf16[256,768]{1,0:T(8,128)(2,1)S(1)} %collective-permute-done.9), channel_id=1, source_target_pairs={{0,224},{8,232},{16,240},{24,248},{32,0},{40,8},{48,16},{56,24},{6... | collective-permute-start | bytes 1179656 | tf_op jit(solution)/shard_map/ppermute | solution.py:52
  37.9 3.8 %collective-permute-done.2 = bf16[64,2048]{1,0:T(8,128)(2,1)S(1)} collective-permute-done((bf16[64,2048]{1,0:T(8,128)(2,1)S(1)}, bf16[64,2048]{1,0:T(8,128)(2,1)S(1)}, u32[]{:S(2)}, u32[]{:S(2)}) %collective-permute-start.2) | collective-permute-done | bytes 262176 | tf_op jit(solution)/shard_map/ppermute | solution.py:57
  41.8 2.5 %collective-permute-start.4 = (bf16[4,64,2048]{2,1,0:T(8,128)(2,1)S(1)}, bf16[4,64,2048]{2,1,0:T(8,128)(2,1)S(1)}, u32[]{:S(2)}, u32[]{:S(2)}) collective-permute-start(bf16[4,64,2048]{2,1,0:T(8,128)(2,1)S(1)} %bitcast_dynamic-update-slice_fusion.7), channel_id=1, source_target_pairs={{0,1},{1,0},{2,3},{3,2},{4,5},{5,4},{6,7},{7,6},{8,9},{9,8},{10,11... | collective-permute-start | bytes 3145736 | tf_op jit(solution)/shard_map/ppermute | solution.py:57
  44.4 1.2 collective-permute-done.10
  45.5 2.7 %collective-permute-start.13 = (bf16[256,768]{1,0:T(8,128)(2,1)S(1)}, bf16[256,768]{1,0:T(8,128)(2,1)S(1)}, u32[]{:S(2)}, u32[]{:S(2)}) collective-permute-start(bf16[256,768]{1,0:T(8,128)(2,1)S(1)} %collective-permute-done.11), channel_id=1, source_target_pairs={{0,224},{8,232},{16,240},{24,248},{32,0},{40,8},{48,16},{56,24},{6... | collective-permute-start | bytes 1179656 | tf_op jit(solution)/shard_map/ppermute | solution.py:52
  48.3 6.7 %collective-permute-done.12 = bf16[256,768]{1,0:T(8,128)(2,1)S(1)} collective-permute-done((bf16[256,768]{1,0:T(8,128)(2,1)S(1)}, bf16[256,768]{1,0:T(8,128)(2,1)S(1)}, u32[]{:S(2)}, u32[]{:S(2)}) %collective-permute-start.12) | collective-permute-done | bytes 393248 | tf_op jit(solution)/shard_map/ppermute | solution.py:52
  55.0 0.1 collective-permute-start.14
  55.1 2.9 %collective-permute-start.15 = (bf16[128,768]{1,0:T(8,128)(2,1)S(1)}, bf16[128,768]{1,0:T(8,128)(2,1)S(1)}, u32[]{:S(2)}, u32[]{:S(2)}) collective-permute-start(bf16[128,768]{1,0:T(8,128)(2,1)S(1)} %slice.73), channel_id=1, source_target_pairs={{0,224},{8,232},{16,240},{24,248},{32,0},{40,8},{48,16},{56,24},{6... | collective-permute-start | bytes 589832 | tf_op jit(solution)/shard_map/ppermute | solution.py:52
  58.1 2.7 %collective-permute-done.14 = bf16[128,768]{1,0:T(8,128)(2,1)S(1)} collective-permute-done((bf16[128,768]{1,0:T(8,128)(2,1)S(1)}, bf16[128,768]{1,0:T(8,128)(2,1)S(1)}, u32[]{:S(2)}, u32[]{:S(2)}) %collective-permute-start.14) | collective-permute-done | bytes 196640 | tf_op jit(solution)/shard_map/ppermute | solution.py:52
  60.8 0.1 select_bitcast_fusion.1
  61.0 0.0 copy-start
  61.0 0.2 pad_maximum_fusion
  61.2 1.4 copy-done
  62.6 5.1 %fusion.proj_ref = f32[1024,768]{1,0:T(8,128)} fusion(bf16[2048,768]{1,0:T(8,128)(2,1)S(1)} %bitcast.77, bf16[512,2048]{1,0:T(8,128)(2,1)S(1)} %bitcast.78, bf16[512,2048]{1,0:T(8,128)(2,1)S(1)} %copy-done), kind=kOutput, calls=%fused_computation | convolution fusion | flops 3229614080 | bytes 10485760 | tf_op jit(solution)/shard_map/dot_general | solution.py:294
  67.6 16.7 %local.1 = (f32[256,128]{1,0:T(8,128)}, f32[1024,128]{1,0:T(8,128)}, f32[1024,128]{1,0:T(8,128)}) custom-call(s32[1]{0:T(128)} %bitcast.swap_ref, f32[1024,768]{1,0:T(8,128)} %fusion.proj_ref, f32[8,128]{1,0:T(8,128)} %select_maximum_fusion.row_ref), custom_call_target="tpu_custom_call" | custom-call | tf_op jit(solution)/shard_map/local/pallas_call | solution.py:196
  84.4 2.9 %collective-permute-start.16 = (f32[256,128]{1,0:T(8,128)}, f32[256,128]{1,0:T(8,128)S(1)}, u32[]{:S(2)}, u32[]{:S(2)}) collective-permute-start(f32[256,128]{1,0:T(8,128)} %get-tuple-element.8), channel_id=1, source_target_pairs={{0,24},{24,32},{32,56},{56,64},{64,88},{88,96},{96,120},{120,128},... | collective-permute-start | bytes 393224 | tf_op jit(solution)/shard_map/ppermute | solution.py:67
  87.3 2.2 %collective-permute-done.16 = f32[256,128]{1,0:T(8,128)S(1)} collective-permute-done((f32[256,128]{1,0:T(8,128)}, f32[256,128]{1,0:T(8,128)S(1)}, u32[]{:S(2)}, u32[]{:S(2)}) %collective-permute-start.16) | collective-permute-done | bytes 131104 | tf_op jit(solution)/shard_map/ppermute | solution.py:67
  89.5 1.2 convolution_add_fusion.2
  90.8 3.8 %collective-permute-start.17 = (f32[256,128]{1,0:T(8,128)S(1)}, f32[256,128]{1,0:T(8,128)S(1)}, u32[]{:S(2)}, u32[]{:S(2)}) collective-permute-start(f32[256,128]{1,0:T(8,128)S(1)} %convolution_add_fusion.2), channel_id=1, source_target_pairs={{0,32},{24,56},{32,64},{56,88},{64,96},{88,120},{96,128},{120,152}... | collective-permute-start | bytes 393224 | tf_op jit(solution)/shard_map/ppermute | solution.py:67
  94.6 1.9 %collective-permute-done.17 = f32[256,128]{1,0:T(8,128)S(1)} collective-permute-done((f32[256,128]{1,0:T(8,128)S(1)}, f32[256,128]{1,0:T(8,128)S(1)}, u32[]{:S(2)}, u32[]{:S(2)}) %collective-permute-start.17) | collective-permute-done | bytes 131104 | tf_op jit(solution)/shard_map/ppermute | solution.py:67
  96.5 0.3 convolution_add_fusion.1
  96.8 6.5 %collective-permute-start.18 = (f32[256,128]{1,0:T(8,128)S(1)}, f32[256,128]{1,0:T(8,128)S(1)}, u32[]{:S(2)}, u32[]{:S(2)}) collective-permute-start(f32[256,128]{1,0:T(8,128)S(1)} %convolution_add_fusion.1), channel_id=1, source_target_pairs={{0,64},{24,88},{32,96},{56,120},{64,128},{88,152},{96,160},{120,18... | collective-permute-start | bytes 393224 | tf_op jit(solution)/shard_map/ppermute | solution.py:67
  103.2 2.4 %collective-permute-done.18 = f32[256,128]{1,0:T(8,128)S(1)} collective-permute-done((f32[256,128]{1,0:T(8,128)S(1)}, f32[256,128]{1,0:T(8,128)S(1)}, u32[]{:S(2)}, u32[]{:S(2)}) %collective-permute-start.18) | collective-permute-done | bytes 131104 | tf_op jit(solution)/shard_map/ppermute | solution.py:67
  105.7 0.3 convolution_add_fusion
  106.0 3.8 %collective-permute-start.20 = (f32[256,128]{1,0:T(8,128)S(1)}, f32[256,128]{1,0:T(8,128)S(1)}, u32[]{:S(2)}, u32[]{:S(2)}) collective-permute-start(f32[256,128]{1,0:T(8,128)S(1)} %convolution_add_fusion), channel_id=1, source_target_pairs={{0,24},{24,32},{32,56},{56,64},{64,88},{88,96},{96,120},{120,128},... | collective-permute-start | bytes 393224 | tf_op jit(solution)/shard_map/ppermute | solution.py:67
  109.8 11.5 %collective-permute-start.19 = (f32[128,128]{1,0:T(8,128)S(1)}, f32[128,128]{1,0:T(8,128)S(1)}, u32[]{:S(2)}, u32[]{:S(2)}) collective-permute-start(f32[128,128]{1,0:T(8,128)S(1)} %slice.76), channel_id=1, source_target_pairs={{0,152},{24,160},{32,184},{56,192},{64,216},{88,224},{96,248},{8,1... | collective-permute-start | bytes 196616 | tf_op jit(solution)/shard_map/ppermute | solution.py:67
  121.3 2.0 %collective-permute-done.19 = f32[128,128]{1,0:T(8,128)S(1)} collective-permute-done((f32[128,128]{1,0:T(8,128)S(1)}, f32[128,128]{1,0:T(8,128)S(1)}, u32[]{:S(2)}, u32[]{:S(2)}) %collective-permute-start.19) | collective-permute-done | bytes 65568 | tf_op jit(solution)/shard_map/ppermute | solution.py:67
  123.3 0.8 convolution_add_fusion.3.state_ref
  124.2 2.5 %finish.1 = bf16[1024,128]{1,0:T(8,128)(2,1)} custom-call(f32[128,128]{1,0:T(8,128)} %convolution_add_fusion.3.state_ref, f32[1024,128]{1,0:T(8,128)} %get-tuple-element.9.query_ref, f32[1024,128]{1,0:T(8,128)} %get-tuple-element.10.part_ref), custom_call_target="tpu_custom_call" | custom-call | tf_op jit(solution)/shard_map/finish/pallas_call | solution.py:313
  126.6 17.0 %all-to-all-start = ((bf16[16,64,128]{2,1,0:T(8,128)(2,1)}), bf16[16,64,128]{2,1,0:T(8,128)(2,1)S(1)}, u32[]{:S(2)}, u32[]{:S(2)}) async-start(bf16[16,64,128]{2,1,0:T(8,128)(2,1)} %bitcast.83), calls=%async_computation | async-start | bytes 524288 | tf_op jit(solution)/shard_map/all_to_all | solution.py:319
  143.6 7.2 %all-to-all-done = bf16[16,64,128]{2,1,0:T(8,128)(2,1)S(1)} async-done(((bf16[16,64,128]{2,1,0:T(8,128)(2,1)}), bf16[16,64,128]{2,1,0:T(8,128)(2,1)S(1)}, u32[]{:S(2)}, u32[]{:S(2)}) %all-to-all-start) | async-done | bytes 262176 | tf_op jit(solution)/shard_map/all_to_all | solution.py:319
  150.8 0.1 reverse_select_fusion
  150.9 0.0 all-gather.2.cloned.1.call-done
  150.9 6.7 %fusion.4 = bf16[64,2048]{1,0:T(8,128)(2,1)} fusion(bf16[8,2048,256]{2,1,0:T(8,128)(2,1)} %bitcast.76, bf16[8,64,128]{2,1,0:T(8,128)(2,1)S(1)} %get-tuple-element.14, bf16[8,64,128]{2,1,0:T(8,128)(2,1)S(1)} %get-tuple-element.13), kind=kOutput, calls=%fused_computation.5 | convolution fusion | flops 537526272 | bytes 8912896 | tf_op jit(solution)/shard_map/hrk,hdk->rd/dot_general | solution.py:323
  (36 shorter events, 0.6 us)
Async XLA Ops:
  6.5 144.4 %all-gather.2.cloned.1.call-start = ((), (), s32[]{:S(2)}) async-start(), calls=%async_computation.1 | async-start | bytes 8421376 | tf_op jit(solution)/shard_map/all_gather | solution.py:247
  9.4 11.8 %collective-permute-start.6 = (bf16[64,768]{1,0:T(8,128)(2,1)S(1)}, bf16[64,768]{1,0:T(8,128)(2,1)S(1)}, u32[]{:S(2)}, u32[]{:S(2)}) collective-permute-start(bf16[64,768]{1,0:T(8,128)(2,1)S(1)} %get-tuple-element.15), channel_id=1, source_target_pairs={{0,8},{8,0},{16,24},{24,16},{32,40},{40,32},{48,56},{56,48},{64,72... | collective-permute-start | bytes 294920 | tf_op jit(solution)/shard_map/ppermute | solution.py:52
  11.6 9.6 %collective-permute-start.7 = (bf16[64,768]{1,0:T(8,128)(2,1)S(1)}, bf16[64,768]{1,0:T(8,128)(2,1)S(1)}, u32[]{:S(2)}, u32[]{:S(2)}) collective-permute-start(bf16[64,768]{1,0:T(8,128)(2,1)S(1)} %get-tuple-element.15), channel_id=1, source_target_pairs={{0,16},{8,24},{16,0},{24,8},{32,48},{40,56},{48,32},{56,40},{64,80... | collective-permute-start | bytes 294920 | tf_op jit(solution)/shard_map/ppermute | solution.py:52
  15.2 12.1 %collective-permute-start = (bf16[64,2048]{1,0:T(8,128)(2,1)S(1)}, bf16[64,2048]{1,0:T(8,128)(2,1)S(1)}, u32[]{:S(2)}, u32[]{:S(2)}) collective-permute-start(bf16[64,2048]{1,0:T(8,128)(2,1)S(1)} %constant_dynamic-slice_fusion), channel_id=1, source_target_pairs={{0,8},{8,0},{16,24},{24,16},{32,40},{40,32},{48,56},{56,48},{64,72... | collective-permute-start | bytes 786440 | tf_op jit(solution)/shard_map/ppermute | solution.py:52
  15.3 5.9 %collective-permute-start.5 = (bf16[64,768]{1,0:T(8,128)(2,1)S(1)}, bf16[64,768]{1,0:T(8,128)(2,1)S(1)}, u32[]{:S(2)}, u32[]{:S(2)}) collective-permute-start(bf16[64,768]{1,0:T(8,128)(2,1)S(1)} %get-tuple-element.16), channel_id=1, source_target_pairs={{0,24},{8,16},{16,8},{24,0},{32,56},{40,48},{48,40},{56,32},{64,88... | collective-permute-start | bytes 294920 | tf_op jit(solution)/shard_map/ppermute | solution.py:52
  21.3 13.9 %collective-permute-start.8 = (bf16[256,768]{1,0:T(8,128)(2,1)S(1)}, bf16[256,768]{1,0:T(8,128)(2,1)S(1)}, u32[]{:S(2)}, u32[]{:S(2)}) collective-permute-start(bf16[256,768]{1,0:T(8,128)(2,1)S(1)} %bitcast.79), channel_id=1, source_target_pairs={{0,32},{8,40},{16,48},{24,56},{32,64},{40,72},{48,80},{56,88},{64,... | collective-permute-start | bytes 1179656 | tf_op jit(solution)/shard_map/ppermute | solution.py:52
  23.0 12.2 %collective-permute-start.9 = (bf16[256,768]{1,0:T(8,128)(2,1)S(1)}, bf16[256,768]{1,0:T(8,128)(2,1)S(1)}, u32[]{:S(2)}, u32[]{:S(2)}) collective-permute-start(bf16[256,768]{1,0:T(8,128)(2,1)S(1)} %bitcast.80), channel_id=1, source_target_pairs={{0,224},{8,232},{16,240},{24,248},{32,0},{40,8},{48,16},{56,24},{6... | collective-permute-start | bytes 1179656 | tf_op jit(solution)/shard_map/ppermute | solution.py:52
  27.3 10.6 %collective-permute-start.1 = (bf16[64,2048]{1,0:T(8,128)(2,1)S(1)}, bf16[64,2048]{1,0:T(8,128)(2,1)S(1)}, u32[]{:S(2)}, u32[]{:S(2)}) collective-permute-start(bf16[64,2048]{1,0:T(8,128)(2,1)S(1)} %collective-permute-done), channel_id=1, source_target_pairs={{0,2},{1,3},{2,4},{3,5},{4,6},{5,7},{6,0},{7,1},{8,10},{9,11},{10,... | collective-permute-start | bytes 786440 | tf_op jit(solution)/shard_map/ppermute | solution.py:57
  28.6 13.2 %collective-permute-start.2 = (bf16[64,2048]{1,0:T(8,128)(2,1)S(1)}, bf16[64,2048]{1,0:T(8,128)(2,1)S(1)}, u32[]{:S(2)}, u32[]{:S(2)}) collective-permute-start(bf16[64,2048]{1,0:T(8,128)(2,1)S(1)} %collective-permute-done), channel_id=1, source_target_pairs={{0,4},{1,5},{2,6},{3,7},{4,0},{5,1},{6,2},{7,3},{8,12},{9,13},{10,... | collective-permute-start | bytes 786440 | tf_op jit(solution)/shard_map/ppermute | solution.py:57
  31.0 10.8 %collective-permute-start.3 = (bf16[64,2048]{1,0:T(8,128)(2,1)S(1)}, bf16[64,2048]{1,0:T(8,128)(2,1)S(1)}, u32[]{:S(2)}, u32[]{:S(2)}) collective-permute-start(bf16[64,2048]{1,0:T(8,128)(2,1)S(1)} %collective-permute-done), channel_id=1, source_target_pairs={{0,6},{1,7},{2,0},{3,1},{4,2},{5,3},{6,4},{7,5},{8,14},{9,15},{10,... | collective-permute-start | bytes 786440 | tf_op jit(solution)/shard_map/ppermute | solution.py:57
  35.1 10.4 %collective-permute-start.10 = (bf16[256,768]{1,0:T(8,128)(2,1)S(1)}, bf16[256,768]{1,0:T(8,128)(2,1)S(1)}, u32[]{:S(2)}, u32[]{:S(2)}) collective-permute-start(bf16[256,768]{1,0:T(8,128)(2,1)S(1)} %collective-permute-done.8), channel_id=1, source_target_pairs={{0,32},{8,40},{16,48},{24,56},{32,64},{40,72},{48,80},{56,88},{64,... | collective-permute-start | bytes 1179656 | tf_op jit(solution)/shard_map/ppermute | solution.py:52
  35.2 10.4 %collective-permute-start.11 = (bf16[256,768]{1,0:T(8,128)(2,1)S(1)}, bf16[256,768]{1,0:T(8,128)(2,1)S(1)}, u32[]{:S(2)}, u32[]{:S(2)}) collective-permute-start(bf16[256,768]{1,0:T(8,128)(2,1)S(1)} %collective-permute-done.9), channel_id=1, source_target_pairs={{0,224},{8,232},{16,240},{24,248},{32,0},{40,8},{48,16},{56,24},{6... | collective-permute-start | bytes 1179656 | tf_op jit(solution)/shard_map/ppermute | solution.py:52
  41.8 19.0 %collective-permute-start.4 = (bf16[4,64,2048]{2,1,0:T(8,128)(2,1)S(1)}, bf16[4,64,2048]{2,1,0:T(8,128)(2,1)S(1)}, u32[]{:S(2)}, u32[]{:S(2)}) collective-permute-start(bf16[4,64,2048]{2,1,0:T(8,128)(2,1)S(1)} %bitcast_dynamic-update-slice_fusion.7), channel_id=1, source_target_pairs={{0,1},{1,0},{2,3},{3,2},{4,5},{5,4},{6,7},{7,6},{8,9},{9,8},{10,11... | collective-permute-start | bytes 3145736 | tf_op jit(solution)/shard_map/ppermute | solution.py:57
  45.5 9.4 %collective-permute-start.12 = (bf16[256,768]{1,0:T(8,128)(2,1)S(1)}, bf16[256,768]{1,0:T(8,128)(2,1)S(1)}, u32[]{:S(2)}, u32[]{:S(2)}) collective-permute-start(bf16[256,768]{1,0:T(8,128)(2,1)S(1)} %collective-permute-done.10), channel_id=1, source_target_pairs={{0,32},{8,40},{16,48},{24,56},{32,64},{40,72},{48,80},{56,88},{64,... | collective-permute-start | bytes 1179656 | tf_op jit(solution)/shard_map/ppermute | solution.py:52
  45.5 9.5 %collective-permute-start.13 = (bf16[256,768]{1,0:T(8,128)(2,1)S(1)}, bf16[256,768]{1,0:T(8,128)(2,1)S(1)}, u32[]{:S(2)}, u32[]{:S(2)}) collective-permute-start(bf16[256,768]{1,0:T(8,128)(2,1)S(1)} %collective-permute-done.11), channel_id=1, source_target_pairs={{0,224},{8,232},{16,240},{24,248},{32,0},{40,8},{48,16},{56,24},{6... | collective-permute-start | bytes 1179656 | tf_op jit(solution)/shard_map/ppermute | solution.py:52
  55.0 5.8 %collective-permute-start.14 = (bf16[128,768]{1,0:T(8,128)(2,1)S(1)}, bf16[128,768]{1,0:T(8,128)(2,1)S(1)}, u32[]{:S(2)}, u32[]{:S(2)}) collective-permute-start(bf16[128,768]{1,0:T(8,128)(2,1)S(1)} %slice.72), channel_id=1, source_target_pairs={{0,32},{8,40},{16,48},{24,56},{32,64},{40,72},{48,80},{56,88},{64,... | collective-permute-start | bytes 589832 | tf_op jit(solution)/shard_map/ppermute | solution.py:52
  55.1 5.7 %collective-permute-start.15 = (bf16[128,768]{1,0:T(8,128)(2,1)S(1)}, bf16[128,768]{1,0:T(8,128)(2,1)S(1)}, u32[]{:S(2)}, u32[]{:S(2)}) collective-permute-start(bf16[128,768]{1,0:T(8,128)(2,1)S(1)} %slice.73), channel_id=1, source_target_pairs={{0,224},{8,232},{16,240},{24,248},{32,0},{40,8},{48,16},{56,24},{6... | collective-permute-start | bytes 589832 | tf_op jit(solution)/shard_map/ppermute | solution.py:52
  61.0 1.6 copy-start
  84.4 5.2 %collective-permute-start.16 = (f32[256,128]{1,0:T(8,128)}, f32[256,128]{1,0:T(8,128)S(1)}, u32[]{:S(2)}, u32[]{:S(2)}) collective-permute-start(f32[256,128]{1,0:T(8,128)} %get-tuple-element.8), channel_id=1, source_target_pairs={{0,24},{24,32},{32,56},{56,64},{64,88},{88,96},{96,120},{120,128},... | collective-permute-start | bytes 393224 | tf_op jit(solution)/shard_map/ppermute | solution.py:67
  90.8 5.7 %collective-permute-start.17 = (f32[256,128]{1,0:T(8,128)S(1)}, f32[256,128]{1,0:T(8,128)S(1)}, u32[]{:S(2)}, u32[]{:S(2)}) collective-permute-start(f32[256,128]{1,0:T(8,128)S(1)} %convolution_add_fusion.2), channel_id=1, source_target_pairs={{0,32},{24,56},{32,64},{56,88},{64,96},{88,120},{96,128},{120,152}... | collective-permute-start | bytes 393224 | tf_op jit(solution)/shard_map/ppermute | solution.py:67
  96.8 8.9 %collective-permute-start.18 = (f32[256,128]{1,0:T(8,128)S(1)}, f32[256,128]{1,0:T(8,128)S(1)}, u32[]{:S(2)}, u32[]{:S(2)}) collective-permute-start(f32[256,128]{1,0:T(8,128)S(1)} %convolution_add_fusion.1), channel_id=1, source_target_pairs={{0,64},{24,88},{32,96},{56,120},{64,128},{88,152},{96,160},{120,18... | collective-permute-start | bytes 393224 | tf_op jit(solution)/shard_map/ppermute | solution.py:67
  106.0 17.4 %collective-permute-start.20 = (f32[256,128]{1,0:T(8,128)S(1)}, f32[256,128]{1,0:T(8,128)S(1)}, u32[]{:S(2)}, u32[]{:S(2)}) collective-permute-start(f32[256,128]{1,0:T(8,128)S(1)} %convolution_add_fusion), channel_id=1, source_target_pairs={{0,24},{24,32},{32,56},{56,64},{64,88},{88,96},{96,120},{120,128},... | collective-permute-start | bytes 393224 | tf_op jit(solution)/shard_map/ppermute | solution.py:67
  109.8 13.6 %collective-permute-start.19 = (f32[128,128]{1,0:T(8,128)S(1)}, f32[128,128]{1,0:T(8,128)S(1)}, u32[]{:S(2)}, u32[]{:S(2)}) collective-permute-start(f32[128,128]{1,0:T(8,128)S(1)} %slice.76), channel_id=1, source_target_pairs={{0,152},{24,160},{32,184},{56,192},{64,216},{88,224},{96,248},{8,1... | collective-permute-start | bytes 196616 | tf_op jit(solution)/shard_map/ppermute | solution.py:67
  126.6 24.2 %all-to-all-start = ((bf16[16,64,128]{2,1,0:T(8,128)(2,1)}), bf16[16,64,128]{2,1,0:T(8,128)(2,1)S(1)}, u32[]{:S(2)}, u32[]{:S(2)}) async-start(bf16[16,64,128]{2,1,0:T(8,128)(2,1)} %bitcast.83), calls=%async_computation | async-start | bytes 524288 | tf_op jit(solution)/shard_map/all_to_all | solution.py:319
Sparse Core Ops, SparseCore 0:
  11.2 122.4 all-gather.1

commit v4 on v3

--- a/solution.py
+++ b/solution.py
@@ -71,22 +71,55 @@
     return rows / jnp.sqrt(jnp.sum(rows * rows, axis=-1, keepdims=True) + 1e-06)
 
 
-def local_kernel(swap_ref, proj_ref, row_ref, state_ref, query_ref, out_ref, held_ref):
+def running_decay(gates, row_ref):
+    soft = jnp.maximum(gates, 0.0) + jnp.log1p(jnp.exp(-jnp.abs(gates)))
+    log_decay = -row_ref[1:2, :] * soft
+    row = lax.broadcasted_iota(jnp.int32, (BLOCK, BLOCK), 0)
+    col = lax.broadcasted_iota(jnp.int32, (BLOCK, BLOCK), 1)
+    lower = jnp.where(row >= col, 1.0, 0.0).astype(F32)
+    return [
+        jnp.dot(
+            lower,
+            log_decay[n * BLOCK : (n + 1) * BLOCK],
+            precision=lax.Precision.HIGHEST,
+            preferred_element_type=F32,
+        )
+        for n in range(gates.shape[0] // BLOCK)
+    ]
+
+
+def seen_before():
+    return (
+        lax.broadcasted_iota(jnp.int32, (BLOCK, 2 * BLOCK), 0)
+        >= lax.broadcasted_iota(jnp.int32, (BLOCK, 2 * BLOCK), 1) % BLOCK
+    )
+
+
+def reach_of(running, visible):
+    across = jnp.transpose(running)[2:3, :]
+    across = jnp.concatenate([across, across], axis=1)
+    return jnp.exp(jnp.where(visible, running[:, 2:3] - across, 0.0))
+
+
+def keys_of(proj_ref, rows):
+    return jnp.concatenate(
+        [
+            unit(proj_ref[rows, LANES : 2 * LANES]),
+            unit(proj_ref[rows, 2 * LANES : 3 * LANES]),
+        ],
+        axis=0,
+    )
+
+
+def local_kernel(swap_ref, proj_ref, row_ref, state_ref, solved_ref, starts_ref, held_ref):
     del swap_ref
     tokens = proj_ref.shape[0]
     width = LANES
     blocks = tokens // BLOCK
     span = 2 * BLOCK
     gates = proj_ref[:, 5 * width :]
-    bias = row_ref[0:1, :]
-    rate = row_ref[1:2, :]
-    betas = 2.0 / (1.0 + jnp.exp(-(gates + bias)))
-    soft = jnp.maximum(gates, 0.0) + jnp.log1p(jnp.exp(-jnp.abs(gates)))
-    log_decay = -rate * soft
-    row64 = lax.broadcasted_iota(jnp.int32, (BLOCK, BLOCK), 0)
-    col64 = lax.broadcasted_iota(jnp.int32, (BLOCK, BLOCK), 1)
-    lower = jnp.where(row64 >= col64, 1.0, 0.0).astype(F32)
-    base = 0
+    betas = 2.0 / (1.0 + jnp.exp(-(gates + row_ref[0:1, :])))
+    runnings = running_decay(gates, row_ref)
     row_i = lax.broadcasted_iota(jnp.int32, (span, span), 0)
     col_i = lax.broadcasted_iota(jnp.int32, (span, span), 1)
     row_t, row_r = row_i % BLOCK, row_i // BLOCK
@@ -94,10 +127,7 @@
     strict = (row_t > col_t) | ((row_t == col_t) & (row_r > col_r))
     within = (row_t == col_t) & (row_r > col_r)
     eye = jnp.where(row_i == col_i, 1.0, 0.0).astype(F32)
-    visible = (
-        lax.broadcasted_iota(jnp.int32, (BLOCK, span), 0)
-        >= lax.broadcasted_iota(jnp.int32, (BLOCK, span), 1) % BLOCK
-    )
+    visible = seen_before()
     levels = []
     size = 1
     while size < BLOCK:
@@ -110,47 +140,26 @@
 
     def prepare(n):
         rows = slice(n * BLOCK, (n + 1) * BLOCK)
-        query = unit(proj_ref[rows, 0:width])
-        keys = jnp.concatenate(
-            [
-                unit(proj_ref[rows, width : 2 * width]),
-                unit(proj_ref[rows, 2 * width : 3 * width]),
-            ],
-            axis=0,
-        )
+        keys = keys_of(proj_ref, rows)
         values = jnp.concatenate(
             [proj_ref[rows, 3 * width : 4 * width], proj_ref[rows, 4 * width : 5 * width]], axis=0
         )
-        beta = jnp.concatenate(
-            [betas[rows, base : base + 1], betas[rows, base + 1 : base + 2]], axis=0
-        )
-        running = jnp.dot(
-            lower, log_decay[rows], precision=lax.Precision.HIGHEST, preferred_element_type=F32
-        )
-        across = jnp.transpose(running)[base + 2 : base + 3, :]
-        down = running[:, base + 2 : base + 3]
-        across = jnp.concatenate([across, across], axis=1)
-        reach = jnp.exp(jnp.where(visible, down - across, 0.0))
+        beta = jnp.concatenate([betas[rows, 0:1], betas[rows, 1:2]], axis=0)
+        running = runnings[n]
+        reach = reach_of(running, visible)
         keys_s = split(keys)
-        both = jnp.concatenate([query, keys], axis=0)
-        scores = dot3(split(both), keys_s, NT)
-        attend = jnp.where(visible, reach, 0.0) * scores[:BLOCK]
-        system = jnp.where(
-            strict, beta * jnp.concatenate([reach, reach], axis=0) * scores[BLOCK:], 0.0
-        )
+        scores = dot3(keys_s, keys_s, NT)
+        system = jnp.where(strict, beta * jnp.concatenate([reach, reach], axis=0) * scores, 0.0)
+        down = running[:, 2:3]
         grow = jnp.exp(down)
         grow2 = jnp.concatenate([grow, grow], axis=0)
-        last = running[BLOCK - 1 : BLOCK, base + 2 : base + 3]
+        last = running[BLOCK - 1 : BLOCK, 2:3]
         tail = jnp.exp(last - down)
-        tail2 = jnp.concatenate([tail, tail], axis=0)
-        right = jnp.concatenate([beta * grow2 * keys, beta * values], axis=1)
         return dict(
-            query=query * grow,
             keys=keys_s,
-            attend=attend,
             system=system,
-            right=right,
-            tail=tail2,
+            right=jnp.concatenate([beta * grow2 * keys, beta * values], axis=1),
+            tail=jnp.concatenate([tail, tail], axis=0),
             last=jnp.exp(last),
             inverse=eye - jnp.where(within, system, 0.0),
         )
@@ -162,12 +171,10 @@
             corner = split(jnp.where(level, part["system"], 0.0))
             middle = dot3(corner, inverse, ROWS)
             part["inverse"] = part["inverse"] - dot3(inverse, split(middle), ROWS)
-    for part in parts:
+    for n, part in enumerate(parts):
         solved = dot3(split(part["inverse"]), split(part["right"]), ROWS)
+        solved_ref[n] = solved
         part["step"] = dot3(split(solved * part["tail"]), part["keys"], TN)
-        seen = dot3(split(part["attend"]), split(solved), ROWS)
-        part["query"] = part["query"] - seen[:, :width]
-        part["seen"] = seen[:, width:]
     zero = jnp.zeros((width, width), F32)
 
     @pl.when(pl.program_id(0) == 0)
@@ -177,41 +184,70 @@
 
     state = held_ref[...]
     for n, part in enumerate(parts):
-        rows = slice(n * BLOCK, (n + 1) * BLOCK)
-        state_s = split(state)
-        reads = dot3(split(part["query"]), state_s, NT)
-        query_ref[rows, :] = reads[:, :width]
-        out_ref[rows, :] = reads[:, width:] + part["seen"]
+        starts_ref[n] = state
         move = part["last"] * eye - part["step"][:width]
-        state = dot3(state_s, split(move), ROWS)
+        state = dot3(split(state), split(move), ROWS)
         state = state + jnp.concatenate([zero, part["step"][width:]], axis=0)
     held_ref[...] = state
     state_ref[...] = state
 
 
+def read_kernel(swap_ref, proj_ref, row_ref, solved_ref, starts_ref, query_ref, out_ref):
+    del swap_ref
+    width = LANES
+    visible = seen_before()
+    runnings = running_decay(proj_ref[:, 5 * width :], row_ref)
+    for n, running in enumerate(runnings):
+        rows = slice(n * BLOCK, (n + 1) * BLOCK)
+        query = unit(proj_ref[rows, 0:width])
+        scores = dot3(split(query), split(keys_of(proj_ref, rows)), NT)
+        attend = jnp.where(visible, reach_of(running, visible), 0.0) * scores
+        seen = dot3(split(attend), split(solved_ref[n]), ROWS)
+        query = query * jnp.exp(running[:, 2:3]) - seen[:, :width]
+        reads = dot3(split(query), split(starts_ref[n]), NT)
+        query_ref[rows, :] = reads[:, :width]
+        out_ref[rows, :] = reads[:, width:] + seen[:, width:]
+
+
 def local_pass(swap, proj, rows):
     tokens = proj.shape[0] // 2
+    blocks = tokens // BLOCK
+    saved = jax.ShapeDtypeStruct((2 * blocks, 2 * LANES, LANES), F32)
+    wide = jax.ShapeDtypeStruct((2 * blocks, LANES, 2 * LANES), F32)
     half = jax.ShapeDtypeStruct((proj.shape[0], LANES), F32)
-    in_order = pl.BlockSpec((tokens, LANES), lambda i, swap: (i, 0))
-    return pl.pallas_call(
+    own_order = pl.BlockSpec((tokens, proj.shape[1]), lambda i, swap: (i ^ swap[0], 0))
+    table = pl.BlockSpec(rows.shape, lambda i, swap: (0, 0))
+    saved_spec = pl.BlockSpec((blocks, 2 * LANES, LANES), lambda i, swap: (i, 0, 0))
+    wide_spec = pl.BlockSpec((blocks, LANES, 2 * LANES), lambda i, swap: (i, 0, 0))
+    half_spec = pl.BlockSpec((tokens, LANES), lambda i, swap: (i, 0))
+    window, solved, starts = pl.pallas_call(
         local_kernel,
         grid_spec=pltpu.PrefetchScalarGridSpec(
             num_scalar_prefetch=1,
             grid=(2,),
-            in_specs=[
-                pl.BlockSpec((tokens, proj.shape[1]), lambda i, swap: (i ^ swap[0], 0)),
-                pl.BlockSpec(rows.shape, lambda i, swap: (0, 0)),
-            ],
+            in_specs=[own_order, table],
             out_specs=[
                 pl.BlockSpec((2 * LANES, LANES), lambda i, swap: (0, 0)),
-                in_order,
-                in_order,
+                wide_spec,
+                saved_spec,
             ],
             scratch_shapes=[pltpu.VMEM((2 * LANES, LANES), F32)],
         ),
-        out_shape=(jax.ShapeDtypeStruct((2 * LANES, LANES), F32), half, half),
+        out_shape=(jax.ShapeDtypeStruct((2 * LANES, LANES), F32), wide, saved),
         name="local",
     )(swap, proj, rows)
+    queries, partial = pl.pallas_call(
+        read_kernel,
+        grid_spec=pltpu.PrefetchScalarGridSpec(
+            num_scalar_prefetch=1,
+            grid=(2,),
+            in_specs=[own_order, table, wide_spec, saved_spec],
+            out_specs=[half_spec, half_spec],
+        ),
+        out_shape=(half, half),
+        name="reads",
+    )(swap, proj, rows, solved, starts)
+    return window, queries, partial
 
 
 def finish_kernel(state_ref, query_ref, part_ref, out_ref):
@@ -281,7 +317,7 @@
         ],
         axis=0,
     )
-    weights = at(weights, last, (z + z_size // 2) % z_size)
+    opposite = (z + z_size // 2) % z_size
     for step in range(1, columns):
         moved = permute_heads(part, lambda i, step=step: i + 2 * step)
         parts = at(parts, moved, (column - step) % columns)
@@ -292,6 +328,8 @@
     both = jnp.concatenate([tokens, partner], axis=0)
     weights = weights.reshape(depth, quad.shape[1])
     projected = jnp.dot(both, weights, preferred_element_type=F32)
+    behind = lax.dynamic_slice_in_dim(both, opposite * quad.shape[0], quad.shape[0], axis=1)
+    projected = projected + jnp.dot(behind, last, preferred_element_type=F32)
 
     bias = jnp.where(second, beta_bias[1], beta_bias[0])
     rate = jnp.where(second, decay_rate[1:], decay_rate[:1])
@@ -305,7 +343,10 @@
     window, queries, partial = local_pass(place.reshape(1), projected, rows)
     by = 1
     while 4 * by < count:
-        window = compose(shift(window, by), window)
+        before = shift(window, by)
+        if by == 1:
+            before, queries, partial = lax.optimization_barrier((before, queries, partial))
+        window = compose(before, window)
         by *= 2
     near = shift(window, 1)
     far = shift(window[LANES:], by + 1)

time: 165 us -> 162 us (0.982)
  Pallas kernels: 19.2 us -> 23.5 us
  starting transfers between devices: 72.5 us -> 68.3 us
  waiting for transfers between devices: 34.7 us -> 33 us
    pallas_call x0 -> x1, Pallas kernels: none -> 7.75 us  [local_pass(): pl.pallas_call(read_kernel, grid_spec=pltpu.PrefetchScalarGridSpec(num_sc...]
    ppermute x5, starting transfers between devices: 28.5 us -> 23.8 us  [shift(): return lax.ppermute(array, CTX, pairs)]
    ppermute x5, waiting for transfers between devices: 8.64 us -> 5.15 us  [shift(): return lax.ppermute(array, CTX, pairs)]
    pallas_call x1, Pallas kernels: 16.7 us -> 13.3 us  [local_pass(): pl.pallas_call(local_kernel, grid_spec=pltpu.PrefetchScalarGridSpec(num_s...]
    ppermute x12, waiting for transfers between devices: 14.3 us -> 16.1 us  [permute(): return lax.ppermute(array, CTX, pairs)]
  transfers between devices with their start and end apart: 23 -> 23, of which waited for: 11 -> 10; matrix products, arithmetic and copies ran while one was open for 9% -> 9% of each run, Pallas kernels for 12% -> 15%
where the time goes in v4:
time: 162 us; the launch traced here: 161 us
  starting transfers between devices  68.3 us (42%)
  waiting for transfers between devices  33 us (20%)
  Pallas kernels  23.5 us (15%)
  between operations  15.4 us (10%)
  matrix products  14 us (9%)
  local copies, waits for them, and re-layouts  5.35 us (3%)
  other arithmetic  1.86 us (1%)
    ppermute x5, starting transfers between devices, shift(): return lax.ppermute(array, CTX, pairs)  23.8 us
    ppermute x12, starting transfers between devices, permute(): return lax.ppermute(array, CTX, pairs)  19 us
    all_to_all x1, starting transfers between devices, shards(): lax.all_to_all(stacked, ('p', 'head'), split_axis=0, concat_axis=0, tiled...  18.5 us
    ppermute x12, waiting for transfers between devices, permute(): return lax.ppermute(array, CTX, pairs)  16.1 us
    pallas_call x1, Pallas kernels, local_pass(): pl.pallas_call(local_kernel, grid_spec=pltpu.PrefetchScalarGridSpec(num_s...  13.3 us
    pallas_call x1, Pallas kernels, local_pass(): pl.pallas_call(read_kernel, grid_spec=pltpu.PrefetchScalarGridSpec(num_sc...  7.75 us
    all_to_all x1, waiting for transfers between devices, shards(): lax.all_to_all(stacked, ('p', 'head'), split_axis=0, concat_axis=0, tiled...  7.2 us
    ppermute x4, starting transfers between devices, permute_heads(): lax.ppermute(array, 'head', [(i, move(i) % count) for i in range(count)])  6.91 us
  transfers between devices with their start and end apart: 23, of which 10 were waited for; matrix products, arithmetic and copies ran while one was open for 9% of the time, Pallas kernels for 15%

profile of v4, /device:TPU:1, one launch (start us, length us, event | category | flops | bytes accessed | tf_op | source)
XLA Modules:
  0.0 161.4 jit_solution(12499831292667822822)
XLA Ops:
  6.5 0.7 all-gather.2.cloned.1.call-update
  7.3 0.8 fusion.23
  8.1 0.1 copy.10
  8.2 0.1 copy.11
  8.3 0.1 pad.32.clone
  8.4 1.0 fusion.22
  9.3 0.1 broadcast_select_fusion
  9.4 2.2 %collective-permute-start.6 = (bf16[64,768]{1,0:T(8,128)(2,1)S(1)}, bf16[64,768]{1,0:T(8,128)(2,1)S(1)}, u32[]{:S(2)}, u32[]{:S(2)}) collective-permute-start(bf16[64,768]{1,0:T(8,128)(2,1)S(1)} %get-tuple-element.25), channel_id=1, source_target_pairs={{0,8},{8,0},{16,24},{24,16},{32,40},{40,32},{48,56},{56,48},{64,72... | collective-permute-start | bytes 294920 | tf_op jit(solution)/shard_map/ppermute | solution.py:52
  11.6 2.6 %collective-permute-start.7 = (bf16[64,768]{1,0:T(8,128)(2,1)S(1)}, bf16[64,768]{1,0:T(8,128)(2,1)S(1)}, u32[]{:S(2)}, u32[]{:S(2)}) collective-permute-start(bf16[64,768]{1,0:T(8,128)(2,1)S(1)} %get-tuple-element.25), channel_id=1, source_target_pairs={{0,16},{8,24},{16,0},{24,8},{32,48},{40,56},{48,32},{56,40},{64,80... | collective-permute-start | bytes 294920 | tf_op jit(solution)/shard_map/ppermute | solution.py:52
  14.2 1.0 constant_dynamic-slice_fusion
  15.2 0.1 collective-permute-start
  15.6 0.1 copy.8
  15.7 0.1 copy.9
  15.9 1.3 fusion.24
  18.4 0.1 pad_bitcast_fusion
  18.4 0.8 fusion.18
  19.3 0.6 select_maximum_fusion.row_ref
  19.9 1.2 collective-permute-done.5
  21.1 0.0 collective-permute-done.6
  21.1 1.7 %collective-permute-start.8 = (bf16[256,768]{1,0:T(8,128)(2,1)S(1)}, bf16[256,768]{1,0:T(8,128)(2,1)S(1)}, u32[]{:S(2)}, u32[]{:S(2)}) collective-permute-start(bf16[256,768]{1,0:T(8,128)(2,1)S(1)} %bitcast.76), channel_id=1, source_target_pairs={{0,32},{8,40},{16,48},{24,56},{32,64},{40,72},{48,80},{56,88},{64,... | collective-permute-start | bytes 1179656 | tf_op jit(solution)/shard_map/ppermute | solution.py:52
  22.9 4.0 %collective-permute-start.9 = (bf16[256,768]{1,0:T(8,128)(2,1)S(1)}, bf16[256,768]{1,0:T(8,128)(2,1)S(1)}, u32[]{:S(2)}, u32[]{:S(2)}) collective-permute-start(bf16[256,768]{1,0:T(8,128)(2,1)S(1)} %bitcast.77), channel_id=1, source_target_pairs={{0,224},{8,232},{16,240},{24,248},{32,0},{40,8},{48,16},{56,24},{6... | collective-permute-start | bytes 1179656 | tf_op jit(solution)/shard_map/ppermute | solution.py:52
  26.9 0.2 broadcast_in_dim.66
  27.1 0.0 collective-permute-done
  27.2 1.3 collective-permute-start.1
  28.4 2.5 %collective-permute-start.2 = (bf16[64,2048]{1,0:T(8,128)(2,1)S(1)}, bf16[64,2048]{1,0:T(8,128)(2,1)S(1)}, u32[]{:S(2)}, u32[]{:S(2)}) collective-permute-start(bf16[64,2048]{1,0:T(8,128)(2,1)S(1)} %collective-permute-done), channel_id=1, source_target_pairs={{0,4},{1,5},{2,6},{3,7},{4,0},{5,1},{6,2},{7,3},{8,12},{9,13},{10,... | collective-permute-start | bytes 786440 | tf_op jit(solution)/shard_map/ppermute | solution.py:57
  30.9 1.2 collective-permute-start.3
  32.0 0.1 broadcast_in_dim.61
  32.2 3.4 %collective-permute-done.8 = bf16[256,768]{1,0:T(8,128)(2,1)S(1)} collective-permute-done((bf16[256,768]{1,0:T(8,128)(2,1)S(1)}, bf16[256,768]{1,0:T(8,128)(2,1)S(1)}, u32[]{:S(2)}, u32[]{:S(2)}) %collective-permute-start.8) | collective-permute-done | bytes 393248 | tf_op jit(solution)/shard_map/ppermute | solution.py:52
  35.6 2.7 %collective-permute-start.11 = (bf16[256,768]{1,0:T(8,128)(2,1)S(1)}, bf16[256,768]{1,0:T(8,128)(2,1)S(1)}, u32[]{:S(2)}, u32[]{:S(2)}) collective-permute-start(bf16[256,768]{1,0:T(8,128)(2,1)S(1)} %collective-permute-done.9), channel_id=1, source_target_pairs={{0,224},{8,232},{16,240},{24,248},{32,0},{40,8},{48,16},{56,24},{6... | collective-permute-start | bytes 1179656 | tf_op jit(solution)/shard_map/ppermute | solution.py:52
  38.3 3.9 %collective-permute-done.2 = bf16[64,2048]{1,0:T(8,128)(2,1)S(1)} collective-permute-done((bf16[64,2048]{1,0:T(8,128)(2,1)S(1)}, bf16[64,2048]{1,0:T(8,128)(2,1)S(1)}, u32[]{:S(2)}, u32[]{:S(2)}) %collective-permute-start.2) | collective-permute-done | bytes 262176 | tf_op jit(solution)/shard_map/ppermute | solution.py:57
  42.2 0.0 collective-permute-done.3
  42.2 2.0 %collective-permute-start.4 = (bf16[4,64,2048]{2,1,0:T(8,128)(2,1)S(1)}, bf16[4,64,2048]{2,1,0:T(8,128)(2,1)S(1)}, u32[]{:S(2)}, u32[]{:S(2)}) collective-permute-start(bf16[4,64,2048]{2,1,0:T(8,128)(2,1)S(1)} %bitcast_dynamic-update-slice_fusion.7), channel_id=1, source_target_pairs={{0,1},{1,0},{2,3},{3,2},{4,5},{5,4},{6,7},{7,6},{8,9},{9,8},{10,11... | collective-permute-start | bytes 3145736 | tf_op jit(solution)/shard_map/ppermute | solution.py:57
  44.3 2.1 %collective-permute-done.10 = bf16[256,768]{1,0:T(8,128)(2,1)S(1)} collective-permute-done((bf16[256,768]{1,0:T(8,128)(2,1)S(1)}, bf16[256,768]{1,0:T(8,128)(2,1)S(1)}, u32[]{:S(2)}, u32[]{:S(2)}) %collective-permute-start.10) | collective-permute-done | bytes 393248 | tf_op jit(solution)/shard_map/ppermute | solution.py:52
  46.4 2.7 %collective-permute-start.13 = (bf16[256,768]{1,0:T(8,128)(2,1)S(1)}, bf16[256,768]{1,0:T(8,128)(2,1)S(1)}, u32[]{:S(2)}, u32[]{:S(2)}) collective-permute-start(bf16[256,768]{1,0:T(8,128)(2,1)S(1)} %collective-permute-done.11), channel_id=1, source_target_pairs={{0,224},{8,232},{16,240},{24,248},{32,0},{40,8},{48,16},{56,24},{6... | collective-permute-start | bytes 1179656 | tf_op jit(solution)/shard_map/ppermute | solution.py:52
  49.1 7.1 %collective-permute-done.12 = bf16[256,768]{1,0:T(8,128)(2,1)S(1)} collective-permute-done((bf16[256,768]{1,0:T(8,128)(2,1)S(1)}, bf16[256,768]{1,0:T(8,128)(2,1)S(1)}, u32[]{:S(2)}, u32[]{:S(2)}) %collective-permute-start.12) | collective-permute-done | bytes 393248 | tf_op jit(solution)/shard_map/ppermute | solution.py:52
  56.3 0.1 collective-permute-start.14
  56.4 2.9 %collective-permute-start.15 = (bf16[128,768]{1,0:T(8,128)(2,1)S(1)}, bf16[128,768]{1,0:T(8,128)(2,1)S(1)}, u32[]{:S(2)}, u32[]{:S(2)}) collective-permute-start(bf16[128,768]{1,0:T(8,128)(2,1)S(1)} %slice.73), channel_id=1, source_target_pairs={{0,224},{8,232},{16,240},{24,248},{32,0},{40,8},{48,16},{56,24},{6... | collective-permute-start | bytes 589832 | tf_op jit(solution)/shard_map/ppermute | solution.py:52
  59.4 0.1 select_bitcast_fusion.1
  59.5 0.0 copy-start
  59.5 0.2 pad_maximum_fusion.2
  59.7 2.3 %collective-permute-done.14 = bf16[128,768]{1,0:T(8,128)(2,1)S(1)} collective-permute-done((bf16[128,768]{1,0:T(8,128)(2,1)S(1)}, bf16[128,768]{1,0:T(8,128)(2,1)S(1)}, u32[]{:S(2)}, u32[]{:S(2)}) %collective-permute-start.14) | collective-permute-done | bytes 196640 | tf_op jit(solution)/shard_map/ppermute | solution.py:52
  62.1 0.6 fusion.4
  62.6 5.1 %fusion.2.proj_ref = f32[1024,768]{1,0:T(8,128)} fusion(f32[1024,768]{1,0:T(8,128)S(1)} %fusion.4, bf16[2048,768]{1,0:T(8,128)(2,1)S(1)} %bitcast.75, bf16[512,2048]{1,0:T(8,128)(2,1)S(1)} %bitcast.74, bf16[512,2048]{1,0:T(8,128)(2,1)S(1)} %copy-done), kind=kOutput, calls=%fused_computation.7 | convolution fusion | flops 3230400512 | bytes 13631488 | tf_op jit(solution)/shard_map/dot_general | solution.py:330
  67.7 13.3 %local.1 = (f32[256,128]{1,0:T(8,128)}, f32[16,128,256]{2,1,0:T(8,128)}, f32[16,256,128]{2,1,0:T(8,128)}) custom-call(s32[1]{0:T(128)} %bitcast.swap_ref, f32[1024,768]{1,0:T(8,128)} %fusion.2.proj_ref, f32[8,128]{1,0:T(8,128)} %select_maximum_fusion.row_ref), custom_call_target="tpu_custom_call" | custom-call | tf_op jit(solution)/shard_map/local/pallas_call | solution.py:223
  81.0 1.6 collective-permute-start.16
  82.6 0.0 copy-start.1
  82.7 7.7 %reads.1 = (f32[1024,128]{1,0:T(8,128)}, f32[1024,128]{1,0:T(8,128)}) custom-call(s32[1]{0:T(128)} %bitcast.swap_ref, f32[1024,768]{1,0:T(8,128)} %fusion.2.proj_ref, f32[8,128]{1,0:T(8,128)} %select_maximum_fusion.row_ref, f32[16,128,256]{2,1,0:T(8,128)} %get-tuple-element.14.solved_ref, f32[16,256,128]{2,1,0:T(8,128)} %get-tuple-element.15.starts_ref), custom_call_target="tpu_custom_call" | custom-call | tf_op jit(solution)/shard_map/reads/pallas_call | solution.py:239
  90.4 0.3 convolution_add_fusion.2
  90.7 1.3 collective-permute-start.17
  92.0 1.9 %collective-permute-done.17 = f32[256,128]{1,0:T(8,128)S(1)} collective-permute-done((f32[256,128]{1,0:T(8,128)S(1)}, f32[256,128]{1,0:T(8,128)S(1)}, u32[]{:S(2)}, u32[]{:S(2)}) %collective-permute-start.17) | collective-permute-done | bytes 131104 | tf_op jit(solution)/shard_map/ppermute | solution.py:67
  93.9 0.3 convolution_add_fusion.1
  94.2 6.7 %collective-permute-start.18 = (f32[256,128]{1,0:T(8,128)S(1)}, f32[256,128]{1,0:T(8,128)S(1)}, u32[]{:S(2)}, u32[]{:S(2)}) collective-permute-start(f32[256,128]{1,0:T(8,128)S(1)} %convolution_add_fusion.1), channel_id=1, source_target_pairs={{0,64},{24,88},{32,96},{56,120},{64,128},{88,152},{96,160},{120,18... | collective-permute-start | bytes 393224 | tf_op jit(solution)/shard_map/ppermute | solution.py:67
  100.9 1.9 %collective-permute-done.18 = f32[256,128]{1,0:T(8,128)S(1)} collective-permute-done((f32[256,128]{1,0:T(8,128)S(1)}, f32[256,128]{1,0:T(8,128)S(1)}, u32[]{:S(2)}, u32[]{:S(2)}) %collective-permute-start.18) | collective-permute-done | bytes 131104 | tf_op jit(solution)/shard_map/ppermute | solution.py:67
  102.8 0.3 convolution_add_fusion
  103.1 7.9 %collective-permute-start.20 = (f32[256,128]{1,0:T(8,128)S(1)}, f32[256,128]{1,0:T(8,128)S(1)}, u32[]{:S(2)}, u32[]{:S(2)}) collective-permute-start(f32[256,128]{1,0:T(8,128)S(1)} %convolution_add_fusion), channel_id=1, source_target_pairs={{0,24},{24,32},{32,56},{56,64},{64,88},{88,96},{96,120},{120,128},... | collective-permute-start | bytes 393224 | tf_op jit(solution)/shard_map/ppermute | solution.py:67
  110.9 6.4 %collective-permute-start.19 = (f32[128,128]{1,0:T(8,128)S(1)}, f32[128,128]{1,0:T(8,128)S(1)}, u32[]{:S(2)}, u32[]{:S(2)}) collective-permute-start(f32[128,128]{1,0:T(8,128)S(1)} %slice.76), channel_id=1, source_target_pairs={{0,152},{24,160},{32,184},{56,192},{64,216},{88,224},{96,248},{8,1... | collective-permute-start | bytes 196616 | tf_op jit(solution)/shard_map/ppermute | solution.py:67
  117.4 1.3 collective-permute-done.19
  118.7 0.8 convolution_add_fusion.3.state_ref
  119.5 2.5 %finish.1 = bf16[1024,128]{1,0:T(8,128)(2,1)} custom-call(f32[128,128]{1,0:T(8,128)} %convolution_add_fusion.3.state_ref, f32[1024,128]{1,0:T(8,128)} %get-tuple-element.19.query_ref, f32[1024,128]{1,0:T(8,128)} %get-tuple-element.20.part_ref), custom_call_target="tpu_custom_call" | custom-call | tf_op jit(solution)/shard_map/finish/pallas_call | solution.py:354
  122.0 18.5 %all-to-all-start = ((bf16[16,64,128]{2,1,0:T(8,128)(2,1)}), bf16[16,64,128]{2,1,0:T(8,128)(2,1)S(1)}, u32[]{:S(2)}, u32[]{:S(2)}) async-start(bf16[16,64,128]{2,1,0:T(8,128)(2,1)} %bitcast.80), calls=%async_computation | async-start | bytes 524288 | tf_op jit(solution)/shard_map/all_to_all | solution.py:360
  140.5 7.2 %all-to-all-done = bf16[16,64,128]{2,1,0:T(8,128)(2,1)S(1)} async-done(((bf16[16,64,128]{2,1,0:T(8,128)(2,1)}), bf16[16,64,128]{2,1,0:T(8,128)(2,1)S(1)}, u32[]{:S(2)}, u32[]{:S(2)}) %all-to-all-start) | async-done | bytes 262176 | tf_op jit(solution)/shard_map/all_to_all | solution.py:360
  147.7 0.1 reverse_select_fusion
  147.8 0.0 all-gather.2.cloned.1.call-done
  147.8 6.7 %fusion.1 = bf16[64,2048]{1,0:T(8,128)(2,1)} fusion(bf16[8,2048,256]{2,1,0:T(8,128)(2,1)} %bitcast.72, bf16[8,64,128]{2,1,0:T(8,128)(2,1)S(1)} %get-tuple-element.24, bf16[8,64,128]{2,1,0:T(8,128)(2,1)S(1)} %get-tuple-element.23), kind=kOutput, calls=%fused_computation.5 | convolution fusion | flops 537526272 | bytes 8912896 | tf_op jit(solution)/shard_map/hrk,hdk->rd/dot_general | solution.py:364
  (39 shorter events, 0.5 us)
Async XLA Ops:
  6.5 141.3 %all-gather.2.cloned.1.call-start = ((), (), s32[]{:S(2)}) async-start(), calls=%async_computation.1 | async-start | bytes 8421376 | tf_op jit(solution)/shard_map/all_gather | solution.py:283
  9.4 11.7 %collective-permute-start.6 = (bf16[64,768]{1,0:T(8,128)(2,1)S(1)}, bf16[64,768]{1,0:T(8,128)(2,1)S(1)}, u32[]{:S(2)}, u32[]{:S(2)}) collective-permute-start(bf16[64,768]{1,0:T(8,128)(2,1)S(1)} %get-tuple-element.25), channel_id=1, source_target_pairs={{0,8},{8,0},{16,24},{24,16},{32,40},{40,32},{48,56},{56,48},{64,72... | collective-permute-start | bytes 294920 | tf_op jit(solution)/shard_map/ppermute | solution.py:52
  11.6 9.5 %collective-permute-start.7 = (bf16[64,768]{1,0:T(8,128)(2,1)S(1)}, bf16[64,768]{1,0:T(8,128)(2,1)S(1)}, u32[]{:S(2)}, u32[]{:S(2)}) collective-permute-start(bf16[64,768]{1,0:T(8,128)(2,1)S(1)} %get-tuple-element.25), channel_id=1, source_target_pairs={{0,16},{8,24},{16,0},{24,8},{32,48},{40,56},{48,32},{56,40},{64,80... | collective-permute-start | bytes 294920 | tf_op jit(solution)/shard_map/ppermute | solution.py:52
  14.2 6.8 %collective-permute-start.5 = (bf16[64,768]{1,0:T(8,128)(2,1)S(1)}, bf16[64,768]{1,0:T(8,128)(2,1)S(1)}, u32[]{:S(2)}, u32[]{:S(2)}) collective-permute-start(bf16[64,768]{1,0:T(8,128)(2,1)S(1)} %get-tuple-element.26), channel_id=1, source_target_pairs={{0,24},{8,16},{16,8},{24,0},{32,56},{40,48},{48,40},{56,32},{64,88... | collective-permute-start | bytes 294920 | tf_op jit(solution)/shard_map/ppermute | solution.py:52
  15.2 11.9 %collective-permute-start = (bf16[64,2048]{1,0:T(8,128)(2,1)S(1)}, bf16[64,2048]{1,0:T(8,128)(2,1)S(1)}, u32[]{:S(2)}, u32[]{:S(2)}) collective-permute-start(bf16[64,2048]{1,0:T(8,128)(2,1)S(1)} %constant_dynamic-slice_fusion), channel_id=1, source_target_pairs={{0,8},{8,0},{16,24},{24,16},{32,40},{40,32},{48,56},{56,48},{64,72... | collective-permute-start | bytes 786440 | tf_op jit(solution)/shard_map/ppermute | solution.py:52
  21.1 14.4 %collective-permute-start.8 = (bf16[256,768]{1,0:T(8,128)(2,1)S(1)}, bf16[256,768]{1,0:T(8,128)(2,1)S(1)}, u32[]{:S(2)}, u32[]{:S(2)}) collective-permute-start(bf16[256,768]{1,0:T(8,128)(2,1)S(1)} %bitcast.76), channel_id=1, source_target_pairs={{0,32},{8,40},{16,48},{24,56},{32,64},{40,72},{48,80},{56,88},{64,... | collective-permute-start | bytes 1179656 | tf_op jit(solution)/shard_map/ppermute | solution.py:52
  22.9 12.7 %collective-permute-start.9 = (bf16[256,768]{1,0:T(8,128)(2,1)S(1)}, bf16[256,768]{1,0:T(8,128)(2,1)S(1)}, u32[]{:S(2)}, u32[]{:S(2)}) collective-permute-start(bf16[256,768]{1,0:T(8,128)(2,1)S(1)} %bitcast.77), channel_id=1, source_target_pairs={{0,224},{8,232},{16,240},{24,248},{32,0},{40,8},{48,16},{56,24},{6... | collective-permute-start | bytes 1179656 | tf_op jit(solution)/shard_map/ppermute | solution.py:52
  27.2 11.1 %collective-permute-start.1 = (bf16[64,2048]{1,0:T(8,128)(2,1)S(1)}, bf16[64,2048]{1,0:T(8,128)(2,1)S(1)}, u32[]{:S(2)}, u32[]{:S(2)}) collective-permute-start(bf16[64,2048]{1,0:T(8,128)(2,1)S(1)} %collective-permute-done), channel_id=1, source_target_pairs={{0,2},{1,3},{2,4},{3,5},{4,6},{5,7},{6,0},{7,1},{8,10},{9,11},{10,... | collective-permute-start | bytes 786440 | tf_op jit(solution)/shard_map/ppermute | solution.py:57
  28.4 13.7 %collective-permute-start.2 = (bf16[64,2048]{1,0:T(8,128)(2,1)S(1)}, bf16[64,2048]{1,0:T(8,128)(2,1)S(1)}, u32[]{:S(2)}, u32[]{:S(2)}) collective-permute-start(bf16[64,2048]{1,0:T(8,128)(2,1)S(1)} %collective-permute-done), channel_id=1, source_target_pairs={{0,4},{1,5},{2,6},{3,7},{4,0},{5,1},{6,2},{7,3},{8,12},{9,13},{10,... | collective-permute-start | bytes 786440 | tf_op jit(solution)/shard_map/ppermute | solution.py:57
  30.9 11.3 %collective-permute-start.3 = (bf16[64,2048]{1,0:T(8,128)(2,1)S(1)}, bf16[64,2048]{1,0:T(8,128)(2,1)S(1)}, u32[]{:S(2)}, u32[]{:S(2)}) collective-permute-start(bf16[64,2048]{1,0:T(8,128)(2,1)S(1)} %collective-permute-done), channel_id=1, source_target_pairs={{0,6},{1,7},{2,0},{3,1},{4,2},{5,3},{6,4},{7,5},{8,14},{9,15},{10,... | collective-permute-start | bytes 786440 | tf_op jit(solution)/shard_map/ppermute | solution.py:57
  35.6 10.8 %collective-permute-start.10 = (bf16[256,768]{1,0:T(8,128)(2,1)S(1)}, bf16[256,768]{1,0:T(8,128)(2,1)S(1)}, u32[]{:S(2)}, u32[]{:S(2)}) collective-permute-start(bf16[256,768]{1,0:T(8,128)(2,1)S(1)} %collective-permute-done.8), channel_id=1, source_target_pairs={{0,32},{8,40},{16,48},{24,56},{32,64},{40,72},{48,80},{56,88},{64,... | collective-permute-start | bytes 1179656 | tf_op jit(solution)/shard_map/ppermute | solution.py:52
  35.6 10.8 %collective-permute-start.11 = (bf16[256,768]{1,0:T(8,128)(2,1)S(1)}, bf16[256,768]{1,0:T(8,128)(2,1)S(1)}, u32[]{:S(2)}, u32[]{:S(2)}) collective-permute-start(bf16[256,768]{1,0:T(8,128)(2,1)S(1)} %collective-permute-done.9), channel_id=1, source_target_pairs={{0,224},{8,232},{16,240},{24,248},{32,0},{40,8},{48,16},{56,24},{6... | collective-permute-start | bytes 1179656 | tf_op jit(solution)/shard_map/ppermute | solution.py:52
  42.2 17.1 %collective-permute-start.4 = (bf16[4,64,2048]{2,1,0:T(8,128)(2,1)S(1)}, bf16[4,64,2048]{2,1,0:T(8,128)(2,1)S(1)}, u32[]{:S(2)}, u32[]{:S(2)}) collective-permute-start(bf16[4,64,2048]{2,1,0:T(8,128)(2,1)S(1)} %bitcast_dynamic-update-slice_fusion.7), channel_id=1, source_target_pairs={{0,1},{1,0},{2,3},{3,2},{4,5},{5,4},{6,7},{7,6},{8,9},{9,8},{10,11... | collective-permute-start | bytes 3145736 | tf_op jit(solution)/shard_map/ppermute | solution.py:57
  46.4 9.9 %collective-permute-start.12 = (bf16[256,768]{1,0:T(8,128)(2,1)S(1)}, bf16[256,768]{1,0:T(8,128)(2,1)S(1)}, u32[]{:S(2)}, u32[]{:S(2)}) collective-permute-start(bf16[256,768]{1,0:T(8,128)(2,1)S(1)} %collective-permute-done.10), channel_id=1, source_target_pairs={{0,32},{8,40},{16,48},{24,56},{32,64},{40,72},{48,80},{56,88},{64,... | collective-permute-start | bytes 1179656 | tf_op jit(solution)/shard_map/ppermute | solution.py:52
  46.4 10.0 %collective-permute-start.13 = (bf16[256,768]{1,0:T(8,128)(2,1)S(1)}, bf16[256,768]{1,0:T(8,128)(2,1)S(1)}, u32[]{:S(2)}, u32[]{:S(2)}) collective-permute-start(bf16[256,768]{1,0:T(8,128)(2,1)S(1)} %collective-permute-done.11), channel_id=1, source_target_pairs={{0,224},{8,232},{16,240},{24,248},{32,0},{40,8},{48,16},{56,24},{6... | collective-permute-start | bytes 1179656 | tf_op jit(solution)/shard_map/ppermute | solution.py:52
  56.3 5.8 %collective-permute-start.14 = (bf16[128,768]{1,0:T(8,128)(2,1)S(1)}, bf16[128,768]{1,0:T(8,128)(2,1)S(1)}, u32[]{:S(2)}, u32[]{:S(2)}) collective-permute-start(bf16[128,768]{1,0:T(8,128)(2,1)S(1)} %slice.72), channel_id=1, source_target_pairs={{0,32},{8,40},{16,48},{24,56},{32,64},{40,72},{48,80},{56,88},{64,... | collective-permute-start | bytes 589832 | tf_op jit(solution)/shard_map/ppermute | solution.py:52
  56.4 5.7 %collective-permute-start.15 = (bf16[128,768]{1,0:T(8,128)(2,1)S(1)}, bf16[128,768]{1,0:T(8,128)(2,1)S(1)}, u32[]{:S(2)}, u32[]{:S(2)}) collective-permute-start(bf16[128,768]{1,0:T(8,128)(2,1)S(1)} %slice.73), channel_id=1, source_target_pairs={{0,224},{8,232},{16,240},{24,248},{32,0},{40,8},{48,16},{56,24},{6... | collective-permute-start | bytes 589832 | tf_op jit(solution)/shard_map/ppermute | solution.py:52
  59.5 2.5 %copy-start = (bf16[512,2048]{1,0:T(8,128)(2,1)S(1)}, bf16[512,2048]{1,0:T(8,128)(2,1)}, u32[]{:S(2)}) copy-start(bf16[512,2048]{1,0:T(8,128)(2,1)} %param.6) | copy-start | bytes 6291460
  81.0 9.4 %collective-permute-start.16 = (f32[256,128]{1,0:T(8,128)}, f32[256,128]{1,0:T(8,128)S(1)}, u32[]{:S(2)}, u32[]{:S(2)}) collective-permute-start(f32[256,128]{1,0:T(8,128)} %get-tuple-element.13), channel_id=1, source_target_pairs={{0,24},{24,32},{32,56},{56,64},{64,88},{88,96},{96,120},{120,128},... | collective-permute-start | bytes 393224 | tf_op jit(solution)/shard_map/ppermute | solution.py:67
  82.6 7.8 %copy-start.1 = (f32[256,128]{1,0:T(8,128)S(1)}, f32[256,128]{1,0:T(8,128)}, u32[]{:S(2)}) copy-start(f32[256,128]{1,0:T(8,128)} %get-tuple-element.13) | copy-start | bytes 393220
  90.7 3.2 %collective-permute-start.17 = (f32[256,128]{1,0:T(8,128)S(1)}, f32[256,128]{1,0:T(8,128)S(1)}, u32[]{:S(2)}, u32[]{:S(2)}) collective-permute-start(f32[256,128]{1,0:T(8,128)S(1)} %convolution_add_fusion.2), channel_id=1, source_target_pairs={{0,32},{24,56},{32,64},{56,88},{64,96},{88,120},{96,128},{120,152}... | collective-permute-start | bytes 393224 | tf_op jit(solution)/shard_map/ppermute | solution.py:67
  94.2 8.6 %collective-permute-start.18 = (f32[256,128]{1,0:T(8,128)S(1)}, f32[256,128]{1,0:T(8,128)S(1)}, u32[]{:S(2)}, u32[]{:S(2)}) collective-permute-start(f32[256,128]{1,0:T(8,128)S(1)} %convolution_add_fusion.1), channel_id=1, source_target_pairs={{0,64},{24,88},{32,96},{56,120},{64,128},{88,152},{96,160},{120,18... | collective-permute-start | bytes 393224 | tf_op jit(solution)/shard_map/ppermute | solution.py:67
  103.1 15.6 %collective-permute-start.20 = (f32[256,128]{1,0:T(8,128)S(1)}, f32[256,128]{1,0:T(8,128)S(1)}, u32[]{:S(2)}, u32[]{:S(2)}) collective-permute-start(f32[256,128]{1,0:T(8,128)S(1)} %convolution_add_fusion), channel_id=1, source_target_pairs={{0,24},{24,32},{32,56},{56,64},{64,88},{88,96},{96,120},{120,128},... | collective-permute-start | bytes 393224 | tf_op jit(solution)/shard_map/ppermute | solution.py:67
  110.9 7.7 %collective-permute-start.19 = (f32[128,128]{1,0:T(8,128)S(1)}, f32[128,128]{1,0:T(8,128)S(1)}, u32[]{:S(2)}, u32[]{:S(2)}) collective-permute-start(f32[128,128]{1,0:T(8,128)S(1)} %slice.76), channel_id=1, source_target_pairs={{0,152},{24,160},{32,184},{56,192},{64,216},{88,224},{96,248},{8,1... | collective-permute-start | bytes 196616 | tf_op jit(solution)/shard_map/ppermute | solution.py:67
  122.0 25.7 %all-to-all-start = ((bf16[16,64,128]{2,1,0:T(8,128)(2,1)}), bf16[16,64,128]{2,1,0:T(8,128)(2,1)S(1)}, u32[]{:S(2)}, u32[]{:S(2)}) async-start(bf16[16,64,128]{2,1,0:T(8,128)(2,1)} %bitcast.80), calls=%async_computation | async-start | bytes 524288 | tf_op jit(solution)/shard_map/all_to_all | solution.py:360
Sparse Core Ops, SparseCore 0:
  11.2 124.3 all-gather.1

commit v5 on v4

--- a/solution.py
+++ b/solution.py
@@ -111,8 +111,11 @@
     )
 
 
-def local_kernel(swap_ref, proj_ref, row_ref, state_ref, solved_ref, starts_ref, held_ref):
+def local_kernel(
+    swap_ref, early_ref, late_ref, row_ref, state_ref, solved_ref, starts_ref, held_ref, proj_ref
+):
     del swap_ref
+    proj_ref[...] = early_ref[...] + late_ref[...]
     tokens = proj_ref.shape[0]
     width = LANES
     blocks = tokens // BLOCK
@@ -192,8 +195,11 @@
     state_ref[...] = state
 
 
-def read_kernel(swap_ref, proj_ref, row_ref, solved_ref, starts_ref, query_ref, out_ref):
+def read_kernel(
+    swap_ref, early_ref, late_ref, row_ref, solved_ref, starts_ref, query_ref, out_ref, proj_ref
+):
     del swap_ref
+    proj_ref[...] = early_ref[...] + late_ref[...]
     width = LANES
     visible = seen_before()
     runnings = running_decay(proj_ref[:, 5 * width :], row_ref)
@@ -209,8 +215,9 @@
         out_ref[rows, :] = reads[:, width:] + seen[:, width:]
 
 
-def local_pass(swap, proj, rows):
+def local_pass(swap, proj, late, rows):
     tokens = proj.shape[0] // 2
+    summed = pltpu.VMEM((tokens, proj.shape[1]), F32)
     blocks = tokens // BLOCK
     saved = jax.ShapeDtypeStruct((2 * blocks, 2 * LANES, LANES), F32)
     wide = jax.ShapeDtypeStruct((2 * blocks, LANES, 2 * LANES), F32)
@@ -225,35 +232,62 @@
         grid_spec=pltpu.PrefetchScalarGridSpec(
             num_scalar_prefetch=1,
             grid=(2,),
-            in_specs=[own_order, table],
+            in_specs=[own_order, own_order, table],
             out_specs=[
                 pl.BlockSpec((2 * LANES, LANES), lambda i, swap: (0, 0)),
                 wide_spec,
                 saved_spec,
             ],
-            scratch_shapes=[pltpu.VMEM((2 * LANES, LANES), F32)],
+            scratch_shapes=[pltpu.VMEM((2 * LANES, LANES), F32), summed],
         ),
         out_shape=(jax.ShapeDtypeStruct((2 * LANES, LANES), F32), wide, saved),
         name="local",
-    )(swap, proj, rows)
+    )(swap, proj, late, rows)
     queries, partial = pl.pallas_call(
         read_kernel,
         grid_spec=pltpu.PrefetchScalarGridSpec(
             num_scalar_prefetch=1,
             grid=(2,),
-            in_specs=[own_order, table, wide_spec, saved_spec],
+            in_specs=[own_order, own_order, table, wide_spec, saved_spec],
             out_specs=[half_spec, half_spec],
+            scratch_shapes=[summed],
         ),
         out_shape=(half, half),
         name="reads",
-    )(swap, proj, rows, solved, starts)
+    )(swap, proj, late, rows, solved, starts)
     return window, queries, partial
 
 
-def finish_kernel(state_ref, query_ref, part_ref, out_ref):
-    total = part_ref[...] + dot3(split(query_ref[...]), split(state_ref[...]), NT)
+def finish_kernel(far_ref, near_ref, query_ref, part_ref, out_ref):
+    near = near_ref[...]
+    state = dot3(split(far_ref[...]), split(near[:LANES]), ROWS) + near[LANES:]
+    total = part_ref[...] + dot3(split(query_ref[...]), split(state), NT)
     scale = jnp.sqrt(jnp.mean(total * total, axis=-1, keepdims=True) + 1e-06)
     out_ref[...] = (total / scale).astype(BF16)
+
+
+def mix_kernel(rows_ref, weight_ref, out_ref):
+    total = dot1(rows_ref[0], weight_ref[0], NT)
+    for group in range(1, rows_ref.shape[0]):
+        total = total + dot1(rows_ref[group], weight_ref[group], NT)
+    out_ref[...] = total.astype(BF16)
+
+
+def mix(rows, weights):
+    groups, count, depth = rows.shape
+    width = weights.shape[1]
+    block = width // 4
+    return pl.pallas_call(
+        mix_kernel,
+        grid=(width // block,),
+        in_specs=[
+            pl.BlockSpec((groups, count, depth), lambda i: (0, 0, 0)),
+            pl.BlockSpec((groups, block, depth), lambda i: (0, i, 0)),
+        ],
+        out_specs=pl.BlockSpec((count, block), lambda i: (0, i)),
+        out_shape=jax.ShapeDtypeStruct((count, width), BF16),
+        name="mix",
+    )(rows, weights)
 
 
 def compose(before, now):
@@ -329,7 +363,7 @@
     weights = weights.reshape(depth, quad.shape[1])
     projected = jnp.dot(both, weights, preferred_element_type=F32)
     behind = lax.dynamic_slice_in_dim(both, opposite * quad.shape[0], quad.shape[0], axis=1)
-    projected = projected + jnp.dot(behind, last, preferred_element_type=F32)
+    late = jnp.dot(behind, last, preferred_element_type=F32)
 
     bias = jnp.where(second, beta_bias[1], beta_bias[0])
     rate = jnp.where(second, decay_rate[1:], decay_rate[:1])
@@ -340,7 +374,7 @@
         ]
     )
     rows = jnp.pad(rows, ((0, 6), (0, 0)))
-    window, queries, partial = local_pass(place.reshape(1), projected, rows)
+    window, queries, partial = local_pass(place.reshape(1), projected, late, rows)
     by = 1
     while 4 * by < count:
         before = shift(window, by)
@@ -350,19 +384,17 @@
         by *= 2
     near = shift(window, 1)
     far = shift(window[LANES:], by + 1)
-    state_in = compose(far, near)
     normed = pl.pallas_call(
         finish_kernel,
         out_shape=jax.ShapeDtypeStruct((2 * tok_rows, LANES), BF16),
         name="finish",
-    )(state_in, queries, partial)
+    )(far, near, queries, partial)
     stacked = normed.reshape(2 * groups, rows_each, LANES)
     taken = lax.all_to_all(stacked, ("p", "head"), split_axis=0, concat_axis=0, tiled=True)
     taken = taken.reshape(2, groups, rows_each, LANES)
     taken = jnp.where(pair == 0, taken, taken[::-1])
     taken = jnp.concatenate([taken[0], taken[1]], axis=2)
-    mixed = jnp.einsum("hrk,hdk->rd", taken, flipped, preferred_element_type=F32)
-    return mixed.astype(BF16)
+    return mix(taken, flipped)
 
 
 def solution(mesh):

time: 162 us -> 167 us (1.031)
  Pallas kernels: 23.5 us -> 31.2 us
  matrix products: 14 us -> 8.09 us
  waiting for transfers between devices: 33 us -> 37.7 us
  starting transfers between devices: 68.3 us -> 65 us
    pallas_call x0 -> x1, Pallas kernels: none -> 6.28 us  [mix(): pl.pallas_call(mix_kernel, grid=(width // block,), in_specs=[pl.BlockSpec...]
    dot_general x2 -> x1, matrix products: 7.28 us -> 2.26 us  [shards(): late = jnp.dot(behind, last, preferred_element_type=F32)]
    all_to_all x1, starting transfers between devices: 18.5 us -> 15.3 us  [shards(): lax.all_to_all(stacked, ('p', 'head'), split_axis=0, concat_axis=0, tiled...]
    ppermute x5, waiting for transfers between devices: 5.15 us -> 8.04 us  [shift(): return lax.ppermute(array, CTX, pairs)]
    ppermute x12, waiting for transfers between devices: 16.1 us -> 17.9 us  [permute(): return lax.ppermute(array, CTX, pairs)]
  transfers between devices with their start and end apart: 23 -> 23, of which waited for: 10 -> 11; matrix products, arithmetic and copies ran while one was open for 9% -> 10% of each run, Pallas kernels for 15% -> 15%
where the time goes in v5:
time: 167 us
  starting transfers between devices  65 us (39%)
  waiting for transfers between devices  37.7 us (23%)
  Pallas kernels  31.2 us (19%)
  between operations  15.4 us (9%)
  matrix products  8.09 us (5%)
  local copies, waits for them, and re-layouts  6.66 us (4%)
  other arithmetic  2.62 us (2%)
    ppermute x5, starting transfers between devices, shift(): return lax.ppermute(array, CTX, pairs)  23.1 us
    ppermute x12, starting transfers between devices, permute(): return lax.ppermute(array, CTX, pairs)  19.7 us
    ppermute x12, waiting for transfers between devices, permute(): return lax.ppermute(array, CTX, pairs)  17.9 us
    all_to_all x1, starting transfers between devices, shards(): lax.all_to_all(stacked, ('p', 'head'), split_axis=0, concat_axis=0, tiled...  15.3 us
    pallas_call x1, Pallas kernels, local_pass(): pl.pallas_call(local_kernel, grid_spec=pltpu.PrefetchScalarGridSpec(num_s...  13.9 us
    pallas_call x1, Pallas kernels, local_pass(): pl.pallas_call(read_kernel, grid_spec=pltpu.PrefetchScalarGridSpec(num_sc...  8.38 us
    ppermute x5, waiting for transfers between devices, shift(): return lax.ppermute(array, CTX, pairs)  8.04 us
    all_to_all x1, waiting for transfers between devices, shards(): lax.all_to_all(stacked, ('p', 'head'), split_axis=0, concat_axis=0, tiled...  7.2 us
  transfers between devices with their start and end apart: 23, of which 11 were waited for; matrix products, arithmetic and copies ran while one was open for 10% of the time, Pallas kernels for 15%

profile of v5, /device:TPU:1, one launch (start us, length us, event | category | flops | bytes accessed | tf_op | source)
XLA Modules:
  0.0 166.6 jit_solution(5837177825532545868)
XLA Ops:
  6.5 0.7 all-gather.2.cloned.1.call-update
  7.3 0.8 fusion.16
  8.1 0.1 copy.11
  8.2 0.1 copy.10
  8.3 0.1 pad.32.clone
  8.4 1.0 fusion.15
  9.3 0.1 broadcast_select_fusion
  9.4 2.2 %collective-permute-start.6 = (bf16[64,768]{1,0:T(8,128)(2,1)S(1)}, bf16[64,768]{1,0:T(8,128)(2,1)S(1)}, u32[]{:S(2)}, u32[]{:S(2)}) collective-permute-start(bf16[64,768]{1,0:T(8,128)(2,1)S(1)} %get-tuple-element.25), channel_id=1, source_target_pairs={{0,8},{8,0},{16,24},{24,16},{32,40},{40,32},{48,56},{56,48},{64,72... | collective-permute-start | bytes 294920 | tf_op jit(solution)/shard_map/ppermute | solution.py:52
  11.6 2.6 %collective-permute-start.7 = (bf16[64,768]{1,0:T(8,128)(2,1)S(1)}, bf16[64,768]{1,0:T(8,128)(2,1)S(1)}, u32[]{:S(2)}, u32[]{:S(2)}) collective-permute-start(bf16[64,768]{1,0:T(8,128)(2,1)S(1)} %get-tuple-element.25), channel_id=1, source_target_pairs={{0,16},{8,24},{16,0},{24,8},{32,48},{40,56},{48,32},{56,40},{64,80... | collective-permute-start | bytes 294920 | tf_op jit(solution)/shard_map/ppermute | solution.py:52
  14.2 0.0 collective-permute-start.5
  14.2 1.0 constant_dynamic-slice_fusion
  15.2 0.1 collective-permute-start
  15.6 0.1 copy.8
  15.7 0.1 copy.9
  15.9 1.3 fusion.17
  18.4 0.1 pad_bitcast_fusion
  18.5 0.8 fusion.12
  19.4 0.6 select_maximum_fusion.row_ref
  20.0 1.1 collective-permute-done.5
  21.1 1.7 %collective-permute-start.8 = (bf16[256,768]{1,0:T(8,128)(2,1)S(1)}, bf16[256,768]{1,0:T(8,128)(2,1)S(1)}, u32[]{:S(2)}, u32[]{:S(2)}) collective-permute-start(bf16[256,768]{1,0:T(8,128)(2,1)S(1)} %bitcast.70), channel_id=1, source_target_pairs={{0,32},{8,40},{16,48},{24,56},{32,64},{40,72},{48,80},{56,88},{64,... | collective-permute-start | bytes 1179656 | tf_op jit(solution)/shard_map/ppermute | solution.py:52
  22.9 4.0 %collective-permute-start.9 = (bf16[256,768]{1,0:T(8,128)(2,1)S(1)}, bf16[256,768]{1,0:T(8,128)(2,1)S(1)}, u32[]{:S(2)}, u32[]{:S(2)}) collective-permute-start(bf16[256,768]{1,0:T(8,128)(2,1)S(1)} %bitcast.71), channel_id=1, source_target_pairs={{0,224},{8,232},{16,240},{24,248},{32,0},{40,8},{48,16},{56,24},{6... | collective-permute-start | bytes 1179656 | tf_op jit(solution)/shard_map/ppermute | solution.py:52
  26.9 0.2 broadcast_in_dim.65
  27.2 1.3 collective-permute-start.1
  28.4 2.5 %collective-permute-start.2 = (bf16[64,2048]{1,0:T(8,128)(2,1)S(1)}, bf16[64,2048]{1,0:T(8,128)(2,1)S(1)}, u32[]{:S(2)}, u32[]{:S(2)}) collective-permute-start(bf16[64,2048]{1,0:T(8,128)(2,1)S(1)} %collective-permute-done), channel_id=1, source_target_pairs={{0,4},{1,5},{2,6},{3,7},{4,0},{5,1},{6,2},{7,3},{8,12},{9,13},{10,... | collective-permute-start | bytes 786440 | tf_op jit(solution)/shard_map/ppermute | solution.py:57
  30.9 1.2 collective-permute-start.3
  32.0 0.1 broadcast_in_dim.60
  32.2 3.4 %collective-permute-done.8 = bf16[256,768]{1,0:T(8,128)(2,1)S(1)} collective-permute-done((bf16[256,768]{1,0:T(8,128)(2,1)S(1)}, bf16[256,768]{1,0:T(8,128)(2,1)S(1)}, u32[]{:S(2)}, u32[]{:S(2)}) %collective-permute-start.8) | collective-permute-done | bytes 393248 | tf_op jit(solution)/shard_map/ppermute | solution.py:52
  35.6 2.7 %collective-permute-start.11 = (bf16[256,768]{1,0:T(8,128)(2,1)S(1)}, bf16[256,768]{1,0:T(8,128)(2,1)S(1)}, u32[]{:S(2)}, u32[]{:S(2)}) collective-permute-start(bf16[256,768]{1,0:T(8,128)(2,1)S(1)} %collective-permute-done.9), channel_id=1, source_target_pairs={{0,224},{8,232},{16,240},{24,248},{32,0},{40,8},{48,16},{56,24},{6... | collective-permute-start | bytes 1179656 | tf_op jit(solution)/shard_map/ppermute | solution.py:52
  38.3 3.9 %collective-permute-done.2 = bf16[64,2048]{1,0:T(8,128)(2,1)S(1)} collective-permute-done((bf16[64,2048]{1,0:T(8,128)(2,1)S(1)}, bf16[64,2048]{1,0:T(8,128)(2,1)S(1)}, u32[]{:S(2)}, u32[]{:S(2)}) %collective-permute-start.2) | collective-permute-done | bytes 262176 | tf_op jit(solution)/shard_map/ppermute | solution.py:57
  42.2 2.0 %collective-permute-start.4 = (bf16[4,64,2048]{2,1,0:T(8,128)(2,1)S(1)}, bf16[4,64,2048]{2,1,0:T(8,128)(2,1)S(1)}, u32[]{:S(2)}, u32[]{:S(2)}) collective-permute-start(bf16[4,64,2048]{2,1,0:T(8,128)(2,1)S(1)} %bitcast_dynamic-update-slice_fusion.7), channel_id=1, source_target_pairs={{0,1},{1,0},{2,3},{3,2},{4,5},{5,4},{6,7},{7,6},{8,9},{9,8},{10,11... | collective-permute-start | bytes 3145736 | tf_op jit(solution)/shard_map/ppermute | solution.py:57
  44.3 2.1 %collective-permute-done.10 = bf16[256,768]{1,0:T(8,128)(2,1)S(1)} collective-permute-done((bf16[256,768]{1,0:T(8,128)(2,1)S(1)}, bf16[256,768]{1,0:T(8,128)(2,1)S(1)}, u32[]{:S(2)}, u32[]{:S(2)}) %collective-permute-start.10) | collective-permute-done | bytes 393248 | tf_op jit(solution)/shard_map/ppermute | solution.py:52
  46.4 2.7 %collective-permute-start.13 = (bf16[256,768]{1,0:T(8,128)(2,1)S(1)}, bf16[256,768]{1,0:T(8,128)(2,1)S(1)}, u32[]{:S(2)}, u32[]{:S(2)}) collective-permute-start(bf16[256,768]{1,0:T(8,128)(2,1)S(1)} %collective-permute-done.11), channel_id=1, source_target_pairs={{0,224},{8,232},{16,240},{24,248},{32,0},{40,8},{48,16},{56,24},{6... | collective-permute-start | bytes 1179656 | tf_op jit(solution)/shard_map/ppermute | solution.py:52
  49.1 6.0 %collective-permute-done.13 = bf16[256,768]{1,0:T(8,128)(2,1)S(1)} collective-permute-done((bf16[256,768]{1,0:T(8,128)(2,1)S(1)}, bf16[256,768]{1,0:T(8,128)(2,1)S(1)}, u32[]{:S(2)}, u32[]{:S(2)}) %collective-permute-start.13) | collective-permute-done | bytes 393248 | tf_op jit(solution)/shard_map/ppermute | solution.py:52
  55.2 3.4 %collective-permute-start.15 = (bf16[128,768]{1,0:T(8,128)(2,1)S(1)}, bf16[128,768]{1,0:T(8,128)(2,1)S(1)}, u32[]{:S(2)}, u32[]{:S(2)}) collective-permute-start(bf16[128,768]{1,0:T(8,128)(2,1)S(1)} %slice.65), channel_id=1, source_target_pairs={{0,224},{8,232},{16,240},{24,248},{32,0},{40,8},{48,16},{56,24},{6... | collective-permute-start | bytes 589832 | tf_op jit(solution)/shard_map/ppermute | solution.py:52
  58.6 0.3 collective-permute-start.14
  59.0 0.1 select_bitcast_fusion.1
  59.2 0.0 copy-start
  59.2 0.2 pad_maximum_fusion.2
  59.4 1.9 %collective-permute-done.15 = bf16[128,768]{1,0:T(8,128)(2,1)S(1)} collective-permute-done((bf16[128,768]{1,0:T(8,128)(2,1)S(1)}, bf16[128,768]{1,0:T(8,128)(2,1)S(1)}, u32[]{:S(2)}, u32[]{:S(2)}) %collective-permute-start.15) | collective-permute-done | bytes 196640 | tf_op jit(solution)/shard_map/ppermute | solution.py:52
  61.2 3.4 %collective-permute-done.14 = bf16[128,768]{1,0:T(8,128)(2,1)S(1)} collective-permute-done((bf16[128,768]{1,0:T(8,128)(2,1)S(1)}, bf16[128,768]{1,0:T(8,128)(2,1)S(1)}, u32[]{:S(2)}, u32[]{:S(2)}) %collective-permute-start.14) | collective-permute-done | bytes 196640 | tf_op jit(solution)/shard_map/ppermute | solution.py:52
  64.6 2.3 %fusion.2.late_ref = f32[1024,768]{1,0:T(8,128)} fusion(s32[]{:T(128)S(6)} %select_n.238, bf16[512,2048]{1,0:T(8,128)(2,1)S(1)} %copy-done, bf16[512,2048]{1,0:T(8,128)(2,1)S(1)} %bitcast.67, bf16[128,768]{1,0:T(8,128)(2,1)S(1)} %collective-permute-done.15, bf16[128,768]{1,0:T(8,128)(2,1)S(1)} %collective-permute-done.14), kind=kOutput, calls=%fused_computation.11 | convolution fusion | flops 404488192 | bytes 7733252 | tf_op jit(solution)/shard_map/dot_general | solution.py:366
  66.9 5.1 %fusion.early_ref = f32[1024,768]{1,0:T(8,128)} fusion(bf16[2048,768]{1,0:T(8,128)(2,1)S(1)} %bitcast.69, bf16[512,2048]{1,0:T(8,128)(2,1)S(1)} %bitcast.68, bf16[512,2048]{1,0:T(8,128)(2,1)S(1)} %copy-done), kind=kOutput, calls=%fused_computation.3 | convolution fusion | flops 3229614080 | bytes 10485760 | tf_op jit(solution)/shard_map/dot_general | solution.py:364
  72.0 13.9 %local.1 = (f32[256,128]{1,0:T(8,128)}, f32[16,128,256]{2,1,0:T(8,128)}, f32[16,256,128]{2,1,0:T(8,128)}) custom-call(s32[1]{0:T(128)} %bitcast.swap_ref, f32[1024,768]{1,0:T(8,128)} %fusion.early_ref, f32[1024,768]{1,0:T(8,128)} %fusion.2.late_ref, f32[8,128]{1,0:T(8,128)} %select_maximum_fusion.row_ref), custom_call_target="tpu_custom_call" | custom-call | tf_op jit(solution)/shard_map/local/pallas_call | solution.py:230
  85.9 1.5 collective-permute-start.16
  87.4 0.0 copy-start.3
  87.4 8.4 %reads.1 = (f32[1024,128]{1,0:T(8,128)}, f32[1024,128]{1,0:T(8,128)}) custom-call(s32[1]{0:T(128)} %bitcast.swap_ref, f32[1024,768]{1,0:T(8,128)} %fusion.early_ref, f32[1024,768]{1,0:T(8,128)} %fusion.2.late_ref, f32[8,128]{1,0:T(8,128)} %select_maximum_fusion.row_ref, f32[16,128,256]{2,1,0:T(8,128)} %get-tuple-element.14.solved_ref, ...), custom_call_target="tpu_custom_call" | custom-call | tf_op jit(solution)/shard_map/reads/pallas_call | solution.py:246
  95.8 0.3 convolution_add_fusion.2
  96.1 1.5 collective-permute-start.17
  97.5 1.9 %collective-permute-done.17 = f32[256,128]{1,0:T(8,128)S(1)} collective-permute-done((f32[256,128]{1,0:T(8,128)S(1)}, f32[256,128]{1,0:T(8,128)S(1)}, u32[]{:S(2)}, u32[]{:S(2)}) %collective-permute-start.17) | collective-permute-done | bytes 131104 | tf_op jit(solution)/shard_map/ppermute | solution.py:67
  99.5 0.3 convolution_add_fusion.1
  99.7 3.5 %collective-permute-start.18 = (f32[256,128]{1,0:T(8,128)S(1)}, f32[256,128]{1,0:T(8,128)S(1)}, u32[]{:S(2)}, u32[]{:S(2)}) collective-permute-start(f32[256,128]{1,0:T(8,128)S(1)} %convolution_add_fusion.1), channel_id=1, source_target_pairs={{0,64},{24,88},{32,96},{56,120},{64,128},{88,152},{96,160},{120,18... | collective-permute-start | bytes 393224 | tf_op jit(solution)/shard_map/ppermute | solution.py:67
  103.2 4.4 %collective-permute-done.18 = f32[256,128]{1,0:T(8,128)S(1)} collective-permute-done((f32[256,128]{1,0:T(8,128)S(1)}, f32[256,128]{1,0:T(8,128)S(1)}, u32[]{:S(2)}, u32[]{:S(2)}) %collective-permute-start.18) | collective-permute-done | bytes 131104 | tf_op jit(solution)/shard_map/ppermute | solution.py:67
  107.6 0.3 convolution_add_fusion
  107.9 4.8 %collective-permute-start.20 = (f32[256,128]{1,0:T(8,128)S(1)}, f32[256,128]{1,0:T(8,128)S(1)}, u32[]{:S(2)}, u32[]{:S(2)}) collective-permute-start(f32[256,128]{1,0:T(8,128)S(1)} %convolution_add_fusion), channel_id=1, source_target_pairs={{0,24},{24,32},{32,56},{56,64},{64,88},{88,96},{96,120},{120,128},... | collective-permute-start | bytes 393224 | tf_op jit(solution)/shard_map/ppermute | solution.py:67
  112.7 11.8 %collective-permute-start.19 = (f32[128,128]{1,0:T(8,128)S(1)}, f32[128,128]{1,0:T(8,128)S(1)}, u32[]{:S(2)}, u32[]{:S(2)}) collective-permute-start(f32[128,128]{1,0:T(8,128)S(1)} %slice.68), channel_id=1, source_target_pairs={{0,152},{24,160},{32,184},{56,192},{64,216},{88,224},{96,248},{8,1... | collective-permute-start | bytes 196616 | tf_op jit(solution)/shard_map/ppermute | solution.py:67
  124.5 1.7 %collective-permute-done.19.far_ref = f32[128,128]{1,0:T(8,128)S(1)} collective-permute-done((f32[128,128]{1,0:T(8,128)S(1)}, f32[128,128]{1,0:T(8,128)S(1)}, u32[]{:S(2)}, u32[]{:S(2)}) %collective-permute-start.19) | collective-permute-done | bytes 65568 | tf_op jit(solution)/shard_map/ppermute | solution.py:67
  126.3 0.6 copy-done.2
  126.9 0.6 copy-done.1
  127.5 2.7 %finish.1 = bf16[1024,128]{1,0:T(8,128)(2,1)} custom-call(f32[128,128]{1,0:T(8,128)} %copy-done.2, f32[256,128]{1,0:T(8,128)} %copy-done.1, f32[1024,128]{1,0:T(8,128)} %get-tuple-element.19.query_ref, f32[1024,128]{1,0:T(8,128)} %get-tuple-element.20.part_ref), custom_call_target="tpu_custom_call" | custom-call | tf_op jit(solution)/shard_map/finish/pallas_call | solution.py:387
  130.2 15.3 %all-to-all-start = ((bf16[16,64,128]{2,1,0:T(8,128)(2,1)}), bf16[16,64,128]{2,1,0:T(8,128)(2,1)S(1)}, u32[]{:S(2)}, u32[]{:S(2)}) async-start(bf16[16,64,128]{2,1,0:T(8,128)(2,1)} %bitcast.74), calls=%async_computation | async-start | bytes 524288 | tf_op jit(solution)/shard_map/all_to_all | solution.py:393
  145.5 7.2 %all-to-all-done = bf16[16,64,128]{2,1,0:T(8,128)(2,1)S(1)} async-done(((bf16[16,64,128]{2,1,0:T(8,128)(2,1)}), bf16[16,64,128]{2,1,0:T(8,128)(2,1)S(1)}, u32[]{:S(2)}, u32[]{:S(2)}) %all-to-all-start) | async-done | bytes 262176 | tf_op jit(solution)/shard_map/all_to_all | solution.py:393
  152.7 0.1 reverse_select_fusion
  152.8 0.8 pad_maximum_fusion.3.rows_ref
  153.5 6.3 %mix.1 = bf16[64,2048]{1,0:T(8,128)(2,1)} custom-call(bf16[8,64,256]{2,1,0:T(8,128)(2,1)} %pad_maximum_fusion.3.rows_ref, bf16[8,2048,256]{2,1,0:T(8,128)(2,1)} %bitcast.66), custom_call_target="tpu_custom_call" | custom-call | tf_op jit(solution)/shard_map/mix/pallas_call | solution.py:280
  (42 shorter events, 0.5 us)
Async XLA Ops:
  6.5 147.0 %all-gather.2.cloned.1.call-start = ((), (), s32[]{:S(2)}) async-start(), calls=%async_computation.1 | async-start | bytes 8421376 | tf_op jit(solution)/shard_map/all_gather | solution.py:317
  9.4 11.7 %collective-permute-start.6 = (bf16[64,768]{1,0:T(8,128)(2,1)S(1)}, bf16[64,768]{1,0:T(8,128)(2,1)S(1)}, u32[]{:S(2)}, u32[]{:S(2)}) collective-permute-start(bf16[64,768]{1,0:T(8,128)(2,1)S(1)} %get-tuple-element.25), channel_id=1, source_target_pairs={{0,8},{8,0},{16,24},{24,16},{32,40},{40,32},{48,56},{56,48},{64,72... | collective-permute-start | bytes 294920 | tf_op jit(solution)/shard_map/ppermute | solution.py:52
  11.6 9.5 %collective-permute-start.7 = (bf16[64,768]{1,0:T(8,128)(2,1)S(1)}, bf16[64,768]{1,0:T(8,128)(2,1)S(1)}, u32[]{:S(2)}, u32[]{:S(2)}) collective-permute-start(bf16[64,768]{1,0:T(8,128)(2,1)S(1)} %get-tuple-element.25), channel_id=1, source_target_pairs={{0,16},{8,24},{16,0},{24,8},{32,48},{40,56},{48,32},{56,40},{64,80... | collective-permute-start | bytes 294920 | tf_op jit(solution)/shard_map/ppermute | solution.py:52
  14.2 6.8 %collective-permute-start.5 = (bf16[64,768]{1,0:T(8,128)(2,1)S(1)}, bf16[64,768]{1,0:T(8,128)(2,1)S(1)}, u32[]{:S(2)}, u32[]{:S(2)}) collective-permute-start(bf16[64,768]{1,0:T(8,128)(2,1)S(1)} %get-tuple-element.26), channel_id=1, source_target_pairs={{0,24},{8,16},{16,8},{24,0},{32,56},{40,48},{48,40},{56,32},{64,88... | collective-permute-start | bytes 294920 | tf_op jit(solution)/shard_map/ppermute | solution.py:52
  15.2 11.9 %collective-permute-start = (bf16[64,2048]{1,0:T(8,128)(2,1)S(1)}, bf16[64,2048]{1,0:T(8,128)(2,1)S(1)}, u32[]{:S(2)}, u32[]{:S(2)}) collective-permute-start(bf16[64,2048]{1,0:T(8,128)(2,1)S(1)} %constant_dynamic-slice_fusion), channel_id=1, source_target_pairs={{0,8},{8,0},{16,24},{24,16},{32,40},{40,32},{48,56},{56,48},{64,72... | collective-permute-start | bytes 786440 | tf_op jit(solution)/shard_map/ppermute | solution.py:52
  21.1 14.4 %collective-permute-start.8 = (bf16[256,768]{1,0:T(8,128)(2,1)S(1)}, bf16[256,768]{1,0:T(8,128)(2,1)S(1)}, u32[]{:S(2)}, u32[]{:S(2)}) collective-permute-start(bf16[256,768]{1,0:T(8,128)(2,1)S(1)} %bitcast.70), channel_id=1, source_target_pairs={{0,32},{8,40},{16,48},{24,56},{32,64},{40,72},{48,80},{56,88},{64,... | collective-permute-start | bytes 1179656 | tf_op jit(solution)/shard_map/ppermute | solution.py:52
  22.9 12.7 %collective-permute-start.9 = (bf16[256,768]{1,0:T(8,128)(2,1)S(1)}, bf16[256,768]{1,0:T(8,128)(2,1)S(1)}, u32[]{:S(2)}, u32[]{:S(2)}) collective-permute-start(bf16[256,768]{1,0:T(8,128)(2,1)S(1)} %bitcast.71), channel_id=1, source_target_pairs={{0,224},{8,232},{16,240},{24,248},{32,0},{40,8},{48,16},{56,24},{6... | collective-permute-start | bytes 1179656 | tf_op jit(solution)/shard_map/ppermute | solution.py:52
  27.2 11.1 %collective-permute-start.1 = (bf16[64,2048]{1,0:T(8,128)(2,1)S(1)}, bf16[64,2048]{1,0:T(8,128)(2,1)S(1)}, u32[]{:S(2)}, u32[]{:S(2)}) collective-permute-start(bf16[64,2048]{1,0:T(8,128)(2,1)S(1)} %collective-permute-done), channel_id=1, source_target_pairs={{0,2},{1,3},{2,4},{3,5},{4,6},{5,7},{6,0},{7,1},{8,10},{9,11},{10,... | collective-permute-start | bytes 786440 | tf_op jit(solution)/shard_map/ppermute | solution.py:57
  28.4 13.7 %collective-permute-start.2 = (bf16[64,2048]{1,0:T(8,128)(2,1)S(1)}, bf16[64,2048]{1,0:T(8,128)(2,1)S(1)}, u32[]{:S(2)}, u32[]{:S(2)}) collective-permute-start(bf16[64,2048]{1,0:T(8,128)(2,1)S(1)} %collective-permute-done), channel_id=1, source_target_pairs={{0,4},{1,5},{2,6},{3,7},{4,0},{5,1},{6,2},{7,3},{8,12},{9,13},{10,... | collective-permute-start | bytes 786440 | tf_op jit(solution)/shard_map/ppermute | solution.py:57
  30.9 11.3 %collective-permute-start.3 = (bf16[64,2048]{1,0:T(8,128)(2,1)S(1)}, bf16[64,2048]{1,0:T(8,128)(2,1)S(1)}, u32[]{:S(2)}, u32[]{:S(2)}) collective-permute-start(bf16[64,2048]{1,0:T(8,128)(2,1)S(1)} %collective-permute-done), channel_id=1, source_target_pairs={{0,6},{1,7},{2,0},{3,1},{4,2},{5,3},{6,4},{7,5},{8,14},{9,15},{10,... | collective-permute-start | bytes 786440 | tf_op jit(solution)/shard_map/ppermute | solution.py:57
  35.6 10.8 %collective-permute-start.10 = (bf16[256,768]{1,0:T(8,128)(2,1)S(1)}, bf16[256,768]{1,0:T(8,128)(2,1)S(1)}, u32[]{:S(2)}, u32[]{:S(2)}) collective-permute-start(bf16[256,768]{1,0:T(8,128)(2,1)S(1)} %collective-permute-done.8), channel_id=1, source_target_pairs={{0,32},{8,40},{16,48},{24,56},{32,64},{40,72},{48,80},{56,88},{64,... | collective-permute-start | bytes 1179656 | tf_op jit(solution)/shard_map/ppermute | solution.py:52
  35.6 10.8 %collective-permute-start.11 = (bf16[256,768]{1,0:T(8,128)(2,1)S(1)}, bf16[256,768]{1,0:T(8,128)(2,1)S(1)}, u32[]{:S(2)}, u32[]{:S(2)}) collective-permute-start(bf16[256,768]{1,0:T(8,128)(2,1)S(1)} %collective-permute-done.9), channel_id=1, source_target_pairs={{0,224},{8,232},{16,240},{24,248},{32,0},{40,8},{48,16},{56,24},{6... | collective-permute-start | bytes 1179656 | tf_op jit(solution)/shard_map/ppermute | solution.py:52
  42.2 16.8 %collective-permute-start.4 = (bf16[4,64,2048]{2,1,0:T(8,128)(2,1)S(1)}, bf16[4,64,2048]{2,1,0:T(8,128)(2,1)S(1)}, u32[]{:S(2)}, u32[]{:S(2)}) collective-permute-start(bf16[4,64,2048]{2,1,0:T(8,128)(2,1)S(1)} %bitcast_dynamic-update-slice_fusion.7), channel_id=1, source_target_pairs={{0,1},{1,0},{2,3},{3,2},{4,5},{5,4},{6,7},{7,6},{8,9},{9,8},{10,11... | collective-permute-start | bytes 3145736 | tf_op jit(solution)/shard_map/ppermute | solution.py:57
  46.4 12.2 %collective-permute-start.12 = (bf16[256,768]{1,0:T(8,128)(2,1)S(1)}, bf16[256,768]{1,0:T(8,128)(2,1)S(1)}, u32[]{:S(2)}, u32[]{:S(2)}) collective-permute-start(bf16[256,768]{1,0:T(8,128)(2,1)S(1)} %collective-permute-done.10), channel_id=1, source_target_pairs={{0,32},{8,40},{16,48},{24,56},{32,64},{40,72},{48,80},{56,88},{64,... | collective-permute-start | bytes 1179656 | tf_op jit(solution)/shard_map/ppermute | solution.py:52
  46.4 8.8 %collective-permute-start.13 = (bf16[256,768]{1,0:T(8,128)(2,1)S(1)}, bf16[256,768]{1,0:T(8,128)(2,1)S(1)}, u32[]{:S(2)}, u32[]{:S(2)}) collective-permute-start(bf16[256,768]{1,0:T(8,128)(2,1)S(1)} %collective-permute-done.11), channel_id=1, source_target_pairs={{0,224},{8,232},{16,240},{24,248},{32,0},{40,8},{48,16},{56,24},{6... | collective-permute-start | bytes 1179656 | tf_op jit(solution)/shard_map/ppermute | solution.py:52
  55.2 6.1 %collective-permute-start.15 = (bf16[128,768]{1,0:T(8,128)(2,1)S(1)}, bf16[128,768]{1,0:T(8,128)(2,1)S(1)}, u32[]{:S(2)}, u32[]{:S(2)}) collective-permute-start(bf16[128,768]{1,0:T(8,128)(2,1)S(1)} %slice.65), channel_id=1, source_target_pairs={{0,224},{8,232},{16,240},{24,248},{32,0},{40,8},{48,16},{56,24},{6... | collective-permute-start | bytes 589832 | tf_op jit(solution)/shard_map/ppermute | solution.py:52
  58.6 6.0 %collective-permute-start.14 = (bf16[128,768]{1,0:T(8,128)(2,1)S(1)}, bf16[128,768]{1,0:T(8,128)(2,1)S(1)}, u32[]{:S(2)}, u32[]{:S(2)}) collective-permute-start(bf16[128,768]{1,0:T(8,128)(2,1)S(1)} %slice.64), channel_id=1, source_target_pairs={{0,32},{8,40},{16,48},{24,56},{32,64},{40,72},{48,80},{56,88},{64,... | collective-permute-start | bytes 589832 | tf_op jit(solution)/shard_map/ppermute | solution.py:52
  59.2 5.5 %copy-start = (bf16[512,2048]{1,0:T(8,128)(2,1)S(1)}, bf16[512,2048]{1,0:T(8,128)(2,1)}, u32[]{:S(2)}) copy-start(bf16[512,2048]{1,0:T(8,128)(2,1)} %param.6) | copy-start | bytes 6291460
  85.9 9.9 %collective-permute-start.16 = (f32[256,128]{1,0:T(8,128)}, f32[256,128]{1,0:T(8,128)S(1)}, u32[]{:S(2)}, u32[]{:S(2)}) collective-permute-start(f32[256,128]{1,0:T(8,128)} %get-tuple-element.13), channel_id=1, source_target_pairs={{0,24},{24,32},{32,56},{56,64},{64,88},{88,96},{96,120},{120,128},... | collective-permute-start | bytes 393224 | tf_op jit(solution)/shard_map/ppermute | solution.py:67
  87.4 8.4 %copy-start.3 = (f32[256,128]{1,0:T(8,128)S(1)}, f32[256,128]{1,0:T(8,128)}, u32[]{:S(2)}) copy-start(f32[256,128]{1,0:T(8,128)} %get-tuple-element.13) | copy-start | bytes 393220
  96.1 3.4 %collective-permute-start.17 = (f32[256,128]{1,0:T(8,128)S(1)}, f32[256,128]{1,0:T(8,128)S(1)}, u32[]{:S(2)}, u32[]{:S(2)}) collective-permute-start(f32[256,128]{1,0:T(8,128)S(1)} %convolution_add_fusion.2), channel_id=1, source_target_pairs={{0,32},{24,56},{32,64},{56,88},{64,96},{88,120},{96,128},{120,152}... | collective-permute-start | bytes 393224 | tf_op jit(solution)/shard_map/ppermute | solution.py:67
  99.7 7.9 %collective-permute-start.18 = (f32[256,128]{1,0:T(8,128)S(1)}, f32[256,128]{1,0:T(8,128)S(1)}, u32[]{:S(2)}, u32[]{:S(2)}) collective-permute-start(f32[256,128]{1,0:T(8,128)S(1)} %convolution_add_fusion.1), channel_id=1, source_target_pairs={{0,64},{24,88},{32,96},{56,120},{64,128},{88,152},{96,160},{120,18... | collective-permute-start | bytes 393224 | tf_op jit(solution)/shard_map/ppermute | solution.py:67
  107.9 18.4 %collective-permute-start.20 = (f32[256,128]{1,0:T(8,128)S(1)}, f32[256,128]{1,0:T(8,128)S(1)}, u32[]{:S(2)}, u32[]{:S(2)}) collective-permute-start(f32[256,128]{1,0:T(8,128)S(1)} %convolution_add_fusion), channel_id=1, source_target_pairs={{0,24},{24,32},{32,56},{56,64},{64,88},{88,96},{96,120},{120,128},... | collective-permute-start | bytes 393224 | tf_op jit(solution)/shard_map/ppermute | solution.py:67
  112.7 13.5 %collective-permute-start.19 = (f32[128,128]{1,0:T(8,128)S(1)}, f32[128,128]{1,0:T(8,128)S(1)}, u32[]{:S(2)}, u32[]{:S(2)}) collective-permute-start(f32[128,128]{1,0:T(8,128)S(1)} %slice.68), channel_id=1, source_target_pairs={{0,152},{24,160},{32,184},{56,192},{64,216},{88,224},{96,248},{8,1... | collective-permute-start | bytes 196616 | tf_op jit(solution)/shard_map/ppermute | solution.py:67
  126.3 0.6 copy-start.2
  126.9 0.6 copy-start.1
  130.2 22.5 %all-to-all-start = ((bf16[16,64,128]{2,1,0:T(8,128)(2,1)}), bf16[16,64,128]{2,1,0:T(8,128)(2,1)S(1)}, u32[]{:S(2)}, u32[]{:S(2)}) async-start(bf16[16,64,128]{2,1,0:T(8,128)(2,1)} %bitcast.74), calls=%async_computation | async-start | bytes 524288 | tf_op jit(solution)/shard_map/all_to_all | solution.py:393
Sparse Core Ops, SparseCore 0:
  11.2 123.9 all-gather.1

commit v6 on v5

--- a/solution.py
+++ b/solution.py
@@ -112,10 +112,10 @@
 
 
 def local_kernel(
-    swap_ref, early_ref, late_ref, row_ref, state_ref, solved_ref, starts_ref, held_ref, proj_ref
+    swap_ref, early_ref, behind_ref, last_ref, row_ref, state_ref, solved_ref, starts_ref, held_ref, proj_ref
 ):
     del swap_ref
-    proj_ref[...] = early_ref[...] + late_ref[...]
+    proj_ref[...] = early_ref[...] + dot1(behind_ref[...], last_ref[...], ROWS)
     tokens = proj_ref.shape[0]
     width = LANES
     blocks = tokens // BLOCK
@@ -196,10 +196,10 @@
 
 
 def read_kernel(
-    swap_ref, early_ref, late_ref, row_ref, solved_ref, starts_ref, query_ref, out_ref, proj_ref
+    swap_ref, early_ref, behind_ref, last_ref, row_ref, solved_ref, starts_ref, query_ref, out_ref, proj_ref
 ):
     del swap_ref
-    proj_ref[...] = early_ref[...] + late_ref[...]
+    proj_ref[...] = early_ref[...] + dot1(behind_ref[...], last_ref[...], ROWS)
     width = LANES
     visible = seen_before()
     runnings = running_decay(proj_ref[:, 5 * width :], row_ref)
@@ -215,7 +215,7 @@
         out_ref[rows, :] = reads[:, width:] + seen[:, width:]
 
 
-def local_pass(swap, proj, late, rows):
+def local_pass(swap, proj, behind, last, rows):
     tokens = proj.shape[0] // 2
     summed = pltpu.VMEM((tokens, proj.shape[1]), F32)
     blocks = tokens // BLOCK
@@ -223,6 +223,8 @@
     wide = jax.ShapeDtypeStruct((2 * blocks, LANES, 2 * LANES), F32)
     half = jax.ShapeDtypeStruct((proj.shape[0], LANES), F32)
     own_order = pl.BlockSpec((tokens, proj.shape[1]), lambda i, swap: (i ^ swap[0], 0))
+    own_behind = pl.BlockSpec((tokens, behind.shape[1]), lambda i, swap: (i ^ swap[0], 0))
+    whole = pl.BlockSpec(last.shape, lambda i, swap: (0, 0))
     table = pl.BlockSpec(rows.shape, lambda i, swap: (0, 0))
     saved_spec = pl.BlockSpec((blocks, 2 * LANES, LANES), lambda i, swap: (i, 0, 0))
     wide_spec = pl.BlockSpec((blocks, LANES, 2 * LANES), lambda i, swap: (i, 0, 0))
@@ -232,7 +234,7 @@
         grid_spec=pltpu.PrefetchScalarGridSpec(
             num_scalar_prefetch=1,
             grid=(2,),
-            in_specs=[own_order, own_order, table],
+            in_specs=[own_order, own_behind, whole, table],
             out_specs=[
                 pl.BlockSpec((2 * LANES, LANES), lambda i, swap: (0, 0)),
                 wide_spec,
@@ -242,19 +244,19 @@
         ),
         out_shape=(jax.ShapeDtypeStruct((2 * LANES, LANES), F32), wide, saved),
         name="local",
-    )(swap, proj, late, rows)
+    )(swap, proj, behind, last, rows)
     queries, partial = pl.pallas_call(
         read_kernel,
         grid_spec=pltpu.PrefetchScalarGridSpec(
             num_scalar_prefetch=1,
             grid=(2,),
-            in_specs=[own_order, own_order, table, wide_spec, saved_spec],
+            in_specs=[own_order, own_behind, whole, table, wide_spec, saved_spec],
             out_specs=[half_spec, half_spec],
             scratch_shapes=[summed],
         ),
         out_shape=(half, half),
         name="reads",
-    )(swap, proj, late, rows, solved, starts)
+    )(swap, proj, behind, last, rows, solved, starts)
     return window, queries, partial
 
 
@@ -343,6 +345,11 @@
         down = permute(down, lambda z, y: (z - 1, y))
         weights = at(weights, up, (z - step) % z_size)
         weights = at(weights, down, (z + step) % z_size)
+    for step in range(1, columns):
+        moved = permute_heads(part, lambda i, step=step: i + 2 * step)
+        parts = at(parts, moved, (column - step) % columns)
+    theirs = permute_heads(parts, lambda i: i ^ 1)
+    up, down, theirs = lax.optimization_barrier((up, down, theirs))
     middle = quad.shape[0] // 2
     last = jnp.concatenate(
         [
@@ -352,10 +359,6 @@
         axis=0,
     )
     opposite = (z + z_size // 2) % z_size
-    for step in range(1, columns):
-        moved = permute_heads(part, lambda i, step=step: i + 2 * step)
-        parts = at(parts, moved, (column - step) % columns)
-    theirs = permute_heads(parts, lambda i: i ^ 1)
     even = jnp.where(core == 0, parts, theirs)
     odd = jnp.where(core == 0, theirs, parts)
     partner = jnp.stack([even, odd], axis=1).reshape(tok_rows, depth)
@@ -363,7 +366,6 @@
     weights = weights.reshape(depth, quad.shape[1])
     projected = jnp.dot(both, weights, preferred_element_type=F32)
     behind = lax.dynamic_slice_in_dim(both, opposite * quad.shape[0], quad.shape[0], axis=1)
-    late = jnp.dot(behind, last, preferred_element_type=F32)
 
     bias = jnp.where(second, beta_bias[1], beta_bias[0])
     rate = jnp.where(second, decay_rate[1:], decay_rate[:1])
@@ -374,7 +376,7 @@
         ]
     )
     rows = jnp.pad(rows, ((0, 6), (0, 0)))
-    window, queries, partial = local_pass(place.reshape(1), projected, late, rows)
+    window, queries, partial = local_pass(place.reshape(1), projected, behind, last, rows)
     by = 1
     while 4 * by < count:
         before = shift(window, by)

time: 167 us -> 160 us (0.958)
  waiting for transfers between devices: 37.7 us -> 31.3 us
  matrix products: 8.09 us -> 5.82 us
  local copies, waits for them, and re-layouts: 6.66 us -> 8.9 us
  starting transfers between devices: 65 us -> 62.8 us
    ppermute x12, waiting for transfers between devices: 17.9 us -> 13.5 us  [permute(): return lax.ppermute(array, CTX, pairs)]
    all_to_all x1, starting transfers between devices: 15.3 us -> 12.1 us  [shards(): lax.all_to_all(stacked, ('p', 'head'), split_axis=0, concat_axis=0, tiled...]
    dot_general x1 -> x0, matrix products: 2.26 us -> none  [shards(): late = jnp.dot(behind, last, preferred_element_type=F32)]
    unnamed x8 -> x11, local copies, waits for them, and re-layouts: 1.28 us -> 3.45 us
    ppermute x5, waiting for transfers between devices: 8.04 us -> 5.96 us  [shift(): return lax.ppermute(array, CTX, pairs)]
  transfers between devices with their start and end apart: 23 -> 23, of which waited for: 11 -> 9; matrix products, arithmetic and copies ran while one was open for 10% -> 9% of each run, Pallas kernels for 15% -> 16%
where the time goes in v6:
time: 160 us; the launch traced here: 159 us
  starting transfers between devices  62.8 us (39%)
  Pallas kernels  31.7 us (20%)
  waiting for transfers between devices  31.3 us (20%)
  between operations  15.5 us (10%)
  local copies, waits for them, and re-layouts  8.9 us (6%)
  matrix products  5.82 us (4%)
  other arithmetic  3.48 us (2%)
    ppermute x5, starting transfers between devices, shift(): return lax.ppermute(array, CTX, pairs)  24.8 us
    ppermute x12, starting transfers between devices, permute(): return lax.ppermute(array, CTX, pairs)  19 us
    pallas_call x1, Pallas kernels, local_pass(): pl.pallas_call(local_kernel, grid_spec=pltpu.PrefetchScalarGridSpec(num_s...  14 us
    ppermute x12, waiting for transfers between devices, permute(): return lax.ppermute(array, CTX, pairs)  13.5 us
    all_to_all x1, starting transfers between devices, shards(): lax.all_to_all(stacked, ('p', 'head'), split_axis=0, concat_axis=0, tiled...  12.1 us
    pallas_call x1, Pallas kernels, local_pass(): pl.pallas_call(read_kernel, grid_spec=pltpu.PrefetchScalarGridSpec(num_sc...  8.82 us
    all_to_all x1, waiting for transfers between devices, shards(): lax.all_to_all(stacked, ('p', 'head'), split_axis=0, concat_axis=0, tiled...  7.2 us
    ppermute x4, starting transfers between devices, permute_heads(): lax.ppermute(array, 'head', [(i, move(i) % count) for i in range(count)])  6.9 us
  transfers between devices with their start and end apart: 23, of which 9 were waited for; matrix products, arithmetic and copies ran while one was open for 9% of the time, Pallas kernels for 16%

profile of v6, /device:TPU:1, one launch (start us, length us, event | category | flops | bytes accessed | tf_op | source)
XLA Modules:
  0.0 159.5 jit_solution(11432463986263242529)
XLA Ops:
  6.5 0.7 all-gather.2.cloned.1.call-update
  7.3 0.8 fusion.9
  8.1 0.1 copy.10
  8.2 0.1 copy.9
  8.3 0.1 pad.34.clone
  8.4 1.0 fusion.8
  9.3 0.1 broadcast_select_fusion
  9.4 2.2 %collective-permute-start.5 = (bf16[64,768]{1,0:T(8,128)(2,1)S(1)}, bf16[64,768]{1,0:T(8,128)(2,1)S(1)}, u32[]{:S(2)}, u32[]{:S(2)}) collective-permute-start(bf16[64,768]{1,0:T(8,128)(2,1)S(1)} %get-tuple-element.31), channel_id=1, source_target_pairs={{0,8},{8,0},{16,24},{24,16},{32,40},{40,32},{48,56},{56,48},{64,72... | collective-permute-start | bytes 294920 | tf_op jit(solution)/shard_map/ppermute | solution.py:52
  11.6 2.6 %collective-permute-start.6 = (bf16[64,768]{1,0:T(8,128)(2,1)S(1)}, bf16[64,768]{1,0:T(8,128)(2,1)S(1)}, u32[]{:S(2)}, u32[]{:S(2)}) collective-permute-start(bf16[64,768]{1,0:T(8,128)(2,1)S(1)} %get-tuple-element.31), channel_id=1, source_target_pairs={{0,16},{8,24},{16,0},{24,8},{32,48},{40,56},{48,32},{56,40},{64,80... | collective-permute-start | bytes 294920 | tf_op jit(solution)/shard_map/ppermute | solution.py:52
  14.2 1.0 constant_dynamic-slice_fusion
  15.2 0.1 collective-permute-start
  15.6 0.1 copy.7
  15.7 0.1 copy.8
  15.9 1.4 fusion.10
  18.6 0.1 pad_bitcast_fusion
  18.7 0.8 fusion.6
  19.5 0.6 select_maximum_fusion.row_ref
  20.1 0.9 collective-permute-done.4
  21.1 0.0 collective-permute-done.5
  21.1 1.7 %collective-permute-start.7 = (bf16[256,768]{1,0:T(8,128)(2,1)S(1)}, bf16[256,768]{1,0:T(8,128)(2,1)S(1)}, u32[]{:S(2)}, u32[]{:S(2)}) collective-permute-start(bf16[256,768]{1,0:T(8,128)(2,1)S(1)} %bitcast.70), channel_id=1, source_target_pairs={{0,32},{8,40},{16,48},{24,56},{32,64},{40,72},{48,80},{56,88},{64,... | collective-permute-start | bytes 1179656 | tf_op jit(solution)/shard_map/ppermute | solution.py:52
  22.9 4.0 %collective-permute-start.10 = (bf16[256,768]{1,0:T(8,128)(2,1)S(1)}, bf16[256,768]{1,0:T(8,128)(2,1)S(1)}, u32[]{:S(2)}, u32[]{:S(2)}) collective-permute-start(bf16[256,768]{1,0:T(8,128)(2,1)S(1)} %bitcast.71), channel_id=1, source_target_pairs={{0,224},{8,232},{16,240},{24,248},{32,0},{40,8},{48,16},{56,24},{6... | collective-permute-start | bytes 1179656 | tf_op jit(solution)/shard_map/ppermute | solution.py:52
  26.9 0.2 broadcast_in_dim.71
  27.2 1.3 collective-permute-start.1
  28.4 2.5 %collective-permute-start.2 = (bf16[64,2048]{1,0:T(8,128)(2,1)S(1)}, bf16[64,2048]{1,0:T(8,128)(2,1)S(1)}, u32[]{:S(2)}, u32[]{:S(2)}) collective-permute-start(bf16[64,2048]{1,0:T(8,128)(2,1)S(1)} %collective-permute-done), channel_id=1, source_target_pairs={{0,4},{1,5},{2,6},{3,7},{4,0},{5,1},{6,2},{7,3},{8,12},{9,13},{10,... | collective-permute-start | bytes 786440 | tf_op jit(solution)/shard_map/ppermute | solution.py:57
  30.9 1.2 collective-permute-start.3
  32.0 0.1 broadcast_in_dim.60
  32.2 3.4 %collective-permute-done.7 = bf16[256,768]{1,0:T(8,128)(2,1)S(1)} collective-permute-done((bf16[256,768]{1,0:T(8,128)(2,1)S(1)}, bf16[256,768]{1,0:T(8,128)(2,1)S(1)}, u32[]{:S(2)}, u32[]{:S(2)}) %collective-permute-start.7) | collective-permute-done | bytes 393248 | tf_op jit(solution)/shard_map/ppermute | solution.py:52
  35.6 2.7 %collective-permute-start.11 = (bf16[256,768]{1,0:T(8,128)(2,1)S(1)}, bf16[256,768]{1,0:T(8,128)(2,1)S(1)}, u32[]{:S(2)}, u32[]{:S(2)}) collective-permute-start(bf16[256,768]{1,0:T(8,128)(2,1)S(1)} %collective-permute-done.10), channel_id=1, source_target_pairs={{0,224},{8,232},{16,240},{24,248},{32,0},{40,8},{48,16},{56,24},{6... | collective-permute-start | bytes 1179656 | tf_op jit(solution)/shard_map/ppermute | solution.py:52
  38.3 3.9 %collective-permute-done.2 = bf16[64,2048]{1,0:T(8,128)(2,1)S(1)} collective-permute-done((bf16[64,2048]{1,0:T(8,128)(2,1)S(1)}, bf16[64,2048]{1,0:T(8,128)(2,1)S(1)}, u32[]{:S(2)}, u32[]{:S(2)}) %collective-permute-start.2) | collective-permute-done | bytes 262176 | tf_op jit(solution)/shard_map/ppermute | solution.py:57
  42.2 2.0 %collective-permute-start.13 = (bf16[4,64,2048]{2,1,0:T(8,128)(2,1)S(1)}, bf16[4,64,2048]{2,1,0:T(8,128)(2,1)S(1)}, u32[]{:S(2)}, u32[]{:S(2)}) collective-permute-start(bf16[4,64,2048]{2,1,0:T(8,128)(2,1)S(1)} %bitcast_dynamic-update-slice_fusion.7), channel_id=1, source_target_pairs={{0,1},{1,0},{2,3},{3,2},{4,5},{5,4},{6,7},{7,6},{8,9},{9,8},{10,11... | collective-permute-start | bytes 3145736 | tf_op jit(solution)/shard_map/ppermute | solution.py:57
  44.3 2.1 %collective-permute-done.8 = bf16[256,768]{1,0:T(8,128)(2,1)S(1)} collective-permute-done((bf16[256,768]{1,0:T(8,128)(2,1)S(1)}, bf16[256,768]{1,0:T(8,128)(2,1)S(1)}, u32[]{:S(2)}, u32[]{:S(2)}) %collective-permute-start.8) | collective-permute-done | bytes 393248 | tf_op jit(solution)/shard_map/ppermute | solution.py:52
  46.4 2.7 %collective-permute-start.12 = (bf16[256,768]{1,0:T(8,128)(2,1)S(1)}, bf16[256,768]{1,0:T(8,128)(2,1)S(1)}, u32[]{:S(2)}, u32[]{:S(2)}) collective-permute-start(bf16[256,768]{1,0:T(8,128)(2,1)S(1)} %collective-permute-done.11), channel_id=1, source_target_pairs={{0,224},{8,232},{16,240},{24,248},{32,0},{40,8},{48,16},{56,24},{6... | collective-permute-start | bytes 1179656 | tf_op jit(solution)/shard_map/ppermute | solution.py:52
  49.1 7.1 %collective-permute-done.9 = bf16[256,768]{1,0:T(8,128)(2,1)S(1)} collective-permute-done((bf16[256,768]{1,0:T(8,128)(2,1)S(1)}, bf16[256,768]{1,0:T(8,128)(2,1)S(1)}, u32[]{:S(2)}, u32[]{:S(2)}) %collective-permute-start.9) | collective-permute-done | bytes 393248 | tf_op jit(solution)/shard_map/ppermute | solution.py:52
  56.4 0.1 collective-permute-start.14
  56.5 2.9 %collective-permute-start.15 = (bf16[128,768]{1,0:T(8,128)(2,1)S(1)}, bf16[128,768]{1,0:T(8,128)(2,1)S(1)}, u32[]{:S(2)}, u32[]{:S(2)}) collective-permute-start(bf16[128,768]{1,0:T(8,128)(2,1)S(1)} %slice.53), channel_id=1, source_target_pairs={{0,224},{8,232},{16,240},{24,248},{32,0},{40,8},{48,16},{56,24},{6... | collective-permute-start | bytes 589832 | tf_op jit(solution)/shard_map/ppermute | solution.py:52
  59.4 0.1 select_bitcast_fusion.1
  59.5 0.0 copy-start
  59.5 0.2 pad_maximum_fusion.2
  59.7 1.4 copy-done
  61.1 5.1 %fusion.early_ref = f32[1024,768]{1,0:T(8,128)} fusion(bf16[2048,768]{1,0:T(8,128)(2,1)S(1)} %bitcast.69, bf16[512,2048]{1,0:T(8,128)(2,1)S(1)} %bitcast.66, bf16[512,2048]{1,0:T(8,128)(2,1)S(1)} %copy-done), kind=kOutput, calls=%fused_computation.3 | convolution fusion | flops 3229614080 | bytes 10485760 | tf_op jit(solution)/shard_map/dot_general | solution.py:367
  66.2 0.9 fusion.1.behind_ref
  67.1 0.8 copy-done.1
  67.9 14.0 %local.1 = (f32[256,128]{1,0:T(8,128)}, f32[16,128,256]{2,1,0:T(8,128)}, f32[16,256,128]{2,1,0:T(8,128)}) custom-call(s32[1]{0:T(128)} %bitcast.swap_ref, f32[1024,768]{1,0:T(8,128)} %fusion.early_ref, bf16[1024,256]{1,0:T(8,128)(2,1)} %fusion.1.behind_ref, bf16[256,768]{1,0:T(8,128)(2,1)} %copy-done.1, f32[8,128]{1,0:T(8,128)} %select_maximum_fusion.row_ref), custom_call_target="tpu_custom_call" | custom-call | tf_op jit(solution)/shard_map/local/pallas_call | solution.py:232
  81.8 1.5 collective-permute-start.16
  83.3 0.0 copy-start.4
  83.4 8.8 %reads.1 = (f32[1024,128]{1,0:T(8,128)}, f32[1024,128]{1,0:T(8,128)}) custom-call(s32[1]{0:T(128)} %bitcast.swap_ref, f32[1024,768]{1,0:T(8,128)} %fusion.early_ref, bf16[1024,256]{1,0:T(8,128)(2,1)} %fusion.1.behind_ref, bf16[256,768]{1,0:T(8,128)(2,1)} %copy-done.1, f32[8,128]{1,0:T(8,128)} %select_maximum_fusion.row_ref, ...), custom_call_target="tpu_custom_call" | custom-call | tf_op jit(solution)/shard_map/reads/pallas_call | solution.py:248
  92.2 0.3 convolution_add_fusion.2
  92.5 1.3 collective-permute-start.17
  93.8 1.9 %collective-permute-done.17 = f32[256,128]{1,0:T(8,128)S(1)} collective-permute-done((f32[256,128]{1,0:T(8,128)S(1)}, f32[256,128]{1,0:T(8,128)S(1)}, u32[]{:S(2)}, u32[]{:S(2)}) %collective-permute-start.17) | collective-permute-done | bytes 131104 | tf_op jit(solution)/shard_map/ppermute | solution.py:67
  95.7 0.3 convolution_add_fusion.1
  96.0 5.4 %collective-permute-start.18 = (f32[256,128]{1,0:T(8,128)S(1)}, f32[256,128]{1,0:T(8,128)S(1)}, u32[]{:S(2)}, u32[]{:S(2)}) collective-permute-start(f32[256,128]{1,0:T(8,128)S(1)} %convolution_add_fusion.1), channel_id=1, source_target_pairs={{0,64},{24,88},{32,96},{56,120},{64,128},{88,152},{96,160},{120,18... | collective-permute-start | bytes 393224 | tf_op jit(solution)/shard_map/ppermute | solution.py:67
  101.3 2.4 %collective-permute-done.18 = f32[256,128]{1,0:T(8,128)S(1)} collective-permute-done((f32[256,128]{1,0:T(8,128)S(1)}, f32[256,128]{1,0:T(8,128)S(1)}, u32[]{:S(2)}, u32[]{:S(2)}) %collective-permute-start.18) | collective-permute-done | bytes 131104 | tf_op jit(solution)/shard_map/ppermute | solution.py:67
  103.7 0.3 convolution_add_fusion
  104.0 6.9 %collective-permute-start.20 = (f32[256,128]{1,0:T(8,128)S(1)}, f32[256,128]{1,0:T(8,128)S(1)}, u32[]{:S(2)}, u32[]{:S(2)}) collective-permute-start(f32[256,128]{1,0:T(8,128)S(1)} %convolution_add_fusion), channel_id=1, source_target_pairs={{0,24},{24,32},{32,56},{56,64},{64,88},{88,96},{96,120},{120,128},... | collective-permute-start | bytes 393224 | tf_op jit(solution)/shard_map/ppermute | solution.py:67
  110.9 9.7 %collective-permute-start.19 = (f32[128,128]{1,0:T(8,128)S(1)}, f32[128,128]{1,0:T(8,128)S(1)}, u32[]{:S(2)}, u32[]{:S(2)}) collective-permute-start(f32[128,128]{1,0:T(8,128)S(1)} %slice.66), channel_id=1, source_target_pairs={{0,152},{24,160},{32,184},{56,192},{64,216},{88,224},{96,248},{8,1... | collective-permute-start | bytes 196616 | tf_op jit(solution)/shard_map/ppermute | solution.py:67
  120.6 1.6 %collective-permute-done.19.far_ref = f32[128,128]{1,0:T(8,128)S(1)} collective-permute-done((f32[128,128]{1,0:T(8,128)S(1)}, f32[128,128]{1,0:T(8,128)S(1)}, u32[]{:S(2)}, u32[]{:S(2)}) %collective-permute-start.19) | collective-permute-done | bytes 65568 | tf_op jit(solution)/shard_map/ppermute | solution.py:67
  122.3 0.6 copy-done.3
  122.9 0.7 copy-done.2
  123.5 2.7 %finish.1 = bf16[1024,128]{1,0:T(8,128)(2,1)} custom-call(f32[128,128]{1,0:T(8,128)} %copy-done.3, f32[256,128]{1,0:T(8,128)} %copy-done.2, f32[1024,128]{1,0:T(8,128)} %get-tuple-element.25.query_ref, f32[1024,128]{1,0:T(8,128)} %get-tuple-element.26.part_ref), custom_call_target="tpu_custom_call" | custom-call | tf_op jit(solution)/shard_map/finish/pallas_call | solution.py:389
  126.2 12.1 %all-to-all-start = ((bf16[16,64,128]{2,1,0:T(8,128)(2,1)}), bf16[16,64,128]{2,1,0:T(8,128)(2,1)S(1)}, u32[]{:S(2)}, u32[]{:S(2)}) async-start(bf16[16,64,128]{2,1,0:T(8,128)(2,1)} %bitcast.74), calls=%async_computation | async-start | bytes 524288 | tf_op jit(solution)/shard_map/all_to_all | solution.py:395
  138.3 7.2 %all-to-all-done = bf16[16,64,128]{2,1,0:T(8,128)(2,1)S(1)} async-done(((bf16[16,64,128]{2,1,0:T(8,128)(2,1)}), bf16[16,64,128]{2,1,0:T(8,128)(2,1)S(1)}, u32[]{:S(2)}, u32[]{:S(2)}) %all-to-all-start) | async-done | bytes 262176 | tf_op jit(solution)/shard_map/all_to_all | solution.py:395
  145.5 0.1 reverse_select_fusion
  145.6 0.8 pad_maximum_fusion.3.rows_ref
  146.4 6.3 %mix.1 = bf16[64,2048]{1,0:T(8,128)(2,1)} custom-call(bf16[8,64,256]{2,1,0:T(8,128)(2,1)} %pad_maximum_fusion.3.rows_ref, bf16[8,2048,256]{2,1,0:T(8,128)(2,1)} %bitcast.68), custom_call_target="tpu_custom_call" | custom-call | tf_op jit(solution)/shard_map/mix/pallas_call | solution.py:282
  (46 shorter events, 0.6 us)
Async XLA Ops:
  6.5 139.8 %all-gather.2.cloned.1.call-start = ((), (), s32[]{:S(2)}) async-start(), calls=%async_computation.1 | async-start | bytes 8421376 | tf_op jit(solution)/shard_map/all_gather | solution.py:319
  9.4 11.7 %collective-permute-start.5 = (bf16[64,768]{1,0:T(8,128)(2,1)S(1)}, bf16[64,768]{1,0:T(8,128)(2,1)S(1)}, u32[]{:S(2)}, u32[]{:S(2)}) collective-permute-start(bf16[64,768]{1,0:T(8,128)(2,1)S(1)} %get-tuple-element.31), channel_id=1, source_target_pairs={{0,8},{8,0},{16,24},{24,16},{32,40},{40,32},{48,56},{56,48},{64,72... | collective-permute-start | bytes 294920 | tf_op jit(solution)/shard_map/ppermute | solution.py:52
  11.6 9.5 %collective-permute-start.6 = (bf16[64,768]{1,0:T(8,128)(2,1)S(1)}, bf16[64,768]{1,0:T(8,128)(2,1)S(1)}, u32[]{:S(2)}, u32[]{:S(2)}) collective-permute-start(bf16[64,768]{1,0:T(8,128)(2,1)S(1)} %get-tuple-element.31), channel_id=1, source_target_pairs={{0,16},{8,24},{16,0},{24,8},{32,48},{40,56},{48,32},{56,40},{64,80... | collective-permute-start | bytes 294920 | tf_op jit(solution)/shard_map/ppermute | solution.py:52
  14.2 6.8 %collective-permute-start.4 = (bf16[64,768]{1,0:T(8,128)(2,1)S(1)}, bf16[64,768]{1,0:T(8,128)(2,1)S(1)}, u32[]{:S(2)}, u32[]{:S(2)}) collective-permute-start(bf16[64,768]{1,0:T(8,128)(2,1)S(1)} %get-tuple-element.32), channel_id=1, source_target_pairs={{0,24},{8,16},{16,8},{24,0},{32,56},{40,48},{48,40},{56,32},{64,88... | collective-permute-start | bytes 294920 | tf_op jit(solution)/shard_map/ppermute | solution.py:52
  15.2 11.9 %collective-permute-start = (bf16[64,2048]{1,0:T(8,128)(2,1)S(1)}, bf16[64,2048]{1,0:T(8,128)(2,1)S(1)}, u32[]{:S(2)}, u32[]{:S(2)}) collective-permute-start(bf16[64,2048]{1,0:T(8,128)(2,1)S(1)} %constant_dynamic-slice_fusion), channel_id=1, source_target_pairs={{0,8},{8,0},{16,24},{24,16},{32,40},{40,32},{48,56},{56,48},{64,72... | collective-permute-start | bytes 786440 | tf_op jit(solution)/shard_map/ppermute | solution.py:52
  21.1 14.4 %collective-permute-start.7 = (bf16[256,768]{1,0:T(8,128)(2,1)S(1)}, bf16[256,768]{1,0:T(8,128)(2,1)S(1)}, u32[]{:S(2)}, u32[]{:S(2)}) collective-permute-start(bf16[256,768]{1,0:T(8,128)(2,1)S(1)} %bitcast.70), channel_id=1, source_target_pairs={{0,32},{8,40},{16,48},{24,56},{32,64},{40,72},{48,80},{56,88},{64,... | collective-permute-start | bytes 1179656 | tf_op jit(solution)/shard_map/ppermute | solution.py:52
  22.9 12.7 %collective-permute-start.10 = (bf16[256,768]{1,0:T(8,128)(2,1)S(1)}, bf16[256,768]{1,0:T(8,128)(2,1)S(1)}, u32[]{:S(2)}, u32[]{:S(2)}) collective-permute-start(bf16[256,768]{1,0:T(8,128)(2,1)S(1)} %bitcast.71), channel_id=1, source_target_pairs={{0,224},{8,232},{16,240},{24,248},{32,0},{40,8},{48,16},{56,24},{6... | collective-permute-start | bytes 1179656 | tf_op jit(solution)/shard_map/ppermute | solution.py:52
  27.2 11.1 %collective-permute-start.1 = (bf16[64,2048]{1,0:T(8,128)(2,1)S(1)}, bf16[64,2048]{1,0:T(8,128)(2,1)S(1)}, u32[]{:S(2)}, u32[]{:S(2)}) collective-permute-start(bf16[64,2048]{1,0:T(8,128)(2,1)S(1)} %collective-permute-done), channel_id=1, source_target_pairs={{0,2},{1,3},{2,4},{3,5},{4,6},{5,7},{6,0},{7,1},{8,10},{9,11},{10,... | collective-permute-start | bytes 786440 | tf_op jit(solution)/shard_map/ppermute | solution.py:57
  28.4 13.7 %collective-permute-start.2 = (bf16[64,2048]{1,0:T(8,128)(2,1)S(1)}, bf16[64,2048]{1,0:T(8,128)(2,1)S(1)}, u32[]{:S(2)}, u32[]{:S(2)}) collective-permute-start(bf16[64,2048]{1,0:T(8,128)(2,1)S(1)} %collective-permute-done), channel_id=1, source_target_pairs={{0,4},{1,5},{2,6},{3,7},{4,0},{5,1},{6,2},{7,3},{8,12},{9,13},{10,... | collective-permute-start | bytes 786440 | tf_op jit(solution)/shard_map/ppermute | solution.py:57
  30.9 11.3 %collective-permute-start.3 = (bf16[64,2048]{1,0:T(8,128)(2,1)S(1)}, bf16[64,2048]{1,0:T(8,128)(2,1)S(1)}, u32[]{:S(2)}, u32[]{:S(2)}) collective-permute-start(bf16[64,2048]{1,0:T(8,128)(2,1)S(1)} %collective-permute-done), channel_id=1, source_target_pairs={{0,6},{1,7},{2,0},{3,1},{4,2},{5,3},{6,4},{7,5},{8,14},{9,15},{10,... | collective-permute-start | bytes 786440 | tf_op jit(solution)/shard_map/ppermute | solution.py:57
  35.6 10.8 %collective-permute-start.8 = (bf16[256,768]{1,0:T(8,128)(2,1)S(1)}, bf16[256,768]{1,0:T(8,128)(2,1)S(1)}, u32[]{:S(2)}, u32[]{:S(2)}) collective-permute-start(bf16[256,768]{1,0:T(8,128)(2,1)S(1)} %collective-permute-done.7), channel_id=1, source_target_pairs={{0,32},{8,40},{16,48},{24,56},{32,64},{40,72},{48,80},{56,88},{64,... | collective-permute-start | bytes 1179656 | tf_op jit(solution)/shard_map/ppermute | solution.py:52
  35.6 10.8 %collective-permute-start.11 = (bf16[256,768]{1,0:T(8,128)(2,1)S(1)}, bf16[256,768]{1,0:T(8,128)(2,1)S(1)}, u32[]{:S(2)}, u32[]{:S(2)}) collective-permute-start(bf16[256,768]{1,0:T(8,128)(2,1)S(1)} %collective-permute-done.10), channel_id=1, source_target_pairs={{0,224},{8,232},{16,240},{24,248},{32,0},{40,8},{48,16},{56,24},{6... | collective-permute-start | bytes 1179656 | tf_op jit(solution)/shard_map/ppermute | solution.py:52
  42.2 14.1 %collective-permute-start.13 = (bf16[4,64,2048]{2,1,0:T(8,128)(2,1)S(1)}, bf16[4,64,2048]{2,1,0:T(8,128)(2,1)S(1)}, u32[]{:S(2)}, u32[]{:S(2)}) collective-permute-start(bf16[4,64,2048]{2,1,0:T(8,128)(2,1)S(1)} %bitcast_dynamic-update-slice_fusion.7), channel_id=1, source_target_pairs={{0,1},{1,0},{2,3},{3,2},{4,5},{5,4},{6,7},{7,6},{8,9},{9,8},{10,11... | collective-permute-start | bytes 3145736 | tf_op jit(solution)/shard_map/ppermute | solution.py:57
  46.4 9.9 %collective-permute-start.9 = (bf16[256,768]{1,0:T(8,128)(2,1)S(1)}, bf16[256,768]{1,0:T(8,128)(2,1)S(1)}, u32[]{:S(2)}, u32[]{:S(2)}) collective-permute-start(bf16[256,768]{1,0:T(8,128)(2,1)S(1)} %collective-permute-done.8), channel_id=1, source_target_pairs={{0,32},{8,40},{16,48},{24,56},{32,64},{40,72},{48,80},{56,88},{64,... | collective-permute-start | bytes 1179656 | tf_op jit(solution)/shard_map/ppermute | solution.py:52
  46.4 9.9 %collective-permute-start.12 = (bf16[256,768]{1,0:T(8,128)(2,1)S(1)}, bf16[256,768]{1,0:T(8,128)(2,1)S(1)}, u32[]{:S(2)}, u32[]{:S(2)}) collective-permute-start(bf16[256,768]{1,0:T(8,128)(2,1)S(1)} %collective-permute-done.11), channel_id=1, source_target_pairs={{0,224},{8,232},{16,240},{24,248},{32,0},{40,8},{48,16},{56,24},{6... | collective-permute-start | bytes 1179656 | tf_op jit(solution)/shard_map/ppermute | solution.py:52
  56.4 10.7 %collective-permute-start.14 = (bf16[128,768]{1,0:T(8,128)(2,1)S(1)}, bf16[128,768]{1,0:T(8,128)(2,1)S(1)}, u32[]{:S(2)}, u32[]{:S(2)}) collective-permute-start(bf16[128,768]{1,0:T(8,128)(2,1)S(1)} %slice.52), channel_id=1, source_target_pairs={{0,32},{8,40},{16,48},{24,56},{32,64},{40,72},{48,80},{56,88},{64,... | collective-permute-start | bytes 589832 | tf_op jit(solution)/shard_map/ppermute | solution.py:52
  56.5 10.6 %collective-permute-start.15 = (bf16[128,768]{1,0:T(8,128)(2,1)S(1)}, bf16[128,768]{1,0:T(8,128)(2,1)S(1)}, u32[]{:S(2)}, u32[]{:S(2)}) collective-permute-start(bf16[128,768]{1,0:T(8,128)(2,1)S(1)} %slice.53), channel_id=1, source_target_pairs={{0,224},{8,232},{16,240},{24,248},{32,0},{40,8},{48,16},{56,24},{6... | collective-permute-start | bytes 589832 | tf_op jit(solution)/shard_map/ppermute | solution.py:52
  59.5 1.6 copy-start
  67.1 0.8 copy-start.1
  81.8 10.4 %collective-permute-start.16 = (f32[256,128]{1,0:T(8,128)}, f32[256,128]{1,0:T(8,128)S(1)}, u32[]{:S(2)}, u32[]{:S(2)}) collective-permute-start(f32[256,128]{1,0:T(8,128)} %get-tuple-element.19), channel_id=1, source_target_pairs={{0,24},{24,32},{32,56},{56,64},{64,88},{88,96},{96,120},{120,128},... | collective-permute-start | bytes 393224 | tf_op jit(solution)/shard_map/ppermute | solution.py:67
  83.3 8.8 %copy-start.4 = (f32[256,128]{1,0:T(8,128)S(1)}, f32[256,128]{1,0:T(8,128)}, u32[]{:S(2)}) copy-start(f32[256,128]{1,0:T(8,128)} %get-tuple-element.19) | copy-start | bytes 393220
  92.5 3.2 %collective-permute-start.17 = (f32[256,128]{1,0:T(8,128)S(1)}, f32[256,128]{1,0:T(8,128)S(1)}, u32[]{:S(2)}, u32[]{:S(2)}) collective-permute-start(f32[256,128]{1,0:T(8,128)S(1)} %convolution_add_fusion.2), channel_id=1, source_target_pairs={{0,32},{24,56},{32,64},{56,88},{64,96},{88,120},{96,128},{120,152}... | collective-permute-start | bytes 393224 | tf_op jit(solution)/shard_map/ppermute | solution.py:67
  96.0 7.8 %collective-permute-start.18 = (f32[256,128]{1,0:T(8,128)S(1)}, f32[256,128]{1,0:T(8,128)S(1)}, u32[]{:S(2)}, u32[]{:S(2)}) collective-permute-start(f32[256,128]{1,0:T(8,128)S(1)} %convolution_add_fusion.1), channel_id=1, source_target_pairs={{0,64},{24,88},{32,96},{56,120},{64,128},{88,152},{96,160},{120,18... | collective-permute-start | bytes 393224 | tf_op jit(solution)/shard_map/ppermute | solution.py:67
  104.0 18.2 %collective-permute-start.20 = (f32[256,128]{1,0:T(8,128)S(1)}, f32[256,128]{1,0:T(8,128)S(1)}, u32[]{:S(2)}, u32[]{:S(2)}) collective-permute-start(f32[256,128]{1,0:T(8,128)S(1)} %convolution_add_fusion), channel_id=1, source_target_pairs={{0,24},{24,32},{32,56},{56,64},{64,88},{88,96},{96,120},{120,128},... | collective-permute-start | bytes 393224 | tf_op jit(solution)/shard_map/ppermute | solution.py:67
  110.9 11.3 %collective-permute-start.19 = (f32[128,128]{1,0:T(8,128)S(1)}, f32[128,128]{1,0:T(8,128)S(1)}, u32[]{:S(2)}, u32[]{:S(2)}) collective-permute-start(f32[128,128]{1,0:T(8,128)S(1)} %slice.66), channel_id=1, source_target_pairs={{0,152},{24,160},{32,184},{56,192},{64,216},{88,224},{96,248},{8,1... | collective-permute-start | bytes 196616 | tf_op jit(solution)/shard_map/ppermute | solution.py:67
  122.2 0.6 copy-start.3
  122.9 0.7 copy-start.2
  126.2 19.3 %all-to-all-start = ((bf16[16,64,128]{2,1,0:T(8,128)(2,1)}), bf16[16,64,128]{2,1,0:T(8,128)(2,1)S(1)}, u32[]{:S(2)}, u32[]{:S(2)}) async-start(bf16[16,64,128]{2,1,0:T(8,128)(2,1)} %bitcast.74), calls=%async_computation | async-start | bytes 524288 | tf_op jit(solution)/shard_map/all_to_all | solution.py:395
Sparse Core Ops, SparseCore 0:
  11.2 124.5 all-gather.1

commit v7 on v6

--- a/solution.py
+++ b/solution.py
@@ -268,28 +268,33 @@
     out_ref[...] = (total / scale).astype(BF16)
 
 
-def mix_kernel(rows_ref, weight_ref, out_ref):
-    total = dot1(rows_ref[0], weight_ref[0], NT)
-    for group in range(1, rows_ref.shape[0]):
-        total = total + dot1(rows_ref[group], weight_ref[group], NT)
+def mix_kernel(first_ref, rows_ref, weight_ref, out_ref):
+    first = first_ref[0]
+    total = 0.0
+    for group in range(rows_ref.shape[1]):
+        rows = jnp.concatenate([rows_ref[first, group], rows_ref[1 - first, group]], axis=1)
+        total = total + dot1(rows, weight_ref[group], NT)
     out_ref[...] = total.astype(BF16)
 
 
-def mix(rows, weights):
-    groups, count, depth = rows.shape
-    width = weights.shape[1]
+def mix(first, rows, weights):
+    count = rows.shape[2]
+    groups, width, depth = weights.shape
     block = width // 4
     return pl.pallas_call(
         mix_kernel,
-        grid=(width // block,),
-        in_specs=[
-            pl.BlockSpec((groups, count, depth), lambda i: (0, 0, 0)),
-            pl.BlockSpec((groups, block, depth), lambda i: (0, i, 0)),
-        ],
-        out_specs=pl.BlockSpec((count, block), lambda i: (0, i)),
+        grid_spec=pltpu.PrefetchScalarGridSpec(
+            num_scalar_prefetch=1,
+            grid=(width // block,),
+            in_specs=[
+                pl.BlockSpec(rows.shape, lambda i, first: (0, 0, 0, 0)),
+                pl.BlockSpec((groups, block, depth), lambda i, first: (0, i, 0)),
+            ],
+            out_specs=pl.BlockSpec((count, block), lambda i, first: (0, i)),
+        ),
         out_shape=jax.ShapeDtypeStruct((count, width), BF16),
         name="mix",
-    )(rows, weights)
+    )(first, rows, weights)
 
 
 def compose(before, now):
@@ -394,9 +399,7 @@
     stacked = normed.reshape(2 * groups, rows_each, LANES)
     taken = lax.all_to_all(stacked, ("p", "head"), split_axis=0, concat_axis=0, tiled=True)
     taken = taken.reshape(2, groups, rows_each, LANES)
-    taken = jnp.where(pair == 0, taken, taken[::-1])
-    taken = jnp.concatenate([taken[0], taken[1]], axis=2)
-    return mix(taken, flipped)
+    return mix(pair.reshape(1), taken, flipped)
 
 
 def solution(mesh):

time: 160 us -> 160 us (level)
    unnamed x11 -> x13, local copies, waits for them, and re-layouts: 3.45 us -> 4.18 us
where the time goes in v7:
time: 160 us; the launch traced here: 159 us
  starting transfers between devices  62.8 us (39%)
  Pallas kernels  31.7 us (20%)
  waiting for transfers between devices  31.3 us (20%)
  between operations  15.5 us (10%)
  local copies, waits for them, and re-layouts  9.61 us (6%)
  matrix products  5.82 us (4%)
  other arithmetic  2.66 us (2%)
    ppermute x5, starting transfers between devices, shift(): return lax.ppermute(array, CTX, pairs)  24.8 us
    ppermute x12, starting transfers between devices, permute(): return lax.ppermute(array, CTX, pairs)  19 us
    pallas_call x1, Pallas kernels, local_pass(): pl.pallas_call(local_kernel, grid_spec=pltpu.PrefetchScalarGridSpec(num_s...  14 us
    ppermute x12, waiting for transfers between devices, permute(): return lax.ppermute(array, CTX, pairs)  13.5 us
    all_to_all x1, starting transfers between devices, shards(): lax.all_to_all(stacked, ('p', 'head'), split_axis=0, concat_axis=0, tiled...  12.1 us
    pallas_call x1, Pallas kernels, local_pass(): pl.pallas_call(read_kernel, grid_spec=pltpu.PrefetchScalarGridSpec(num_sc...  8.82 us
    all_to_all x1, waiting for transfers between devices, shards(): lax.all_to_all(stacked, ('p', 'head'), split_axis=0, concat_axis=0, tiled...  7.2 us
    ppermute x4, starting transfers between devices, permute_heads(): lax.ppermute(array, 'head', [(i, move(i) % count) for i in range(count)])  6.9 us
  transfers between devices with their start and end apart: 23, of which 9 were waited for; matrix products, arithmetic and copies ran while one was open for 9% of the time, Pallas kernels for 16%

profile of v7, /device:TPU:1, one launch (start us, length us, event | category | flops | bytes accessed | tf_op | source)
XLA Modules:
  0.0 159.4 jit_solution(1214605600025011107)
XLA Ops:
  6.5 0.7 all-gather.2.cloned.1.call-update
  7.3 0.8 fusion.9
  8.1 0.1 copy.10
  8.2 0.1 copy.9
  8.3 0.1 pad.32.clone
  8.4 1.0 fusion.8
  9.3 0.1 broadcast_select_fusion
  9.4 2.2 %collective-permute-start.5 = (bf16[64,768]{1,0:T(8,128)(2,1)S(1)}, bf16[64,768]{1,0:T(8,128)(2,1)S(1)}, u32[]{:S(2)}, u32[]{:S(2)}) collective-permute-start(bf16[64,768]{1,0:T(8,128)(2,1)S(1)} %get-tuple-element.29), channel_id=1, source_target_pairs={{0,8},{8,0},{16,24},{24,16},{32,40},{40,32},{48,56},{56,48},{64,72... | collective-permute-start | bytes 294920 | tf_op jit(solution)/shard_map/ppermute | solution.py:52
  11.6 2.6 %collective-permute-start.6 = (bf16[64,768]{1,0:T(8,128)(2,1)S(1)}, bf16[64,768]{1,0:T(8,128)(2,1)S(1)}, u32[]{:S(2)}, u32[]{:S(2)}) collective-permute-start(bf16[64,768]{1,0:T(8,128)(2,1)S(1)} %get-tuple-element.29), channel_id=1, source_target_pairs={{0,16},{8,24},{16,0},{24,8},{32,48},{40,56},{48,32},{56,40},{64,80... | collective-permute-start | bytes 294920 | tf_op jit(solution)/shard_map/ppermute | solution.py:52
  14.2 0.0 collective-permute-start.4
  14.2 1.0 constant_dynamic-slice_fusion
  15.2 0.1 collective-permute-start
  15.6 0.1 copy.7
  15.7 0.1 copy.8
  15.9 1.4 fusion.10
  18.6 0.1 pad_bitcast_fusion
  18.7 0.8 fusion.6
  19.5 0.6 select_maximum_fusion.row_ref
  20.1 0.9 collective-permute-done.4
  21.1 0.0 collective-permute-done.6
  21.1 1.7 %collective-permute-start.7 = (bf16[256,768]{1,0:T(8,128)(2,1)S(1)}, bf16[256,768]{1,0:T(8,128)(2,1)S(1)}, u32[]{:S(2)}, u32[]{:S(2)}) collective-permute-start(bf16[256,768]{1,0:T(8,128)(2,1)S(1)} %bitcast.67), channel_id=1, source_target_pairs={{0,32},{8,40},{16,48},{24,56},{32,64},{40,72},{48,80},{56,88},{64,... | collective-permute-start | bytes 1179656 | tf_op jit(solution)/shard_map/ppermute | solution.py:52
  22.9 4.0 %collective-permute-start.10 = (bf16[256,768]{1,0:T(8,128)(2,1)S(1)}, bf16[256,768]{1,0:T(8,128)(2,1)S(1)}, u32[]{:S(2)}, u32[]{:S(2)}) collective-permute-start(bf16[256,768]{1,0:T(8,128)(2,1)S(1)} %bitcast.68), channel_id=1, source_target_pairs={{0,224},{8,232},{16,240},{24,248},{32,0},{40,8},{48,16},{56,24},{6... | collective-permute-start | bytes 1179656 | tf_op jit(solution)/shard_map/ppermute | solution.py:52
  26.9 0.2 broadcast_in_dim.71
  27.2 1.3 collective-permute-start.1
  28.4 2.5 %collective-permute-start.2 = (bf16[64,2048]{1,0:T(8,128)(2,1)S(1)}, bf16[64,2048]{1,0:T(8,128)(2,1)S(1)}, u32[]{:S(2)}, u32[]{:S(2)}) collective-permute-start(bf16[64,2048]{1,0:T(8,128)(2,1)S(1)} %collective-permute-done), channel_id=1, source_target_pairs={{0,4},{1,5},{2,6},{3,7},{4,0},{5,1},{6,2},{7,3},{8,12},{9,13},{10,... | collective-permute-start | bytes 786440 | tf_op jit(solution)/shard_map/ppermute | solution.py:57
  30.9 1.2 collective-permute-start.3
  32.0 0.1 broadcast_in_dim.60
  32.2 3.4 %collective-permute-done.7 = bf16[256,768]{1,0:T(8,128)(2,1)S(1)} collective-permute-done((bf16[256,768]{1,0:T(8,128)(2,1)S(1)}, bf16[256,768]{1,0:T(8,128)(2,1)S(1)}, u32[]{:S(2)}, u32[]{:S(2)}) %collective-permute-start.7) | collective-permute-done | bytes 393248 | tf_op jit(solution)/shard_map/ppermute | solution.py:52
  35.6 2.7 %collective-permute-start.11 = (bf16[256,768]{1,0:T(8,128)(2,1)S(1)}, bf16[256,768]{1,0:T(8,128)(2,1)S(1)}, u32[]{:S(2)}, u32[]{:S(2)}) collective-permute-start(bf16[256,768]{1,0:T(8,128)(2,1)S(1)} %collective-permute-done.10), channel_id=1, source_target_pairs={{0,224},{8,232},{16,240},{24,248},{32,0},{40,8},{48,16},{56,24},{6... | collective-permute-start | bytes 1179656 | tf_op jit(solution)/shard_map/ppermute | solution.py:52
  38.3 3.9 %collective-permute-done.2 = bf16[64,2048]{1,0:T(8,128)(2,1)S(1)} collective-permute-done((bf16[64,2048]{1,0:T(8,128)(2,1)S(1)}, bf16[64,2048]{1,0:T(8,128)(2,1)S(1)}, u32[]{:S(2)}, u32[]{:S(2)}) %collective-permute-start.2) | collective-permute-done | bytes 262176 | tf_op jit(solution)/shard_map/ppermute | solution.py:57
  42.2 2.0 %collective-permute-start.13 = (bf16[4,64,2048]{2,1,0:T(8,128)(2,1)S(1)}, bf16[4,64,2048]{2,1,0:T(8,128)(2,1)S(1)}, u32[]{:S(2)}, u32[]{:S(2)}) collective-permute-start(bf16[4,64,2048]{2,1,0:T(8,128)(2,1)S(1)} %bitcast_dynamic-update-slice_fusion.7), channel_id=1, source_target_pairs={{0,1},{1,0},{2,3},{3,2},{4,5},{5,4},{6,7},{7,6},{8,9},{9,8},{10,11... | collective-permute-start | bytes 3145736 | tf_op jit(solution)/shard_map/ppermute | solution.py:57
  44.3 2.1 %collective-permute-done.8 = bf16[256,768]{1,0:T(8,128)(2,1)S(1)} collective-permute-done((bf16[256,768]{1,0:T(8,128)(2,1)S(1)}, bf16[256,768]{1,0:T(8,128)(2,1)S(1)}, u32[]{:S(2)}, u32[]{:S(2)}) %collective-permute-start.8) | collective-permute-done | bytes 393248 | tf_op jit(solution)/shard_map/ppermute | solution.py:52
  46.4 2.7 %collective-permute-start.12 = (bf16[256,768]{1,0:T(8,128)(2,1)S(1)}, bf16[256,768]{1,0:T(8,128)(2,1)S(1)}, u32[]{:S(2)}, u32[]{:S(2)}) collective-permute-start(bf16[256,768]{1,0:T(8,128)(2,1)S(1)} %collective-permute-done.11), channel_id=1, source_target_pairs={{0,224},{8,232},{16,240},{24,248},{32,0},{40,8},{48,16},{56,24},{6... | collective-permute-start | bytes 1179656 | tf_op jit(solution)/shard_map/ppermute | solution.py:52
  49.1 7.1 %collective-permute-done.9 = bf16[256,768]{1,0:T(8,128)(2,1)S(1)} collective-permute-done((bf16[256,768]{1,0:T(8,128)(2,1)S(1)}, bf16[256,768]{1,0:T(8,128)(2,1)S(1)}, u32[]{:S(2)}, u32[]{:S(2)}) %collective-permute-start.9) | collective-permute-done | bytes 393248 | tf_op jit(solution)/shard_map/ppermute | solution.py:52
  56.4 0.1 collective-permute-start.14
  56.5 2.9 %collective-permute-start.15 = (bf16[128,768]{1,0:T(8,128)(2,1)S(1)}, bf16[128,768]{1,0:T(8,128)(2,1)S(1)}, u32[]{:S(2)}, u32[]{:S(2)}) collective-permute-start(bf16[128,768]{1,0:T(8,128)(2,1)S(1)} %slice.47), channel_id=1, source_target_pairs={{0,224},{8,232},{16,240},{24,248},{32,0},{40,8},{48,16},{56,24},{6... | collective-permute-start | bytes 589832 | tf_op jit(solution)/shard_map/ppermute | solution.py:52
  59.4 0.1 select_bitcast_fusion.1
  59.5 0.0 copy-start
  59.5 0.2 pad_maximum_fusion.2
  59.7 1.4 copy-done
  61.1 5.1 %fusion.early_ref = f32[1024,768]{1,0:T(8,128)} fusion(bf16[2048,768]{1,0:T(8,128)(2,1)S(1)} %bitcast.66, bf16[512,2048]{1,0:T(8,128)(2,1)S(1)} %bitcast.63, bf16[512,2048]{1,0:T(8,128)(2,1)S(1)} %copy-done), kind=kOutput, calls=%fused_computation.3 | convolution fusion | flops 3229614080 | bytes 10485760 | tf_op jit(solution)/shard_map/dot_general | solution.py:372
  66.2 0.9 fusion.1.behind_ref
  67.1 0.8 copy-done.1
  67.9 14.0 %local.1 = (f32[256,128]{1,0:T(8,128)}, f32[16,128,256]{2,1,0:T(8,128)}, f32[16,256,128]{2,1,0:T(8,128)}) custom-call(s32[1]{0:T(128)} %bitcast.1.swap_ref, f32[1024,768]{1,0:T(8,128)} %fusion.early_ref, bf16[1024,256]{1,0:T(8,128)(2,1)} %fusion.1.behind_ref, bf16[256,768]{1,0:T(8,128)(2,1)} %copy-done.1, f32[8,128]{1,0:T(8,128)} %select_maximum_fusion.row_ref), custom_call_target="tpu_custom_call" | custom-call | tf_op jit(solution)/shard_map/local/pallas_call | solution.py:232
  81.8 1.5 collective-permute-start.16
  83.3 0.0 copy-start.5
  83.4 8.8 %reads.1 = (f32[1024,128]{1,0:T(8,128)}, f32[1024,128]{1,0:T(8,128)}) custom-call(s32[1]{0:T(128)} %bitcast.1.swap_ref, f32[1024,768]{1,0:T(8,128)} %fusion.early_ref, bf16[1024,256]{1,0:T(8,128)(2,1)} %fusion.1.behind_ref, bf16[256,768]{1,0:T(8,128)(2,1)} %copy-done.1, f32[8,128]{1,0:T(8,128)} %select_maximum_fusion.row_ref, ...), custom_call_target="tpu_custom_call" | custom-call | tf_op jit(solution)/shard_map/reads/pallas_call | solution.py:248
  92.2 0.3 convolution_add_fusion.2
  92.5 1.3 collective-permute-start.17
  93.8 1.9 %collective-permute-done.17 = f32[256,128]{1,0:T(8,128)S(1)} collective-permute-done((f32[256,128]{1,0:T(8,128)S(1)}, f32[256,128]{1,0:T(8,128)S(1)}, u32[]{:S(2)}, u32[]{:S(2)}) %collective-permute-start.17) | collective-permute-done | bytes 131104 | tf_op jit(solution)/shard_map/ppermute | solution.py:67
  95.7 0.3 convolution_add_fusion.1
  96.0 5.4 %collective-permute-start.18 = (f32[256,128]{1,0:T(8,128)S(1)}, f32[256,128]{1,0:T(8,128)S(1)}, u32[]{:S(2)}, u32[]{:S(2)}) collective-permute-start(f32[256,128]{1,0:T(8,128)S(1)} %convolution_add_fusion.1), channel_id=1, source_target_pairs={{0,64},{24,88},{32,96},{56,120},{64,128},{88,152},{96,160},{120,18... | collective-permute-start | bytes 393224 | tf_op jit(solution)/shard_map/ppermute | solution.py:67
  101.3 2.4 %collective-permute-done.18 = f32[256,128]{1,0:T(8,128)S(1)} collective-permute-done((f32[256,128]{1,0:T(8,128)S(1)}, f32[256,128]{1,0:T(8,128)S(1)}, u32[]{:S(2)}, u32[]{:S(2)}) %collective-permute-start.18) | collective-permute-done | bytes 131104 | tf_op jit(solution)/shard_map/ppermute | solution.py:67
  103.7 0.3 convolution_add_fusion
  104.0 6.9 %collective-permute-start.20 = (f32[256,128]{1,0:T(8,128)S(1)}, f32[256,128]{1,0:T(8,128)S(1)}, u32[]{:S(2)}, u32[]{:S(2)}) collective-permute-start(f32[256,128]{1,0:T(8,128)S(1)} %convolution_add_fusion), channel_id=1, source_target_pairs={{0,24},{24,32},{32,56},{56,64},{64,88},{88,96},{96,120},{120,128},... | collective-permute-start | bytes 393224 | tf_op jit(solution)/shard_map/ppermute | solution.py:67
  110.9 9.7 %collective-permute-start.19 = (f32[128,128]{1,0:T(8,128)S(1)}, f32[128,128]{1,0:T(8,128)S(1)}, u32[]{:S(2)}, u32[]{:S(2)}) collective-permute-start(f32[128,128]{1,0:T(8,128)S(1)} %slice.58), channel_id=1, source_target_pairs={{0,152},{24,160},{32,184},{56,192},{64,216},{88,224},{96,248},{8,1... | collective-permute-start | bytes 196616 | tf_op jit(solution)/shard_map/ppermute | solution.py:67
  120.6 1.6 %collective-permute-done.19.far_ref = f32[128,128]{1,0:T(8,128)S(1)} collective-permute-done((f32[128,128]{1,0:T(8,128)S(1)}, f32[128,128]{1,0:T(8,128)S(1)}, u32[]{:S(2)}, u32[]{:S(2)}) %collective-permute-start.19) | collective-permute-done | bytes 65568 | tf_op jit(solution)/shard_map/ppermute | solution.py:67
  122.3 0.6 copy-done.4
  122.9 0.7 copy-done.3
  123.5 2.7 %finish.1 = bf16[1024,128]{1,0:T(8,128)(2,1)} custom-call(f32[128,128]{1,0:T(8,128)} %copy-done.4, f32[256,128]{1,0:T(8,128)} %copy-done.3, f32[1024,128]{1,0:T(8,128)} %get-tuple-element.25.query_ref, f32[1024,128]{1,0:T(8,128)} %get-tuple-element.26.part_ref), custom_call_target="tpu_custom_call" | custom-call | tf_op jit(solution)/shard_map/finish/pallas_call | solution.py:394
  126.2 12.1 %all-to-all-start = ((bf16[16,64,128]{2,1,0:T(8,128)(2,1)}), bf16[16,64,128]{2,1,0:T(8,128)(2,1)S(1)}, u32[]{:S(2)}, u32[]{:S(2)}) async-start(bf16[16,64,128]{2,1,0:T(8,128)(2,1)} %bitcast.71), calls=%async_computation | async-start | bytes 524288 | tf_op jit(solution)/shard_map/all_to_all | solution.py:400
  138.3 7.2 %all-to-all-done = bf16[16,64,128]{2,1,0:T(8,128)(2,1)S(1)} async-done(((bf16[16,64,128]{2,1,0:T(8,128)(2,1)}), bf16[16,64,128]{2,1,0:T(8,128)(2,1)S(1)}, u32[]{:S(2)}, u32[]{:S(2)}) %all-to-all-start) | async-done | bytes 262176 | tf_op jit(solution)/shard_map/all_to_all | solution.py:400
  145.5 0.7 copy-done.2
  146.2 6.3 %mix.1 = bf16[64,2048]{1,0:T(8,128)(2,1)} custom-call(s32[1]{0:T(128)} %bitcast.first_ref, bf16[2,8,64,128]{3,2,1,0:T(8,128)(2,1)} %bitcast.70, bf16[8,2048,256]{2,1,0:T(8,128)(2,1)} %bitcast.65), custom_call_target="tpu_custom_call" | custom-call | tf_op jit(solution)/shard_map/mix/pallas_call | solution.py:284
  (45 shorter events, 0.6 us)
Async XLA Ops:
  6.5 139.0 %all-gather.2.cloned.1.call-start = ((), (), s32[]{:S(2)}) async-start(), calls=%async_computation.1 | async-start | bytes 8421376 | tf_op jit(solution)/shard_map/all_gather | solution.py:324
  9.4 11.7 %collective-permute-start.5 = (bf16[64,768]{1,0:T(8,128)(2,1)S(1)}, bf16[64,768]{1,0:T(8,128)(2,1)S(1)}, u32[]{:S(2)}, u32[]{:S(2)}) collective-permute-start(bf16[64,768]{1,0:T(8,128)(2,1)S(1)} %get-tuple-element.29), channel_id=1, source_target_pairs={{0,8},{8,0},{16,24},{24,16},{32,40},{40,32},{48,56},{56,48},{64,72... | collective-permute-start | bytes 294920 | tf_op jit(solution)/shard_map/ppermute | solution.py:52
  11.6 9.5 %collective-permute-start.6 = (bf16[64,768]{1,0:T(8,128)(2,1)S(1)}, bf16[64,768]{1,0:T(8,128)(2,1)S(1)}, u32[]{:S(2)}, u32[]{:S(2)}) collective-permute-start(bf16[64,768]{1,0:T(8,128)(2,1)S(1)} %get-tuple-element.29), channel_id=1, source_target_pairs={{0,16},{8,24},{16,0},{24,8},{32,48},{40,56},{48,32},{56,40},{64,80... | collective-permute-start | bytes 294920 | tf_op jit(solution)/shard_map/ppermute | solution.py:52
  14.2 6.8 %collective-permute-start.4 = (bf16[64,768]{1,0:T(8,128)(2,1)S(1)}, bf16[64,768]{1,0:T(8,128)(2,1)S(1)}, u32[]{:S(2)}, u32[]{:S(2)}) collective-permute-start(bf16[64,768]{1,0:T(8,128)(2,1)S(1)} %get-tuple-element.30), channel_id=1, source_target_pairs={{0,24},{8,16},{16,8},{24,0},{32,56},{40,48},{48,40},{56,32},{64,88... | collective-permute-start | bytes 294920 | tf_op jit(solution)/shard_map/ppermute | solution.py:52
  15.2 11.9 %collective-permute-start = (bf16[64,2048]{1,0:T(8,128)(2,1)S(1)}, bf16[64,2048]{1,0:T(8,128)(2,1)S(1)}, u32[]{:S(2)}, u32[]{:S(2)}) collective-permute-start(bf16[64,2048]{1,0:T(8,128)(2,1)S(1)} %constant_dynamic-slice_fusion), channel_id=1, source_target_pairs={{0,8},{8,0},{16,24},{24,16},{32,40},{40,32},{48,56},{56,48},{64,72... | collective-permute-start | bytes 786440 | tf_op jit(solution)/shard_map/ppermute | solution.py:52
  21.1 14.4 %collective-permute-start.7 = (bf16[256,768]{1,0:T(8,128)(2,1)S(1)}, bf16[256,768]{1,0:T(8,128)(2,1)S(1)}, u32[]{:S(2)}, u32[]{:S(2)}) collective-permute-start(bf16[256,768]{1,0:T(8,128)(2,1)S(1)} %bitcast.67), channel_id=1, source_target_pairs={{0,32},{8,40},{16,48},{24,56},{32,64},{40,72},{48,80},{56,88},{64,... | collective-permute-start | bytes 1179656 | tf_op jit(solution)/shard_map/ppermute | solution.py:52
  22.9 12.7 %collective-permute-start.10 = (bf16[256,768]{1,0:T(8,128)(2,1)S(1)}, bf16[256,768]{1,0:T(8,128)(2,1)S(1)}, u32[]{:S(2)}, u32[]{:S(2)}) collective-permute-start(bf16[256,768]{1,0:T(8,128)(2,1)S(1)} %bitcast.68), channel_id=1, source_target_pairs={{0,224},{8,232},{16,240},{24,248},{32,0},{40,8},{48,16},{56,24},{6... | collective-permute-start | bytes 1179656 | tf_op jit(solution)/shard_map/ppermute | solution.py:52
  27.2 11.1 %collective-permute-start.1 = (bf16[64,2048]{1,0:T(8,128)(2,1)S(1)}, bf16[64,2048]{1,0:T(8,128)(2,1)S(1)}, u32[]{:S(2)}, u32[]{:S(2)}) collective-permute-start(bf16[64,2048]{1,0:T(8,128)(2,1)S(1)} %collective-permute-done), channel_id=1, source_target_pairs={{0,2},{1,3},{2,4},{3,5},{4,6},{5,7},{6,0},{7,1},{8,10},{9,11},{10,... | collective-permute-start | bytes 786440 | tf_op jit(solution)/shard_map/ppermute | solution.py:57
  28.4 13.7 %collective-permute-start.2 = (bf16[64,2048]{1,0:T(8,128)(2,1)S(1)}, bf16[64,2048]{1,0:T(8,128)(2,1)S(1)}, u32[]{:S(2)}, u32[]{:S(2)}) collective-permute-start(bf16[64,2048]{1,0:T(8,128)(2,1)S(1)} %collective-permute-done), channel_id=1, source_target_pairs={{0,4},{1,5},{2,6},{3,7},{4,0},{5,1},{6,2},{7,3},{8,12},{9,13},{10,... | collective-permute-start | bytes 786440 | tf_op jit(solution)/shard_map/ppermute | solution.py:57
  30.9 11.3 %collective-permute-start.3 = (bf16[64,2048]{1,0:T(8,128)(2,1)S(1)}, bf16[64,2048]{1,0:T(8,128)(2,1)S(1)}, u32[]{:S(2)}, u32[]{:S(2)}) collective-permute-start(bf16[64,2048]{1,0:T(8,128)(2,1)S(1)} %collective-permute-done), channel_id=1, source_target_pairs={{0,6},{1,7},{2,0},{3,1},{4,2},{5,3},{6,4},{7,5},{8,14},{9,15},{10,... | collective-permute-start | bytes 786440 | tf_op jit(solution)/shard_map/ppermute | solution.py:57
  35.6 10.8 %collective-permute-start.8 = (bf16[256,768]{1,0:T(8,128)(2,1)S(1)}, bf16[256,768]{1,0:T(8,128)(2,1)S(1)}, u32[]{:S(2)}, u32[]{:S(2)}) collective-permute-start(bf16[256,768]{1,0:T(8,128)(2,1)S(1)} %collective-permute-done.7), channel_id=1, source_target_pairs={{0,32},{8,40},{16,48},{24,56},{32,64},{40,72},{48,80},{56,88},{64,... | collective-permute-start | bytes 1179656 | tf_op jit(solution)/shard_map/ppermute | solution.py:52
  35.6 10.8 %collective-permute-start.11 = (bf16[256,768]{1,0:T(8,128)(2,1)S(1)}, bf16[256,768]{1,0:T(8,128)(2,1)S(1)}, u32[]{:S(2)}, u32[]{:S(2)}) collective-permute-start(bf16[256,768]{1,0:T(8,128)(2,1)S(1)} %collective-permute-done.10), channel_id=1, source_target_pairs={{0,224},{8,232},{16,240},{24,248},{32,0},{40,8},{48,16},{56,24},{6... | collective-permute-start | bytes 1179656 | tf_op jit(solution)/shard_map/ppermute | solution.py:52
  42.2 14.1 %collective-permute-start.13 = (bf16[4,64,2048]{2,1,0:T(8,128)(2,1)S(1)}, bf16[4,64,2048]{2,1,0:T(8,128)(2,1)S(1)}, u32[]{:S(2)}, u32[]{:S(2)}) collective-permute-start(bf16[4,64,2048]{2,1,0:T(8,128)(2,1)S(1)} %bitcast_dynamic-update-slice_fusion.7), channel_id=1, source_target_pairs={{0,1},{1,0},{2,3},{3,2},{4,5},{5,4},{6,7},{7,6},{8,9},{9,8},{10,11... | collective-permute-start | bytes 3145736 | tf_op jit(solution)/shard_map/ppermute | solution.py:57
  46.4 9.9 %collective-permute-start.9 = (bf16[256,768]{1,0:T(8,128)(2,1)S(1)}, bf16[256,768]{1,0:T(8,128)(2,1)S(1)}, u32[]{:S(2)}, u32[]{:S(2)}) collective-permute-start(bf16[256,768]{1,0:T(8,128)(2,1)S(1)} %collective-permute-done.8), channel_id=1, source_target_pairs={{0,32},{8,40},{16,48},{24,56},{32,64},{40,72},{48,80},{56,88},{64,... | collective-permute-start | bytes 1179656 | tf_op jit(solution)/shard_map/ppermute | solution.py:52
  46.4 9.9 %collective-permute-start.12 = (bf16[256,768]{1,0:T(8,128)(2,1)S(1)}, bf16[256,768]{1,0:T(8,128)(2,1)S(1)}, u32[]{:S(2)}, u32[]{:S(2)}) collective-permute-start(bf16[256,768]{1,0:T(8,128)(2,1)S(1)} %collective-permute-done.11), channel_id=1, source_target_pairs={{0,224},{8,232},{16,240},{24,248},{32,0},{40,8},{48,16},{56,24},{6... | collective-permute-start | bytes 1179656 | tf_op jit(solution)/shard_map/ppermute | solution.py:52
  56.4 10.7 %collective-permute-start.14 = (bf16[128,768]{1,0:T(8,128)(2,1)S(1)}, bf16[128,768]{1,0:T(8,128)(2,1)S(1)}, u32[]{:S(2)}, u32[]{:S(2)}) collective-permute-start(bf16[128,768]{1,0:T(8,128)(2,1)S(1)} %slice.46), channel_id=1, source_target_pairs={{0,32},{8,40},{16,48},{24,56},{32,64},{40,72},{48,80},{56,88},{64,... | collective-permute-start | bytes 589832 | tf_op jit(solution)/shard_map/ppermute | solution.py:52
  56.5 10.6 %collective-permute-start.15 = (bf16[128,768]{1,0:T(8,128)(2,1)S(1)}, bf16[128,768]{1,0:T(8,128)(2,1)S(1)}, u32[]{:S(2)}, u32[]{:S(2)}) collective-permute-start(bf16[128,768]{1,0:T(8,128)(2,1)S(1)} %slice.47), channel_id=1, source_target_pairs={{0,224},{8,232},{16,240},{24,248},{32,0},{40,8},{48,16},{56,24},{6... | collective-permute-start | bytes 589832 | tf_op jit(solution)/shard_map/ppermute | solution.py:52
  59.5 1.6 %copy-start = (bf16[512,2048]{1,0:T(8,128)(2,1)S(1)}, bf16[512,2048]{1,0:T(8,128)(2,1)}, u32[]{:S(2)}) copy-start(bf16[512,2048]{1,0:T(8,128)(2,1)} %param.6) | copy-start | bytes 6291460
  67.1 0.8 copy-start.1
  81.8 10.4 %collective-permute-start.16 = (f32[256,128]{1,0:T(8,128)}, f32[256,128]{1,0:T(8,128)S(1)}, u32[]{:S(2)}, u32[]{:S(2)}) collective-permute-start(f32[256,128]{1,0:T(8,128)} %get-tuple-element.19), channel_id=1, source_target_pairs={{0,24},{24,32},{32,56},{56,64},{64,88},{88,96},{96,120},{120,128},... | collective-permute-start | bytes 393224 | tf_op jit(solution)/shard_map/ppermute | solution.py:67
  83.3 8.8 %copy-start.5 = (f32[256,128]{1,0:T(8,128)S(1)}, f32[256,128]{1,0:T(8,128)}, u32[]{:S(2)}) copy-start(f32[256,128]{1,0:T(8,128)} %get-tuple-element.19) | copy-start | bytes 393220
  92.5 3.2 %collective-permute-start.17 = (f32[256,128]{1,0:T(8,128)S(1)}, f32[256,128]{1,0:T(8,128)S(1)}, u32[]{:S(2)}, u32[]{:S(2)}) collective-permute-start(f32[256,128]{1,0:T(8,128)S(1)} %convolution_add_fusion.2), channel_id=1, source_target_pairs={{0,32},{24,56},{32,64},{56,88},{64,96},{88,120},{96,128},{120,152}... | collective-permute-start | bytes 393224 | tf_op jit(solution)/shard_map/ppermute | solution.py:67
  96.0 7.8 %collective-permute-start.18 = (f32[256,128]{1,0:T(8,128)S(1)}, f32[256,128]{1,0:T(8,128)S(1)}, u32[]{:S(2)}, u32[]{:S(2)}) collective-permute-start(f32[256,128]{1,0:T(8,128)S(1)} %convolution_add_fusion.1), channel_id=1, source_target_pairs={{0,64},{24,88},{32,96},{56,120},{64,128},{88,152},{96,160},{120,18... | collective-permute-start | bytes 393224 | tf_op jit(solution)/shard_map/ppermute | solution.py:67
  104.0 18.2 %collective-permute-start.20 = (f32[256,128]{1,0:T(8,128)S(1)}, f32[256,128]{1,0:T(8,128)S(1)}, u32[]{:S(2)}, u32[]{:S(2)}) collective-permute-start(f32[256,128]{1,0:T(8,128)S(1)} %convolution_add_fusion), channel_id=1, source_target_pairs={{0,24},{24,32},{32,56},{56,64},{64,88},{88,96},{96,120},{120,128},... | collective-permute-start | bytes 393224 | tf_op jit(solution)/shard_map/ppermute | solution.py:67
  110.9 11.3 %collective-permute-start.19 = (f32[128,128]{1,0:T(8,128)S(1)}, f32[128,128]{1,0:T(8,128)S(1)}, u32[]{:S(2)}, u32[]{:S(2)}) collective-permute-start(f32[128,128]{1,0:T(8,128)S(1)} %slice.58), channel_id=1, source_target_pairs={{0,152},{24,160},{32,184},{56,192},{64,216},{88,224},{96,248},{8,1... | collective-permute-start | bytes 196616 | tf_op jit(solution)/shard_map/ppermute | solution.py:67
  122.2 0.6 copy-start.4
  122.9 0.7 copy-start.3
  126.2 19.3 %all-to-all-start = ((bf16[16,64,128]{2,1,0:T(8,128)(2,1)}), bf16[16,64,128]{2,1,0:T(8,128)(2,1)S(1)}, u32[]{:S(2)}, u32[]{:S(2)}) async-start(bf16[16,64,128]{2,1,0:T(8,128)(2,1)} %bitcast.71), calls=%async_computation | async-start | bytes 524288 | tf_op jit(solution)/shard_map/all_to_all | solution.py:400
  145.5 0.7 copy-start.2
Sparse Core Ops, SparseCore 0:
  11.2 124.5 all-gather.1
